TPU v7x, 128 devices: a whole 4x4x4 slice. The times are simulated.
128 devices in a mesh: slab: 8 (over x, core), grp: 16 (over y, z).
Axes of the slice: x: 4, y: 4, z: 4, core: 2. Of those that a mesh axis runs over, the one named last changes fastest.
Arguments:
- raw_frames: bfloat16 [512, 96, 10752], P('grp', 'slab'), may hold values from -700 to 700
- mask_index: int32 [229376], P(('slab', 'grp')), may hold values from 0 to 1032191, as said below
- subspace: bfloat16 [1200, 229376], P(None, ('slab', 'grp')), may hold values from -6 to 6
- rotation: bfloat16 [1712, 1200], replicated, may hold values from -0.15625 to 0.15625
Outputs:
- gram: float32 [1712, 1712], P('grp')
- new_subspace: bfloat16 [1200, 229376], P(None, ('slab', 'grp'))
Inputs may be any that keep to these rules, and one draw needn't show every extreme that they name: `mask_index`: entries are distinct flat grid positions that come in runs of 128 consecutive positions, each run starting at a multiple of 128; the 28672 entries of aligned block s lie in z planes s * 12 to (s + 1) * 12 - 1 and rise within the block; the first 7168 of a block lie in its lowest 3 planes, the last 7168 in its highest 3 planes, the others in the planes between.
All inputs are finite; a program needn't handle non-finite values.
Results may differ from a plain program's by a relative error of at most 0.006.
Values may be sent and summed in bfloat16 or wider, within the bound.
No kernel may reach another device: no remote copies, remote signals or barrier semaphores. Data moves between devices by JAX's collectives and lax.ppermute only.
A program may use at most 192 MiB of HBM per device.

v0:
```python
import math

import jax
import jax.numpy as jnp
from jax import lax
from jax.sharding import PartitionSpec as P

NX = 96
RUN = 128
RAD = 3
K = 1200


smooth_sigma = 1.0617
epsilon = 1e-06


def padded_2(cells, sides, width):
    for axis, dim in sides:
        count = lax.axis_size(axis)
        ends = count - 1
        head = lax.slice_in_dim(cells, 0, width, axis=dim)
        tail = lax.slice_in_dim(cells, cells.shape[dim] - width, cells.shape[dim], axis=dim)
        cells = jnp.concatenate(
            [
                lax.ppermute(tail, axis, [(i, (i + 1) % count) for i in range(ends)]),
                cells,
                lax.ppermute(head, axis, [((i + 1) % count, i) for i in range(ends)]),
            ],
            axis=dim,
        )
    return cells


def copy_for_each(value, axis):
    size = lax.axis_size(axis)
    return lax.all_to_all(
        jnp.broadcast_to(value[None], (size, *value.shape)), axis, 0, 0, tiled=True
    )


def over_copies(value, axis):
    everything = copy_for_each(value, axis)
    return jnp.sum(everything.astype(jnp.float32), axis=0)


def over_copies_2(value, axis):
    everything = copy_for_each(value, axis)
    return jnp.sum(everything, axis=0)


def tap_weights():
    unscaled = [
        math.exp(-offset * offset / (2.0 * smooth_sigma * smooth_sigma))
        for offset in range(-RAD, RAD + 1)
    ]
    summed = sum(unscaled)
    return [weight / summed for weight in unscaled]


def along_rows(volume):
    weights = tap_weights()
    extent = volume.shape[-1]
    column = lax.broadcasted_iota(jnp.int32, (extent,), 0) % NX
    padded = jnp.pad(volume, [(0, 0)] * (volume.ndim - 1) + [(RAD, RAD)])
    summed = jnp.zeros(volume.shape, jnp.float32)
    for offset in range(-RAD, RAD + 1):
        shifted = lax.slice_in_dim(
            padded, RAD + offset, RAD + offset + extent, axis=volume.ndim - 1
        )
        inside = (column + offset >= 0) & (column + offset < NX)
        summed = summed + weights[offset + RAD] * jnp.where(inside, shifted, 0.0)
    return summed


def along_columns(volume):
    weights = tap_weights()
    extent = volume.shape[-1]
    reach_cells = RAD * NX
    padded = jnp.pad(volume, [(0, 0)] * (volume.ndim - 1) + [(reach_cells, reach_cells)])
    summed = jnp.zeros(volume.shape, jnp.float32)
    for offset in range(-RAD, RAD + 1):
        begin = reach_cells + offset * NX
        shifted = lax.slice_in_dim(padded, begin, begin + extent, axis=volume.ndim - 1)
        summed = summed + weights[offset + RAD] * shifted
    return summed


def along_depth(padded, slab_depth):
    weights = tap_weights()
    summed = None
    for offset in range(-RAD, RAD + 1):
        shifted = lax.slice_in_dim(
            padded, RAD + offset, RAD + offset + slab_depth, axis=padded.ndim - 2
        )
        term = weights[offset + RAD] * shifted
        summed = term if summed is None else summed + term
    return summed


def pick_columns(matrix, wanted):
    row_total = matrix.shape[0]
    blocked = matrix.reshape(row_total, matrix.shape[1] // RUN, RUN)
    run_starts = wanted.reshape(-1, RUN)[:, 0] // RUN
    picked_runs = jnp.take(blocked, run_starts, axis=1)
    return picked_runs.reshape(row_total, wanted.shape[0])


def body(raw_frames, mask_index, subspace, rotation):
    frames_here = raw_frames.shape[0]
    slab_depth = raw_frames.shape[1]
    extent = raw_frames.shape[2]
    per_device = subspace.shape[1]
    group_count = lax.axis_size("grp")
    masked = per_device * lax.axis_size("slab") * group_count
    positions = lax.all_gather(mask_index, "grp", axis=0, tiled=True) - lax.axis_index("slab") * (
        slab_depth * extent
    )
    padded = padded_2(raw_frames, (("slab", 1),), RAD)
    planar = along_columns(along_rows(padded.astype(jnp.float32)))
    smoothed = (
        along_depth(planar, slab_depth)
        .reshape(frames_here, slab_depth * extent)
        .astype(jnp.bfloat16)
    )
    picked = pick_columns(smoothed, positions)
    regrouped = lax.all_to_all(picked, "grp", split_axis=1, concat_axis=0, tiled=True)
    frame_count = regrouped.shape[0]
    subject_frames = frame_count // 2
    halves = regrouped.astype(jnp.float32).reshape(2, subject_frames, per_device)
    centered = (halves - jnp.mean(halves, axis=1, keepdims=True)).astype(jnp.bfloat16)
    order_rows = K + frame_count
    stacked = jnp.concatenate([subspace, centered.reshape(frame_count, per_device)], 0)
    rows_here = order_rows // group_count
    first_row = lax.axis_index("grp") * rows_here
    owned = lax.psum_scatter(
        jnp.dot(stacked, stacked.T, preferred_element_type=jnp.float32).astype(jnp.bfloat16),
        "grp",
        scatter_dimension=0,
        tiled=True,
    ).astype(jnp.float32)
    owned = over_copies(owned.astype(jnp.bfloat16), "slab").astype(jnp.float32)
    square = lax.dynamic_slice_in_dim(owned, first_row, rows_here, 1)
    diagonal_terms = jnp.diagonal(square)
    row_number = first_row + lax.broadcasted_iota(jnp.int32, (rows_here,), 0)
    subject_of = (row_number - K) // subject_frames
    member = (row_number[None, :] >= K) & (
        subject_of[None, :] == lax.broadcasted_iota(jnp.int32, (2, 1), 0)
    )
    partial_power = jnp.sum(jnp.where(member, diagonal_terms[None, :], 0.0), axis=1)
    power = over_copies_2(partial_power, "grp")
    scales = lax.rsqrt(power / (masked * subject_frames) + epsilon)
    row_scale = jnp.concatenate([jnp.ones((K,), jnp.float32), jnp.repeat(scales, subject_frames)])
    owned_scale = lax.dynamic_slice_in_dim(row_scale, first_row, rows_here, 0)
    gram_rows = owned * (owned_scale[:, None] * row_scale[None, :]) / masked
    contract = (((0,), (0,)), ((), ()))
    from_basis = lax.dot_general(
        rotation[:K], subspace, contract, preferred_element_type=jnp.float32
    )
    from_first = lax.dot_general(
        rotation[K : K + subject_frames], centered[0], contract, preferred_element_type=jnp.float32
    )
    from_second = lax.dot_general(
        rotation[K + subject_frames :], centered[1], contract, preferred_element_type=jnp.float32
    )
    new_subspace = (from_basis + scales[0] * from_first + scales[1] * from_second).astype(
        jnp.bfloat16
    )
    return (gram_rows, new_subspace)


def solution(mesh):
    placed = (P("grp", "slab", None), P(("slab", "grp")), P(None, ("slab", "grp")), P())
    return jax.shard_map(
        body,
        mesh=mesh,
        in_specs=placed,
        out_specs=(P("grp", None), P(None, ("slab", "grp"))),
        check_vma=False,
    )
```

profile of v0, /device:TPU:0, one launch (start us, length us, event | category | flops | bytes accessed | tf_op | source)
XLA Modules:
  0.0 488.2 jit_solution(15574134261321810649)
XLA Ops:
  0.6 4.5 fusion.62
  5.1 1.4 collective-permute-start
  6.5 1.3 collective-permute-start.1
  7.8 0.7 reshape.99
  8.5 25.8 %all-gather = s32[16,1,1792]{2,1,0:T(1,128)S(1)} all-gather(s32[1,1,1792]{2,1,0:T(1,128)S(1)} %reshape.99), channel_id=1, replica_groups=mesh['slab'=8,'grp'=16] {'grp'}, dimensions={0}, use_global_device_ids=true | all-gather | bytes 121856 | tf_op jit(solution)/shard_map/all_gather | solution.py:116
  34.3 0.2 and_reduce_fusion
  34.5 0.1 broadcast_in_dim.86
  34.6 0.1 broadcast_in_dim.87
  34.7 0.1 reduce.5
  35.1 12.9 %maximum_convert_fusion = f32[32,18,10752]{2,0,1:T(8,128)} fusion(bf16[32,3,10752]{2,0,1:T(8,128)(2,1)} %collective-permute-done.1, bf16[32,12,10752]{2,0,1:T(8,128)(2,1)} %param.4, bf16[32,3,10752]{2,0,1:T(8,128)(2,1)S(1)} %collective-permute-done), kind=kLoop, calls=%fused_computation.30 | loop fusion | flops 18579456 | bytes 37158912 | tf_op jit(solution)/shard_map/convert_element_type | solution.py:120
  48.0 64.2 %multiply_add_fusion.1 = f32[32,18,10752]{2,0,1:T(8,128)} fusion(f32[32,18,10752]{2,0,1:T(8,128)} %maximum_convert_fusion, pred[10752]{0:T(1024)(128)(4,1)S(1)} %get-tuple-element.8, pred[10752]{0:T(1024)(128)(4,1)S(1)} %get-tuple-element.9, pred[10752]{0:T(1024)(128)(4,1)S(1)} %get-tuple-element.10, pred[10752]{0:T(1024)(128)(4,1)S(1)} %fusion.57, ...), kind=kLoop, calls=%fused_computation.8 | loop fusion | flops 123863040 | bytes 49620480 | tf_op jit(solution)/shard_map/add | solution.py:72
  112.2 64.0 %multiply_add_fusion = f32[32,18,10752]{2,0,1:T(8,128)} fusion(f32[32,18,10752]{2,0,1:T(8,128)} %multiply_add_fusion.1), kind=kLoop, calls=%fused_computation.2 | loop fusion | flops 80510976 | bytes 49545216 | tf_op jit(solution)/shard_map/add | solution.py:85
  176.1 40.3 %fusion.10 = bf16[32,12,10752]{2,0,1:T(8,128)(2,1)} fusion(f32[32,18,10752]{2,0,1:T(8,128)} %multiply_add_fusion), kind=kLoop, calls=%fused_computation.18 | loop fusion | flops 57802752 | bytes 123863040 | tf_op jit(solution)/shard_map/convert_element_type | solution.py:124
  216.5 12.2 %copy.28 = bf16[32,12,10752]{2,1,0:T(8,128)(2,1)} copy(bf16[32,12,10752]{2,0,1:T(8,128)(2,1)} %fusion.10) | data formatting | bytes 16515072 | tf_op jit(solution)/shard_map/convert_element_type | solution.py:124
  228.7 18.6 %convert_element_type.54 = bf16[32,1008,128]{2,1,0:T(8,128)(2,1)} reshape(bf16[32,12,10752]{2,1,0:T(8,128)(2,1)} %copy.28) | data formatting | bytes 16515072 | tf_op jit(solution)/shard_map/convert_element_type | solution.py:124
  247.2 8.6 %copy.29 = bf16[32,1008,128]{2,0,1:T(8,128)(2,1)} copy(bf16[32,1008,128]{2,1,0:T(8,128)(2,1)} %convert_element_type.54) | data formatting | bytes 16515072 | tf_op jit(solution)/shard_map/convert_element_type | solution.py:124
  255.9 5.4 %gather_fusion = bf16[224,32,128]{2,1,0:T(8,128)(2,1)} fusion(bf16[32,1008,128]{2,0,1:T(8,128)(2,1)} %copy.29, s32[1024]{0:T(1024)S(1)} %pad_clamp_fusion), kind=kCustom, calls=%fused_computation | custom fusion | bytes 3670912 | tf_op jit(solution)/shard_map/jit(_take)/gather | solution.py:105
  261.3 2.2 copy.30
  263.5 3.2 gather.11
  266.7 1.7 broadcast_select_fusion
  268.4 0.5 copy.31
  269.0 28.2 %all_to_all.21 = bf16[32,16,1792]{2,0,1:T(8,128)(2,1)S(1)} all-to-all(bf16[32,16,1792]{2,0,1:T(8,128)(2,1)S(1)} %copy.31), channel_id=1, replica_groups=mesh['slab'=8,'grp'=16] {'grp'}, dimensions={1} | all-to-all | bytes 3670016 | tf_op jit(solution)/shard_map/all_to_all | solution.py:127
  297.1 0.4 convert_reduce_fusion.1
  297.6 0.3 fusion.23
  297.9 17.7 %convolution_convert_fusion = bf16[1712,1712]{1,0:T(8,128)(2,1)} fusion(bf16[512,1792]{1,0:T(8,128)(2,1)S(1)} %fusion.23, bf16[1200,1792]{1,0:T(8,128)(2,1)} %param.6), kind=kOutput, calls=%fused_computation.38 | convolution fusion | flops 10519705600 | bytes 11997696 | tf_op jit(solution)/shard_map/dot_general | solution.py:137
  315.6 78.0 %fusion = bf16[112,1712]{1,0:T(8,128)(2,1)S(1)} fusion(bf16[1712,1712]{1,0:T(8,128)(2,1)} %convolution_convert_fusion), kind=kCustom, calls=%all-reduce-scatter | all-reduce-scatter fusion | flops 3067905 | bytes 6245888
  393.7 3.6 collective-permute-start.2
  397.4 0.6 dynamic-slice.4
  398.6 2.9 collective-permute-done.2
  401.5 1.3 concatenate.19
  402.8 0.1 constant_dynamic-slice_fusion
  402.9 1.9 broadcast_in_dim.99
  404.8 4.7 all-to-all-start.1
  409.6 2.2 convert_element_type.68
  411.8 36.8 %all-to-all-done.1 = bf16[8,107,1712]{2,1,0:T(8,128)(2,1)} async-done(((bf16[8,107,1712]{2,1,0:T(8,128)(2,1)}), bf16[8,107,1712]{2,1,0:T(8,128)(2,1)}, u32[]{:S(2)}, u32[]{:S(2)}) %all-to-all-start.1) | async-done | bytes 2930976 | tf_op jit(solution)/shard_map/all_to_all | solution.py:37
  448.6 4.6 convert_reduce_fusion
  453.2 0.1 constant_dynamic-slice_fusion.1
  453.3 1.7 gather_fusion.1
  455.0 0.1 fusion.59
  455.1 0.6 broadcast_in_dim.102
  455.8 6.2 %all-to-all-start.2 = ((f32[16,1,2]{2,1,0:T(1,128)}), f32[16,1,2]{2,1,0:T(1,128)S(1)}, u32[]{:S(2)}, u32[]{:S(2)}) async-start(f32[16,1,2]{2,1,0:T(1,128)} %broadcast_in_dim.102), calls=%async_computation.2 | async-start | bytes 16384 | tf_op jit(solution)/shard_map/all_to_all | solution.py:37
  462.0 2.3 subtract_convert_fusion
  464.3 5.2 %all-to-all-done.2 = f32[16,1,2]{2,1,0:T(1,128)S(1)} async-done(((f32[16,1,2]{2,1,0:T(1,128)}), f32[16,1,2]{2,1,0:T(1,128)S(1)}, u32[]{:S(2)}, u32[]{:S(2)}) %all-to-all-start.2) | async-done | bytes 160 | tf_op jit(solution)/shard_map/all_to_all | solution.py:37
  469.5 0.6 fusion.63
  470.2 3.2 fusion.17
  473.3 3.2 fusion.18
  476.7 10.1 %fusion.19 = bf16[1200,1792]{1,0:T(8,128)(2,1)} fusion(f32[1200,1792]{1,0:T(8,128)S(1)} %fusion.18, f32[1200,1792]{1,0:T(8,128)S(1)} %fusion.17, bf16[1200,1792]{1,0:T(8,128)(2,1)} %param.6, bf16[1712,1200]{0,1:T(8,128)(2,1)} %param.7), kind=kOutput, calls=%fused_computation.37 | convolution fusion | flops 5167411200 | bytes 28876800 | tf_op jit(solution)/shard_map/dot_general | solution.py:157
  486.7 1.0 multiply_multiply_fusion
  (23 shorter events, 0.6 us)
Async XLA Ops:
  5.1 29.9 %collective-permute-start = (bf16[32,3,10752]{2,0,1:T(8,128)(2,1)}, bf16[32,3,10752]{2,0,1:T(8,128)(2,1)S(1)}, u32[]{:S(2)}, u32[]{:S(2)}) collective-permute-start(bf16[32,3,10752]{2,0,1:T(8,128)(2,1)} %get-tuple-element.4), channel_id=1, source_target_pairs={{0,16},{16,32},{32,48},{48,64},{64,80},{80,96},{96,112},{1,17},{17... | collective-permute-start | bytes 6193160 | tf_op jit(solution)/shard_map/ppermute | solution.py:26
  6.5 28.5 %collective-permute-start.1 = (bf16[32,3,10752]{2,0,1:T(8,128)(2,1)}, bf16[32,3,10752]{2,0,1:T(8,128)(2,1)}, u32[]{:S(2)}, u32[]{:S(2)}) collective-permute-start(bf16[32,3,10752]{2,0,1:T(8,128)(2,1)} %get-tuple-element.5), channel_id=1, source_target_pairs={{16,0},{32,16},{48,32},{64,48},{80,64},{96,80},{112,96},{17,1},{33... | collective-permute-start | bytes 6193160 | tf_op jit(solution)/shard_map/ppermute | solution.py:28
  297.9 99.5 %copy-start = (u32[128]{0:T(128)S(1)}, u32[128]{0:T(128)}, u32[]{:S(2)}) copy-start(u32[128]{0:T(128)} %constant.143) | copy-start | bytes 1540
  393.7 7.8 %collective-permute-start.2 = (bf16[75,1712]{1,0:T(8,128)(2,1)S(1)}, bf16[75,1712]{1,0:T(8,128)(2,1)S(1)}, u32[]{:S(2)}, u32[]{:S(2)}) collective-permute-start(bf16[75,1712]{1,0:T(8,128)(2,1)S(1)} %slice.132), channel_id=1, source_target_pairs={{0,1},{1,2},{2,3},{3,4},{4,5},{5,6},{6,7},{7,8},{8,9},{9,10},{10,1... | collective-permute-start | bytes 770408
  404.8 43.8 %all-to-all-start.1 = ((bf16[8,107,1712]{2,1,0:T(8,128)(2,1)}), bf16[8,107,1712]{2,1,0:T(8,128)(2,1)}, u32[]{:S(2)}, u32[]{:S(2)}) async-start(bf16[8,107,1712]{2,1,0:T(8,128)(2,1)} %broadcast_in_dim.99), calls=%async_computation.1 | async-start | bytes 6422528 | tf_op jit(solution)/shard_map/all_to_all | solution.py:37
  455.8 13.7 %all-to-all-start.2 = ((f32[16,1,2]{2,1,0:T(1,128)}), f32[16,1,2]{2,1,0:T(1,128)S(1)}, u32[]{:S(2)}, u32[]{:S(2)}) async-start(f32[16,1,2]{2,1,0:T(1,128)} %broadcast_in_dim.102), calls=%async_computation.2 | async-start | bytes 16384 | tf_op jit(solution)/shard_map/all_to_all | solution.py:37
where the time goes:
time: 498 us; the launch traced here: 488 us
  other arithmetic  195 us (39%)
  blocking collectives  132 us (27%)
  local copies, waits for them, and re-layouts  63.3 us (13%)
  waiting for transfers between devices  44.9 us (9%)
  matrix products  34.1 us (7%)
  starting transfers between devices  17.2 us (3%)
    unnamed x1, blocking collectives  78 us
    add x1, other arithmetic, along_rows(): summed = summed + weights[offset + RAD] * jnp.where(inside, shifted, 0.0)  64.2 us
    add x1, other arithmetic, along_columns(): summed = summed + weights[offset + RAD] * shifted  64 us
    all_to_all x2, waiting for transfers between devices, copy_for_each(): lax.all_to_all(jnp.broadcast_to(value[None], (size, *value.shape)), axis,...  42 us
    convert_element_type x1, other arithmetic, body(): smoothed = along_depth(planar, slab_depth).reshape(frames_here, slab_dept...  40.3 us
    convert_element_type x3, local copies, waits for them, and re-layouts, body(): smoothed = along_depth(planar, slab_depth).reshape(frames_here, slab_dept...  39.4 us
    all_to_all x1, blocking collectives, body(): lax.all_to_all(picked, 'grp', split_axis=1, concat_axis=0, tiled=True)  28.2 us
    all_gather x1, blocking collectives, body(): lax.all_gather(mask_index, 'grp', axis=0, tiled=True)  25.8 us
  transfers between devices with their start and end apart: 5, of which 3 were waited for; matrix products, arithmetic and copies ran while one was open for 1% of the time, Pallas kernels for 0%

commit v1 on v0

v1 whole, which is shorter than its diff:
```python
import functools
import math

import jax
import jax.numpy as jnp
import numpy as np
from jax import lax
from jax.experimental import pallas as pl
from jax.experimental.pallas import tpu as pltpu
from jax.sharding import Mesh
from jax.sharding import PartitionSpec as P

NX = 96
RUN = 128
RAD = 3
K = 1200
KX = 1712
SUBJ = 256
ROWS = 107
WIN = 120
LEAD = 384
BLOCK = 256
PHASES = 3
GRP = 16
TAB = 64
TAB_MID = 31

smooth_sigma = 1.0617
epsilon = 1e-06


def tap_weights():
    unscaled = [
        math.exp(-offset * offset / (2.0 * smooth_sigma * smooth_sigma))
        for offset in range(-RAD, RAD + 1)
    ]
    summed = sum(unscaled)
    return [weight / summed for weight in unscaled]


def plane_matrix():
    taps = np.array(tap_weights())
    cells_in = np.arange(LEAD + BLOCK + LEAD)[:, None]
    cells_out = np.arange(BLOCK)[None, :]
    parts = []
    for phase in range(PHASES):
        column = (phase * BLOCK + cells_out) % NX
        reach = cells_in - LEAD - cells_out
        rows = np.floor((reach + NX // 2) / NX).astype(np.int64)
        along = reach - rows * NX
        ok = (np.abs(rows) <= RAD) & (np.abs(along) <= RAD) & (column + along >= 0) & (column + along < NX)
        weight = taps[np.clip(rows + RAD, 0, 2 * RAD)] * taps[np.clip(along + RAD, 0, 2 * RAD)]
        parts.append(np.where(ok, weight, 0.0))
    return np.stack(parts).astype(np.float32)


def depth_table():
    table = np.zeros((TAB,), np.float32)
    table[TAB_MID - RAD : TAB_MID + RAD + 1] = tap_weights()
    return table


def smooth_kernel(depth, own_ref, near_ref, tab_ref, mat_ref, raw_ref, mid_ref, rim_ref, up_ref, down_ref, pad, planar, sems):
    frames = raw_ref.shape[1]
    extent = raw_ref.shape[2]
    step = PHASES * BLOCK
    steps = extent // step
    tiles = extent // RUN

    def fetch(i):
        return pltpu.make_async_copy(
            raw_ref.at[:, :, pl.ds(i * step, step)],
            pad.at[:, :, pl.ds(LEAD + i * step, step)],
            sems.at[i],
        )

    for i in range(steps):
        fetch(i).start()
    edge = jnp.zeros((depth, frames, LEAD), pad.dtype)
    pad[:, :, :LEAD] = edge
    pad[:, :, LEAD + extent :] = edge
    fetch(0).wait()

    def block(i, carry):
        @pl.when(i + 1 < steps)
        def _():
            fetch(i + 1).wait()

        for phase in range(PHASES):
            start = pl.multiple_of(i * step + phase * BLOCK, BLOCK)
            cells = pad[:, :, pl.ds(start, LEAD + BLOCK + LEAD)].reshape(depth * frames, LEAD + BLOCK + LEAD)
            out = jnp.dot(cells, mat_ref[phase], preferred_element_type=jnp.float32)
            planar[:, :, pl.ds(start, BLOCK)] = out.reshape(depth, frames, BLOCK)
        return carry

    lax.fori_loop(0, steps, block, 0)

    taps = tap_weights()

    def place(tile):
        plane = tile // tiles
        return plane, pl.multiple_of((tile - plane * tiles) * RUN, RUN)

    per = mid_ref.shape[2] // RUN

    def middle(g, carry):
        for j in range(per):
            plane, lane = place(own_ref[(g + GRP // 4) * per + j])
            total = taps[0] * planar[plane - RAD, :, pl.ds(lane, RUN)]
            for k in range(1, 2 * RAD + 1):
                total = total + taps[k] * planar[plane - RAD + k, :, pl.ds(lane, RUN)]
            mid_ref[g, :, j * RUN : (j + 1) * RUN] = total.astype(mid_ref.dtype)
        return carry

    def some(tile, first, count, shift):
        plane, lane = place(tile)
        total = None
        for q in range(first, first + count):
            weight = tab_ref[q - plane + shift + TAB_MID]
            term = weight * planar[q, :, pl.ds(lane, RUN)]
            total = term if total is None else total + term
        return total

    def rims(g, carry):
        for j in range(per):
            cols = slice(j * RUN, (j + 1) * RUN)
            at = g * per + j
            up_ref[g, :, cols] = some(near_ref[at], depth - RAD, RAD, -depth)
            down_ref[g, :, cols] = some(near_ref[GRP // 4 * per + at], 0, RAD, depth)
            rim_ref[g, :, cols] = some(own_ref[at], 0, 2 * RAD, 0)
            rim_ref[GRP // 4 + g, :, cols] = some(own_ref[GRP * 3 // 4 * per + at], depth - 2 * RAD, 2 * RAD, 0)
        return carry

    lax.fori_loop(0, GRP // 4, rims, 0)
    lax.fori_loop(0, GRP // 2, middle, 0)


def smooth(own, near, raw):
    depth, frames, extent = raw.shape
    per_device = own.shape[0] // GRP * RUN
    smem = pl.BlockSpec(memory_space=pltpu.SMEM)
    vmem = pl.BlockSpec(memory_space=pltpu.VMEM)
    quarter = (GRP // 4, frames, per_device)
    half = (GRP // 2, frames, per_device)
    return pl.pallas_call(
        functools.partial(smooth_kernel, depth),
        out_shape=[
            jax.ShapeDtypeStruct(half, jnp.bfloat16),
            jax.ShapeDtypeStruct(half, jnp.float32),
            jax.ShapeDtypeStruct(quarter, jnp.float32),
            jax.ShapeDtypeStruct(quarter, jnp.float32),
        ],
        in_specs=[smem, smem, smem, vmem, pl.BlockSpec(memory_space=pl.ANY)],
        out_specs=[vmem] * 4,
        scratch_shapes=[
            pltpu.VMEM((depth, frames, extent + 2 * LEAD), jnp.bfloat16),
            pltpu.VMEM((depth, frames, extent), jnp.float32),
            pltpu.SemaphoreType.DMA((extent // (PHASES * BLOCK),)),
        ],
        compiler_params=pltpu.CompilerParams(vmem_limit_bytes=48 * 1024 * 1024),
        name="smooth",
    )(own, near, jnp.asarray(depth_table()), jnp.asarray(plane_matrix()).astype(jnp.bfloat16), raw)


def window_starts(length, count, window, total):
    return [min(8 * (length * i // 8), total - window) for i in range(count)]


def copies(value, axis, count):
    return lax.all_to_all(jnp.broadcast_to(value[None], (count, *value.shape)), axis, 0, 0, tiled=True)


def body(raw_frames, mask_index, subspace, rotation):
    depth = raw_frames.shape[1]
    extent = raw_frames.shape[2]
    per_device = subspace.shape[1]
    slab = ("x", "core")
    masked = per_device * 8 * GRP
    slab_at = lax.axis_index("x") * 2 + lax.axis_index("core")
    core = lax.axis_index("core")
    grp = lax.axis_index("grp")
    bf16 = jnp.bfloat16
    f32 = jnp.float32
    swap = [(0, 1), (1, 0)]

    tiles = mask_index.reshape(-1, RUN)[:, 0] // RUN - slab_at * (depth * extent // RUN)
    up = [(i, i + 1) for i in range(7)]
    down = [(i + 1, i) for i in range(7)]
    packed = jnp.stack([tiles, lax.ppermute(tiles, slab, up), lax.ppermute(tiles, slab, down)])
    every = copies(packed, "grp", GRP)
    own = every[:, 0].reshape(-1)
    near = jnp.concatenate([every[: GRP // 4, 2].reshape(-1), every[3 * GRP // 4 :, 1].reshape(-1)])

    mid, rim, to_up, to_down = smooth(own, near, jnp.transpose(raw_frames, (1, 0, 2)))
    from_low = lax.ppermute(to_up, slab, up)
    from_high = lax.ppermute(to_down, slab, down)
    quarter = GRP // 4
    low = (rim[:quarter] + from_low).astype(bf16)
    high = (rim[quarter:] + from_high).astype(bf16)
    regrouped = lax.all_to_all(jnp.concatenate([low, mid, high]), "grp", 0, 0, tiled=True)

    across = (((1,), (1,)), ((), ()))
    col_starts = window_starts(150, 8, 160, K)
    starts = jnp.array(col_starts, jnp.int32)

    def some_rows(which):
        return jnp.concatenate(
            [lax.dynamic_slice_in_dim(subspace, starts[2 * x + which], 160, 0) for x in range(4)]
        )

    other_ss = lax.dot_general(some_rows(1 - core), subspace, across, preferred_element_type=f32).astype(bf16)
    got_ss = lax.ppermute(other_ss, "core", swap)
    own_ss = lax.dot_general(some_rows(core), subspace, across, preferred_element_type=f32)
    pair_ss = (own_ss + got_ss.astype(f32)).astype(bf16).reshape(4, 160, K)
    slab_ss = jnp.sum(lax.all_to_all(pair_ss, "x", 0, 0, tiled=True).astype(f32), axis=0)
    row_starts = window_starts(ROWS, GRP, WIN, KX + 0)
    tall = jnp.pad(slab_ss.astype(bf16).T, ((0, KX - K), (0, 0)))
    by_row = jnp.stack([tall[a : a + WIN] for a in row_starts])
    grp_ss = jnp.sum(lax.all_to_all(by_row, "grp", 0, 0, tiled=True).astype(f32), axis=0).astype(bf16)
    all_ss = copies(grp_ss, slab, 8)
    rows_ss = jnp.concatenate(
        [all_ss[p][:, 150 * p - col_starts[p] : 150 * p - col_starts[p] + 150] for p in range(8)], axis=1
    )

    contract = (((0,), (0,)), ((), ()))
    from_basis = lax.dot_general(rotation[:K], subspace, contract, preferred_element_type=f32)

    halves = regrouped.astype(f32).reshape(2, SUBJ, per_device)
    centered = (halves - jnp.mean(halves, axis=1, keepdims=True)).astype(bf16)
    wide = centered.astype(f32)
    partial_power = jnp.sum(wide * wide, axis=(1, 2))
    power = jnp.sum(copies(partial_power[None], ("x", "core", "grp"), 8 * GRP), axis=(0, 1))
    scales = lax.rsqrt(power / (masked * SUBJ) + epsilon)

    def data_columns(which):
        mine = lax.dynamic_index_in_dim(centered, which, 0, keepdims=False)
        return jnp.concatenate(
            [
                lax.dot_general(subspace, mine, across, preferred_element_type=f32),
                lax.dot_general(centered.reshape(2 * SUBJ, per_device), mine, across, preferred_element_type=f32),
            ]
        )

    got_c = lax.ppermute(data_columns(1 - core).astype(bf16), "core", swap)
    pair_c = (data_columns(core) + got_c.astype(f32)).astype(bf16)
    by_row_c = jnp.stack([pair_c[a : a + WIN] for a in row_starts])
    grp_c = jnp.sum(lax.all_to_all(by_row_c, "grp", 0, 0, tiled=True).astype(f32), axis=0).astype(bf16)
    all_c = copies(grp_c, slab, 8).astype(f32).reshape(4, 2, WIN, SUBJ)
    sum_c = jnp.sum(all_c, axis=0)
    first_row = grp * ROWS
    offset = first_row - jnp.array(row_starts, jnp.int32)[grp]
    rows_c = lax.dynamic_slice_in_dim(jnp.concatenate([sum_c[0], sum_c[1]], axis=1), offset, ROWS, 0)

    first_data = K // ROWS
    data_devices = GRP - first_data
    wanted = np.zeros((data_devices, ROWS, 2 * SUBJ), np.float32)
    for d in range(data_devices):
        for i in range(ROWS):
            at = (first_data + d) * ROWS + i - K
            if at >= 0:
                wanted[d, i, at] = 1.0
    turned = lax.dot_general(
        jnp.asarray(wanted).astype(bf16), rows_c.astype(bf16), (((2,), (1,)), ((), ())), preferred_element_type=f32
    ).astype(bf16)
    turned = jnp.concatenate([jnp.zeros((first_data, ROWS, ROWS), bf16), turned])
    back = lax.all_to_all(turned, "grp", 0, 0, tiled=True)
    rows_t = jnp.transpose(back[: first_data + 1], (1, 0, 2)).reshape(ROWS, (first_data + 1) * ROWS)[:, :K]
    rows_ss = lax.dynamic_slice_in_dim(rows_ss, offset, ROWS, 0)
    row_number = first_row + lax.broadcasted_iota(jnp.int32, (ROWS, 1), 0)
    left = jnp.where(row_number < K, rows_ss.astype(f32), rows_t.astype(f32))
    owned = jnp.concatenate([left, rows_c], axis=1)

    row_scale = jnp.concatenate([jnp.ones((K,), f32), jnp.repeat(scales, SUBJ)])
    owned_scale = lax.dynamic_slice_in_dim(row_scale, first_row, ROWS, 0)
    gram_rows = owned * (owned_scale[:, None] * row_scale[None, :]) / masked

    from_first = lax.dot_general(rotation[K : K + SUBJ], centered[0], contract, preferred_element_type=f32)
    from_second = lax.dot_general(rotation[K + SUBJ :], centered[1], contract, preferred_element_type=f32)
    new_subspace = (from_basis + scales[0] * from_first + scales[1] * from_second).astype(bf16)
    return (gram_rows, new_subspace)


def solution(mesh):
    fine = Mesh(mesh.devices.reshape(4, 2, GRP), ("x", "core", "grp"))
    slab = ("x", "core")
    placed = (P("grp", slab, None), P((*slab, "grp")), P(None, (*slab, "grp")), P())
    return jax.shard_map(
        body,
        mesh=fine,
        in_specs=placed,
        out_specs=(P("grp", None), P(None, (*slab, "grp"))),
        check_vma=False,
    )
```

time: 498 us -> 267 us (0.54); the launches traced: 488 us -> 266 us
  other arithmetic: 195 us -> 12.3 us
  blocking collectives: 132 us -> 0 us
  starting transfers between devices: 17.2 us -> 73.4 us
  local copies, waits for them, and re-layouts: 63.3 us -> 42 us
  matrix products: 34.1 us -> 51.9 us
  Pallas kernels: 0 us -> 17.6 us
  between operations: 2.01 us -> 16.6 us
  waiting for transfers between devices: 44.9 us -> 51.7 us
    add x2 -> x0, other arithmetic: 128 us -> none  [the longest x1 64.2 us: along_rows(): summed = summed + weights[offset + RAD] * jnp.where(inside, shifted, 0.0)]
    unnamed x1 -> x0, blocking collectives: 78 us -> none
    convert_element_type x5 -> x4, other arithmetic: 58.1 us -> 2.83 us  [the longest x1 1.95 us: body(): pair_c = (data_columns(core) + got_c.astype(f32)).astype(bf16)]
    all_to_all x2 -> x9, starting transfers between devices: 10.9 us -> 61.9 us  [the longest x4 34.9 us: copies(): lax.all_to_all(jnp.broadcast_to(value[None], (count, *value.shape)), axis...]
    convert_element_type x3 -> x1, local copies, waits for them, and re-layouts: 39.4 us -> 2.19 us  [body(): pair_ss = (own_ss + got_ss.astype(f32)).astype(bf16).reshape(4, 160, K)]
    all_to_all x1 -> x0, blocking collectives: 28.2 us -> none  [body(): lax.all_to_all(picked, 'grp', split_axis=1, concat_axis=0, tiled=True)]
    all_gather x1 -> x0, blocking collectives: 25.8 us -> none  [body(): lax.all_gather(mask_index, 'grp', axis=0, tiled=True)]
    unnamed x10 -> x51, local copies, waits for them, and re-layouts: 2.84 us -> 27.2 us
  transfers between devices with their start and end apart: 5 -> 15, of which waited for: 3 -> 7; matrix products, arithmetic and copies ran while one was open for 1% -> 31% of each run, Pallas kernels for 0% -> 0%
where the time goes in v1:
time: 267 us; the launch traced here: 266 us
  starting transfers between devices  73.4 us (27%)
  matrix products  51.9 us (19%)
  waiting for transfers between devices  51.7 us (19%)
  local copies, waits for them, and re-layouts  42 us (16%)
  Pallas kernels  17.6 us (7%)
  between operations  16.6 us (6%)
  other arithmetic  12.3 us (5%)
    all_to_all x4, starting transfers between devices, copies(): lax.all_to_all(jnp.broadcast_to(value[None], (count, *value.shape)), axis...  34.9 us
    unnamed x51, local copies, waits for them, and re-layouts  27.2 us
    pallas_call x1, Pallas kernels, smooth(): pl.pallas_call(functools.partial(smooth_kernel, depth), out_shape=[jax.Sh...  17.6 us
    dot_general x1, matrix products, body(): lax.dot_general(rotation[:K], subspace, contract, preferred_element_type=...  13.7 us
    all_to_all x1, waiting for transfers between devices, body(): lax.all_to_all(jnp.concatenate([low, mid, high]), 'grp', 0, 0, tiled=True)  11 us
    all_to_all x1, waiting for transfers between devices, body(): lax.all_to_all(pair_ss, 'x', 0, 0, tiled=True).astype(f32)  11 us
    all_to_all x1, waiting for transfers between devices, body(): lax.all_to_all(by_row_c, 'grp', 0, 0, tiled=True).astype(f32)  11 us
    all_to_all x4, waiting for transfers between devices, copies(): lax.all_to_all(jnp.broadcast_to(value[None], (count, *value.shape)), axis...  9.69 us
  transfers between devices with their start and end apart: 15, of which 7 were waited for; matrix products, arithmetic and copies ran while one was open for 31% of the time, Pallas kernels for 0%

profile of v1, /device:TPU:0, one launch (start us, length us, event | category | flops | bytes accessed | tf_op | source)
XLA Modules:
  0.0 265.5 jit_solution(3553005367707328634)
XLA Ops:
  1.5 1.3 collective-permute-start.2
  2.8 3.0 %collective-permute-start.1 = (s32[14]{0:T(128)S(1)}, s32[14]{0:T(128)S(1)}, u32[]{:S(2)}, u32[]{:S(2)}) collective-permute-start(s32[14]{0:T(128)S(1)} %fusion.46), channel_id=1, source_target_pairs={{0,16},{16,32},{32,48},{48,64},{64,80},{80,96},{96,112},{1,17},{17... | collective-permute-start | bytes 176 | tf_op jit(solution)/shard_map/ppermute | solution.py:189
  7.2 8.2 %all-to-all-start.3 = ((s32[16,3,14]{2,1,0:T(4,128)}), s32[16,3,14]{2,1,0:T(4,128)S(1)}, u32[]{:S(2)}, u32[]{:S(2)}) async-start(s32[16,3,14]{2,1,0:T(4,128)} %broadcast_in_dim.17), calls=%async_computation.3 | async-start | bytes 65536 | tf_op jit(solution)/shard_map/all_to_all | solution.py:170
  15.4 1.7 fusion.51
  32.4 1.4 copy-done
  34.5 17.6 %smooth.1 = (bf16[8,32,1792]{2,1,0:T(8,128)(2,1)S(1)}, f32[8,32,1792]{2,1,0:T(8,128)S(1)}, f32[4,32,1792]{2,1,0:T(8,128)S(1)}, f32[4,32,1792]{2,1,0:T(8,128)S(1)}) custom-call(s32[224]{0:T(256)S(1)} %reshape_squeeze.9.own_ref, s32[112]{0:T(128)S(1)} %pad_add_fusion.1.near_ref, f32[64]{0:T(128)S(1)} %copy-done.1, bf16[3,1024,256]{2,1,0:T(8,128)(2,1)S(1)} %copy-done, ...), custom_call_target="tpu_custom_call" | custom-call | tf_op jit(solution)/shard_map/smooth/pallas_call | solution.py:145
  52.2 2.7 %collective-permute-start.3 = (f32[4,32,1792]{2,1,0:T(8,128)S(1)}, f32[4,32,1792]{2,1,0:T(8,128)S(1)}, u32[]{:S(2)}, u32[]{:S(2)}) collective-permute-start(f32[4,32,1792]{2,1,0:T(8,128)S(1)} %get-tuple-element.7), channel_id=1, source_target_pairs={{0,16},{16,32},{32,48},{48,64},{64,80},{80,96},{96,112},{1,17},{17... | collective-permute-start | bytes 2752520 | tf_op jit(solution)/shard_map/ppermute | solution.py:195
  54.9 1.3 collective-permute-start.4
  56.2 1.6 constant_dynamic-slice_fusion.7
  57.8 4.7 %convolution_convert_fusion = bf16[640,1200]{0,1:T(8,128)(2,1)} fusion(bf16[1200,1792]{1,0:T(8,128)(2,1)S(1)} %copy-done.2, bf16[160,1792]{1,0:T(8,128)(2,1)S(1)} %get-tuple-element.25, bf16[160,1792]{1,0:T(8,128)(2,1)S(1)} %get-tuple-element.26, bf16[160,1792]{1,0:T(8,128)(2,1)S(1)} %get-tuple-element.27, bf16[160,1792]{1,0:T(8,128)(2,1)S(1)} %get-tuple-element.28), kind=kOutput, calls=%fused_computation.11 | convolution fusion | flops 2762455040 | bytes 8130560 | tf_op jit(solution)/shard_map/dot_general | solution.py:211
  62.5 3.2 %collective-permute-start = (bf16[640,1200]{0,1:T(8,128)(2,1)}, bf16[640,1200]{0,1:T(8,128)(2,1)S(1)}, u32[]{:S(2)}, u32[]{:S(2)}) collective-permute-start(bf16[640,1200]{0,1:T(8,128)(2,1)} %convolution_convert_fusion), channel_id=1, source_target_pairs={{0,16},{16,0},{1,17},{17,1},{2,18},{18,2},{3,19},{19,3},{4,20},{20... | collective-permute-start | bytes 4608008 | tf_op jit(solution)/shard_map/ppermute | solution.py:212
  65.9 1.4 pad_maximum_fusion
  67.3 7.2 %all-to-all-start.4 = ((bf16[16,32,1792]{2,1,0:T(8,128)(2,1)}), bf16[16,32,1792]{2,1,0:T(8,128)(2,1)S(1)}, u32[]{:S(2)}, u32[]{:S(2)}) async-start(bf16[16,32,1792]{2,1,0:T(8,128)(2,1)} %pad_maximum_fusion), calls=%async_computation.4 | async-start | bytes 3670016 | tf_op jit(solution)/shard_map/all_to_all | solution.py:200
  75.7 1.1 copy-done.7
  76.9 6.9 %add_convert_fusion = bf16[640,1200]{0,1:T(8,128)(2,1)S(1)} fusion(bf16[640,1200]{0,1:T(8,128)(2,1)} %copy-done.7, bf16[1200,1792]{1,0:T(8,128)(2,1)} %param.11, bf16[160,1792]{1,0:T(8,128)(2,1)} %get-tuple-element.29, bf16[160,1792]{1,0:T(8,128)(2,1)} %get-tuple-element.30, bf16[160,1792]{1,0:T(8,128)(2,1)} %get-tuple-element.31, ...), kind=kOutput, calls=%fused_computation.13 | convolution fusion | flops 2763991040 | bytes 9666560 | tf_op jit(solution)/shard_map/dot_general | solution.py:213
  83.8 2.2 copy.24
  86.0 11.0 %all-to-all-done.4 = bf16[16,32,1792]{2,1,0:T(8,128)(2,1)S(1)} async-done(((bf16[16,32,1792]{2,1,0:T(8,128)(2,1)}), bf16[16,32,1792]{2,1,0:T(8,128)(2,1)S(1)}, u32[]{:S(2)}, u32[]{:S(2)}) %all-to-all-start.4) | async-done | bytes 1835040 | tf_op jit(solution)/shard_map/all_to_all | solution.py:200
  97.4 2.0 multiply_reduce_fusion
  100.2 18.6 %all-to-all-start.8 = ((f32[128,1,2]{2,1,0:T(1,128)}), f32[128,1,2]{2,1,0:T(1,128)S(1)}, u32[]{:S(2)}, u32[]{:S(2)}) async-start(f32[128,1,2]{2,1,0:T(1,128)} %broadcast_in_dim.19), calls=%async_computation.8 | async-start | bytes 131072 | tf_op jit(solution)/shard_map/all_to_all | solution.py:170
  119.5 4.5 %fusion.6 = bf16[1200,256]{1,0:T(8,128)(2,1)} fusion(bf16[1200,1792]{1,0:T(8,128)(2,1)} %param.11, bf16[2,256,1792]{2,1,0:T(8,128)(2,1)S(1)} %fusion.4, s32[]{:T(128)S(6)} %select_n.104), kind=kOutput, calls=%fused_computation.16 | convolution fusion | flops 1101312000 | bytes 5832708 | tf_op jit(solution)/shard_map/dot_general | solution.py:239
  124.0 1.4 convolution_convert_fusion.2
  125.4 2.8 %all-to-all-done.8 = f32[128,1,2]{2,1,0:T(1,128)S(1)} async-done(((f32[128,1,2]{2,1,0:T(1,128)}), f32[128,1,2]{2,1,0:T(1,128)S(1)}, u32[]{:S(2)}, u32[]{:S(2)}) %all-to-all-start.8) | async-done | bytes 1056 | tf_op jit(solution)/shard_map/all_to_all | solution.py:170
  128.2 3.6 %all-to-all-start = ((bf16[4,160,1200]{2,1,0:T(8,128)(2,1)}), bf16[4,160,1200]{2,1,0:T(8,128)(2,1)S(1)}, u32[]{:S(2)}, u32[]{:S(2)}) async-start(bf16[4,160,1200]{2,1,0:T(8,128)(2,1)} %bitcast.8), calls=%async_computation | async-start | bytes 3276800 | tf_op jit(solution)/shard_map/all_to_all | solution.py:215
  131.7 2.1 pad_maximum_fusion.1
  133.9 3.0 %fusion.28 = f32[512,256]{1,0:T(8,128)} fusion(bf16[512,1792]{1,0:T(8,128)(2,1)} %bitcast.230, bf16[2,256,1792]{2,1,0:T(8,128)(2,1)S(1)} %fusion.4, s32[]{:T(128)S(6)} %select_n.103), kind=kOutput, calls=%fused_computation.44 | convolution fusion | flops 469762048 | bytes 3276804 | tf_op jit(solution)/shard_map/dot_general | solution.py:240
  136.8 4.6 %convolution_bitcast_fusion = f32[1200,256]{1,0:T(8,128)} fusion(bf16[1200,1792]{1,0:T(8,128)(2,1)} %param.11, bf16[2,256,1792]{2,1,0:T(8,128)(2,1)S(1)} %fusion.4, s32[]{:T(128)S(6)} %select_n.103), kind=kOutput, calls=%fused_computation.14 | convolution fusion | flops 1101004800 | bytes 6447108 | tf_op jit(solution)/shard_map/dot_general | solution.py:239
  142.1 11.0 %all-to-all-done = bf16[4,160,1200]{2,1,0:T(8,128)(2,1)S(1)} async-done(((bf16[4,160,1200]{2,1,0:T(8,128)(2,1)}), bf16[4,160,1200]{2,1,0:T(8,128)(2,1)S(1)}, u32[]{:S(2)}, u32[]{:S(2)}) %all-to-all-start) | async-done | bytes 1536032 | tf_op jit(solution)/shard_map/all_to_all | solution.py:215
  153.1 1.1 reduce_sum.86
  156.0 1.0 constant_dynamic-update-slice_fusion.13
  156.9 1.0 constant_dynamic-update-slice_fusion.12
  157.9 1.0 constant_dynamic-update-slice_fusion.11
  158.9 1.0 constant_dynamic-update-slice_fusion.10
  161.7 1.0 constant_dynamic-update-slice_fusion.7
  163.5 1.9 fusion.24
  175.5 4.9 %all-to-all-start.5 = ((bf16[16,120,256]{2,1,0:T(8,128)(2,1)}), bf16[16,120,256]{2,1,0:T(8,128)(2,1)S(1)}, u32[]{:S(2)}, u32[]{:S(2)}) async-start(bf16[16,120,256]{2,1,0:T(8,128)(2,1)} %constant_dynamic-update-slice_fusion.16), calls=%async_computation.5 | async-start | bytes 1966080 | tf_op jit(solution)/shard_map/all_to_all | solution.py:247
  185.0 11.0 %all-to-all-done.5 = bf16[16,120,256]{2,1,0:T(8,128)(2,1)S(1)} async-done(((bf16[16,120,256]{2,1,0:T(8,128)(2,1)}), bf16[16,120,256]{2,1,0:T(8,128)(2,1)S(1)}, u32[]{:S(2)}, u32[]{:S(2)}) %all-to-all-start.5) | async-done | bytes 983072 | tf_op jit(solution)/shard_map/all_to_all | solution.py:247
  195.9 4.3 %all-to-all-start.1 = ((bf16[16,120,160]{1,2,0:T(8,128)(2,1)}), bf16[16,120,160]{1,2,0:T(8,128)(2,1)}, u32[]{:S(2)}, u32[]{:S(2)}) async-start(bf16[16,120,160]{1,2,0:T(8,128)(2,1)} %constant_dynamic-update-slice_fusion), calls=%async_computation.1 | async-start | bytes 1310720 | tf_op jit(solution)/shard_map/all_to_all | solution.py:219
  200.2 6.4 %fusion.2 = f32[1200,1792]{1,0:T(8,128)} fusion(f32[]{:T(128)} %bitcast.68, bf16[2,256,1792]{2,1,0:T(8,128)(2,1)S(1)} %fusion.4, bf16[1712,1200]{0,1:T(8,128)(2,1)} %param.12), kind=kOutput, calls=%fused_computation.5 | convolution fusion | flops 1103155200 | bytes 10134016 | tf_op jit(solution)/shard_map/dot_general | solution.py:278
  206.6 6.4 %fusion.1 = f32[1200,1792]{1,0:T(8,128)} fusion(f32[]{:T(128)} %bitcast.65, bf16[2,256,1792]{2,1,0:T(8,128)(2,1)S(1)} %fusion.4, bf16[1712,1200]{0,1:T(8,128)(2,1)} %param.12), kind=kOutput, calls=%fused_computation.4 | convolution fusion | flops 1103155200 | bytes 10134016 | tf_op jit(solution)/shard_map/dot_general | solution.py:277
  214.0 3.5 %all-to-all-start.6 = ((bf16[8,120,256]{2,1,0:T(8,128)(2,1)}), bf16[8,120,256]{2,1,0:T(8,128)(2,1)S(1)}, u32[]{:S(2)}, u32[]{:S(2)}) async-start(bf16[8,120,256]{2,1,0:T(8,128)(2,1)} %broadcast_in_dim.18), calls=%async_computation.6 | async-start | bytes 983040 | tf_op jit(solution)/shard_map/all_to_all | solution.py:170
  217.5 13.7 %fusion.3 = bf16[1200,1792]{1,0:T(8,128)(2,1)} fusion(f32[1200,1792]{1,0:T(8,128)} %fusion.2, f32[1200,1792]{1,0:T(8,128)} %fusion.1, bf16[1200,1792]{1,0:T(8,128)(2,1)} %param.11, bf16[1712,1200]{0,1:T(8,128)(2,1)} %param.12), kind=kOutput, calls=%fused_computation.6 | convolution fusion | flops 5167411200 | bytes 28876800 | tf_op jit(solution)/shard_map/dot_general | solution.py:226
  231.3 1.3 reduce_sum.87
  233.4 4.7 %all-to-all-start.2 = ((bf16[8,120,160]{1,2,0:T(8,128)(2,1)}), bf16[8,120,160]{1,2,0:T(8,128)(2,1)S(1)}, u32[]{:S(2)}, u32[]{:S(2)}) async-start(bf16[8,120,160]{1,2,0:T(8,128)(2,1)} %broadcast_in_dim.16), calls=%async_computation.2 | async-start | bytes 655360 | tf_op jit(solution)/shard_map/all_to_all | solution.py:170
  239.4 6.9 %all-to-all-done.2 = bf16[8,120,160]{1,2,0:T(8,128)(2,1)S(1)} async-done(((bf16[8,120,160]{1,2,0:T(8,128)(2,1)}), bf16[8,120,160]{1,2,0:T(8,128)(2,1)S(1)}, u32[]{:S(2)}, u32[]{:S(2)}) %all-to-all-start.2) | async-done | bytes 307232 | tf_op jit(solution)/shard_map/all_to_all | solution.py:170
  246.3 7.1 %all-to-all-start.7 = ((bf16[16,107,107]{1,2,0:T(8,128)(2,1)}), bf16[16,107,107]{1,2,0:T(8,128)(2,1)S(1)}, u32[]{:S(2)}, u32[]{:S(2)}) async-start(bf16[16,107,107]{1,2,0:T(8,128)(2,1)} %concatenate.42), calls=%async_computation.7 | async-start | bytes 917504 | tf_op jit(solution)/shard_map/all_to_all | solution.py:266
  253.7 1.5 concatenate.36
  255.3 8.4 %all-to-all-done.7 = bf16[16,107,107]{1,2,0:T(8,128)(2,1)S(1)} async-done(((bf16[16,107,107]{1,2,0:T(8,128)(2,1)}), bf16[16,107,107]{1,2,0:T(8,128)(2,1)S(1)}, u32[]{:S(2)}, u32[]{:S(2)}) %all-to-all-start.7) | async-done | bytes 366400 | tf_op jit(solution)/shard_map/all_to_all | solution.py:266
  264.3 1.2 copy.27
  (105 shorter events, 29.9 us)
Async XLA Ops:
  1.5 4.4 %collective-permute-start.2 = (s32[14]{0:T(128)S(1)}, s32[14]{0:T(128)S(1)}, u32[]{:S(2)}, u32[]{:S(2)}) collective-permute-start(s32[14]{0:T(128)S(1)} %fusion.46), channel_id=1, source_target_pairs={{16,0},{32,16},{48,32},{64,48},{80,64},{96,80},{112,96},{17,1},{33... | collective-permute-start | bytes 176 | tf_op jit(solution)/shard_map/ppermute | solution.py:189
  2.8 3.8 %collective-permute-start.1 = (s32[14]{0:T(128)S(1)}, s32[14]{0:T(128)S(1)}, u32[]{:S(2)}, u32[]{:S(2)}) collective-permute-start(s32[14]{0:T(128)S(1)} %fusion.46), channel_id=1, source_target_pairs={{0,16},{16,32},{32,48},{48,64},{64,80},{80,96},{96,112},{1,17},{17... | collective-permute-start | bytes 176 | tf_op jit(solution)/shard_map/ppermute | solution.py:189
  7.2 24.8 %all-to-all-start.3 = ((s32[16,3,14]{2,1,0:T(4,128)}), s32[16,3,14]{2,1,0:T(4,128)S(1)}, u32[]{:S(2)}, u32[]{:S(2)}) async-start(s32[16,3,14]{2,1,0:T(4,128)} %broadcast_in_dim.17), calls=%async_computation.3 | async-start | bytes 65536 | tf_op jit(solution)/shard_map/all_to_all | solution.py:170
  32.4 1.4 copy-start
  33.8 0.7 copy-start.1
  34.5 21.7 %copy-start.2 = (bf16[1200,1792]{1,0:T(8,128)(2,1)S(1)}, bf16[1200,1792]{1,0:T(8,128)(2,1)}, u32[]{:S(2)}) copy-start(bf16[1200,1792]{1,0:T(8,128)(2,1)} %param.11) | copy-start | bytes 12902404
  52.2 13.5 %collective-permute-start.3 = (f32[4,32,1792]{2,1,0:T(8,128)S(1)}, f32[4,32,1792]{2,1,0:T(8,128)S(1)}, u32[]{:S(2)}, u32[]{:S(2)}) collective-permute-start(f32[4,32,1792]{2,1,0:T(8,128)S(1)} %get-tuple-element.7), channel_id=1, source_target_pairs={{0,16},{16,32},{32,48},{48,64},{64,80},{80,96},{96,112},{1,17},{17... | collective-permute-start | bytes 2752520 | tf_op jit(solution)/shard_map/ppermute | solution.py:195
  54.9 10.8 %collective-permute-start.4 = (f32[4,32,1792]{2,1,0:T(8,128)S(1)}, f32[4,32,1792]{2,1,0:T(8,128)S(1)}, u32[]{:S(2)}, u32[]{:S(2)}) collective-permute-start(f32[4,32,1792]{2,1,0:T(8,128)S(1)} %get-tuple-element.9), channel_id=1, source_target_pairs={{16,0},{32,16},{48,32},{64,48},{80,64},{96,80},{112,96},{17,1},{33... | collective-permute-start | bytes 2752520 | tf_op jit(solution)/shard_map/ppermute | solution.py:196
  62.5 13.2 %collective-permute-start = (bf16[640,1200]{0,1:T(8,128)(2,1)}, bf16[640,1200]{0,1:T(8,128)(2,1)S(1)}, u32[]{:S(2)}, u32[]{:S(2)}) collective-permute-start(bf16[640,1200]{0,1:T(8,128)(2,1)} %convolution_convert_fusion), channel_id=1, source_target_pairs={{0,16},{16,0},{1,17},{17,1},{2,18},{18,2},{3,19},{19,3},{4,20},{20... | collective-permute-start | bytes 4608008 | tf_op jit(solution)/shard_map/ppermute | solution.py:212
  65.9 8.7 %copy-start.8 = (s32[16]{0:T(128)S(1)}, s32[16]{0:T(128)}, u32[]{:S(2)}) copy-start(s32[16]{0:T(128)} %constant.113.clone) | copy-start | bytes 196
  67.3 29.6 %all-to-all-start.4 = ((bf16[16,32,1792]{2,1,0:T(8,128)(2,1)}), bf16[16,32,1792]{2,1,0:T(8,128)(2,1)S(1)}, u32[]{:S(2)}, u32[]{:S(2)}) async-start(bf16[16,32,1792]{2,1,0:T(8,128)(2,1)} %pad_maximum_fusion), calls=%async_computation.4 | async-start | bytes 3670016 | tf_op jit(solution)/shard_map/all_to_all | solution.py:200
  75.7 1.1 copy-start.7
  100.2 27.9 %all-to-all-start.8 = ((f32[128,1,2]{2,1,0:T(1,128)}), f32[128,1,2]{2,1,0:T(1,128)S(1)}, u32[]{:S(2)}, u32[]{:S(2)}) async-start(f32[128,1,2]{2,1,0:T(1,128)} %broadcast_in_dim.19), calls=%async_computation.8 | async-start | bytes 131072 | tf_op jit(solution)/shard_map/all_to_all | solution.py:170
  119.5 4.5 %copy-start.4 = (bf16[16,32,1792]{2,1,0:T(8,128)(2,1)S(1)}, bf16[16,32,1792]{2,1,0:T(8,128)(2,1)}, u32[]{:S(2)}) copy-start(bf16[16,32,1792]{2,1,0:T(8,128)(2,1)} %get-tuple-element.23) | copy-start | bytes 5505028
  128.2 24.9 %all-to-all-start = ((bf16[4,160,1200]{2,1,0:T(8,128)(2,1)}), bf16[4,160,1200]{2,1,0:T(8,128)(2,1)S(1)}, u32[]{:S(2)}, u32[]{:S(2)}) async-start(bf16[4,160,1200]{2,1,0:T(8,128)(2,1)} %bitcast.8), calls=%async_computation | async-start | bytes 3276800 | tf_op jit(solution)/shard_map/all_to_all | solution.py:215
  133.8 29.6 %collective-permute-start.5 = (bf16[1712,256]{1,0:T(8,128)(2,1)}, bf16[1712,256]{1,0:T(8,128)(2,1)}, u32[]{:S(2)}, u32[]{:S(2)}) collective-permute-start(bf16[1712,256]{1,0:T(8,128)(2,1)} %pad_maximum_fusion.1), channel_id=1, source_target_pairs={{0,16},{16,0},{1,17},{17,1},{2,18},{18,2},{3,19},{19,3},{4,20},{20... | collective-permute-start | bytes 2629640 | tf_op jit(solution)/shard_map/ppermute | solution.py:244
  162.6 0.8 copy-start.5
  163.5 16.9 %copy-start.3 = (bf16[160,1200]{1,0:T(8,128)(2,1)S(1)}, bf16[160,1200]{1,0:T(8,128)(2,1)}, u32[]{:S(2)}) copy-start(bf16[160,1200]{1,0:T(8,128)(2,1)} %reduce_sum.86) | copy-start | bytes 1152004
  175.5 20.4 %all-to-all-start.5 = ((bf16[16,120,256]{2,1,0:T(8,128)(2,1)}), bf16[16,120,256]{2,1,0:T(8,128)(2,1)S(1)}, u32[]{:S(2)}, u32[]{:S(2)}) async-start(bf16[16,120,256]{2,1,0:T(8,128)(2,1)} %constant_dynamic-update-slice_fusion.16), calls=%async_computation.5 | async-start | bytes 1966080 | tf_op jit(solution)/shard_map/all_to_all | solution.py:247
  195.9 17.2 %all-to-all-start.1 = ((bf16[16,120,160]{1,2,0:T(8,128)(2,1)}), bf16[16,120,160]{1,2,0:T(8,128)(2,1)}, u32[]{:S(2)}, u32[]{:S(2)}) async-start(bf16[16,120,160]{1,2,0:T(8,128)(2,1)} %constant_dynamic-update-slice_fusion), calls=%async_computation.1 | async-start | bytes 1310720 | tf_op jit(solution)/shard_map/all_to_all | solution.py:219
  214.0 18.6 %all-to-all-start.6 = ((bf16[8,120,256]{2,1,0:T(8,128)(2,1)}), bf16[8,120,256]{2,1,0:T(8,128)(2,1)S(1)}, u32[]{:S(2)}, u32[]{:S(2)}) async-start(bf16[8,120,256]{2,1,0:T(8,128)(2,1)} %broadcast_in_dim.18), calls=%async_computation.6 | async-start | bytes 983040 | tf_op jit(solution)/shard_map/all_to_all | solution.py:170
  231.2 7.0 %copy-start.6 = (bf16[5,107,512]{2,1,0:T(8,128)(2,1)S(1)}, bf16[5,107,512]{2,1,0:T(8,128)(2,1)}, u32[]{:S(2)}) copy-start(bf16[5,107,512]{2,1,0:T(8,128)(2,1)} %constant.123) | copy-start | bytes 1643524
  233.4 12.9 %all-to-all-start.2 = ((bf16[8,120,160]{1,2,0:T(8,128)(2,1)}), bf16[8,120,160]{1,2,0:T(8,128)(2,1)S(1)}, u32[]{:S(2)}, u32[]{:S(2)}) async-start(bf16[8,120,160]{1,2,0:T(8,128)(2,1)} %broadcast_in_dim.16), calls=%async_computation.2 | async-start | bytes 655360 | tf_op jit(solution)/shard_map/all_to_all | solution.py:170
  246.3 17.4 %all-to-all-start.7 = ((bf16[16,107,107]{1,2,0:T(8,128)(2,1)}), bf16[16,107,107]{1,2,0:T(8,128)(2,1)S(1)}, u32[]{:S(2)}, u32[]{:S(2)}) async-start(bf16[16,107,107]{1,2,0:T(8,128)(2,1)} %concatenate.42), calls=%async_computation.7 | async-start | bytes 917504 | tf_op jit(solution)/shard_map/all_to_all | solution.py:266

commit v2 on v1

--- a/solution.py
+++ b/solution.py
@@ -18,6 +18,9 @@
 SUBJ = 256
 ROWS = 107
 WIN = 120
+TALL = 128
+PART = 150
+WIDE = 176
 LEAD = 384
 BLOCK = 256
 PHASES = 3
@@ -162,8 +165,194 @@
     )(own, near, jnp.asarray(depth_table()), jnp.asarray(plane_matrix()).astype(jnp.bfloat16), raw)
 
 
-def window_starts(length, count, window, total):
-    return [min(8 * (length * i // 8), total - window) for i in range(count)]
+NT = (((1,), (1,)), ((), ()))
+
+
+def row_start(first):
+    return min(first // 8 * 8, KX - WIN) if isinstance(first, int) else jnp.minimum(first // 8 * 8, KX - WIN)
+
+
+def part_start(part):
+    return jnp.minimum(part * PART // 16 * 16, K - WIDE)
+
+
+def vmem(count):
+    return [pl.BlockSpec(memory_space=pltpu.VMEM)] * count
+
+
+def smem():
+    return pl.BlockSpec(memory_space=pltpu.SMEM)
+
+
+def params(mib):
+    return pltpu.CompilerParams(vmem_limit_bytes=mib * 1024 * 1024)
+
+
+def gather_parts(x, which, sub_ref, left):
+    for k in range(4):
+        start = pl.multiple_of(part_start((x + k) % 4 * 2 + which), 16)
+        left[k * WIDE : (k + 1) * WIDE, :] = sub_ref[pl.ds(start, WIDE), :]
+
+
+def basis_other_kernel(at_ref, sub_ref, out_ref, left):
+    gather_parts(at_ref[0], 1 - at_ref[1], sub_ref, left)
+    out_ref[...] = lax.dot_general(left[...], sub_ref[...], NT, preferred_element_type=jnp.float32).astype(out_ref.dtype)
+
+
+def basis_own_kernel(at_ref, sub_ref, got_ref, *refs):
+    left = refs[-1]
+    gather_parts(at_ref[0], at_ref[1], sub_ref, left)
+    for k in range(4):
+        rows = slice(k * WIDE, (k + 1) * WIDE)
+        made = lax.dot_general(left[rows, :], sub_ref[...], NT, preferred_element_type=jnp.float32)
+        refs[k][...] = (made + got_ref[rows, :].astype(jnp.float32)).astype(refs[k].dtype)
+
+
+def basis_rows_kernel(a_ref, b_ref, c_ref, d_ref, out_ref, flat):
+    flat[...] = jnp.zeros_like(flat)
+    total = a_ref[...].astype(jnp.float32) + b_ref[...].astype(jnp.float32)
+    flat[:WIDE, :K] = total + c_ref[...].astype(jnp.float32) + d_ref[...].astype(jnp.float32)
+    turned = flat[...].T
+    for g in range(GRP):
+        first = row_start(g * ROWS)
+        if first + WIN <= turned.shape[0]:
+            out_ref[g] = turned[first : first + WIN, :WIDE].astype(out_ref.dtype)
+        else:
+            out_ref[g] = jnp.zeros((WIN, WIDE), out_ref.dtype)
+
+
+def columns_kernel(at_ref, got_ref, sub_ref, cen_ref, other_ref, own_ref, power_ref):
+    per_device = sub_ref.shape[1]
+    core = at_ref[1]
+    each = GRP // 2
+
+    def centre(i, sums):
+        cols = pl.ds(pl.multiple_of(i * RUN, RUN), RUN)
+        new = []
+        for s in range(2):
+            wide = got_ref[s * each : (s + 1) * each, :, cols].reshape(SUBJ, RUN).astype(jnp.float32)
+            mean = jnp.sum(wide, axis=0, keepdims=True) * (1.0 / SUBJ)
+            cen = (wide - mean).astype(cen_ref.dtype)
+            cen_ref[s, :, cols] = cen
+            back = cen.astype(jnp.float32)
+            new.append(sums[s] + jnp.sum((back * back).reshape(SUBJ // 8, 8, RUN), axis=0))
+        return tuple(new)
+
+    zero = jnp.zeros((8, RUN), jnp.float32)
+    sums = lax.fori_loop(0, per_device // RUN, centre, (zero, zero))
+    line = lax.broadcasted_iota(jnp.int32, (8, RUN), 0)
+    first = jnp.sum(sums[0], keepdims=True)
+    second = jnp.sum(sums[1], keepdims=True)
+    power_ref[...] = jnp.where(line == 0, first, jnp.where(line == 1, second, 0.0))
+
+    for which, out in ((1 - core, other_ref), (core, own_ref)):
+        right = cen_ref[which]
+        for lo in range(0, K, 400):
+            out[lo : lo + 400, :] = lax.dot_general(
+                sub_ref[lo : lo + 400, :], right, NT, preferred_element_type=jnp.float32
+            ).astype(out.dtype)
+        for s in range(2):
+            lo = K + s * SUBJ
+            out[lo : lo + SUBJ, :] = lax.dot_general(
+                cen_ref[s], right, NT, preferred_element_type=jnp.float32
+            ).astype(out.dtype)
+
+
+def write_power(power, out_ref, at):
+    high = power.astype(jnp.bfloat16)
+    low = (power - high.astype(jnp.float32)).astype(jnp.bfloat16)
+    out_ref[at, WIN:, :RUN] = high
+    out_ref[at, WIN:, RUN:] = low
+
+
+def windows_kernel(own_ref, got_ref, power_ref, out_ref, whole):
+    whole[...] = own_ref[...] + got_ref[...].astype(jnp.float32)
+    for g in range(GRP):
+        first = row_start(g * ROWS)
+        out_ref[g, :WIN, :] = whole[first : first + WIN, :].astype(out_ref.dtype)
+        write_power(power_ref[...], out_ref, g)
+
+
+def total_kernel(got_ref, out_ref):
+    total = got_ref[0].astype(jnp.float32)
+    for g in range(1, GRP):
+        total = total + got_ref[g].astype(jnp.float32)
+    power = total[WIN:, :RUN] + total[WIN:, RUN:]
+    rows = total[:WIN].astype(out_ref.dtype)
+    for p in range(8):
+        out_ref[p, :WIN, :] = rows
+        write_power(power, out_ref, p)
+
+
+def finish_kernel(count, at_ref, got_ref, rows_ref, scale_ref, turned_ref):
+    halves = []
+    power = jnp.zeros((8, RUN), jnp.float32)
+    for c in range(2):
+        total = got_ref[c].astype(jnp.float32)
+        for x in range(1, 4):
+            total = total + got_ref[2 * x + c].astype(jnp.float32)
+        power = power + total[WIN:, :RUN] + total[WIN:, RUN:]
+        halves.append(total)
+    scale_ref[...] = lax.rsqrt(power / count + epsilon)
+    first = at_ref[2] * ROWS
+    shift = (TALL - (first - row_start(first))) % TALL
+    rows = pltpu.roll(jnp.concatenate(halves, axis=1), shift, 0)
+    rows_ref[...] = rows
+    narrow = rows.astype(jnp.bfloat16)
+    turned_ref[: K // ROWS] = jnp.zeros((K // ROWS, TALL, TALL), turned_ref.dtype)
+    line = lax.broadcasted_iota(jnp.int32, (TALL, 2 * SUBJ), 0)
+    lane = lax.broadcasted_iota(jnp.int32, (TALL, 2 * SUBJ), 1)
+    for g in range(K // ROWS, GRP):
+        pick = jnp.where(line + (g * ROWS - K) == lane, 1.0, 0.0).astype(jnp.bfloat16)
+        turned_ref[g] = lax.dot_general(pick, narrow, NT, preferred_element_type=jnp.float32).astype(turned_ref.dtype)
+
+
+def assemble_kernel(masked, at_ref, back_ref, rows_ref, scale_ref, *refs):
+    out_ref, basis, cross = refs[-3:]
+    x, core, grp = at_ref[0], at_ref[1], at_ref[2]
+    first = grp * ROWS
+    basis[...] = jnp.zeros_like(basis)
+    cross[...] = jnp.zeros_like(cross)
+    line = lax.broadcasted_iota(jnp.int32, (WIDE, 384), 0)
+    lane = lax.broadcasted_iota(jnp.int32, (WIDE, 384), 1)
+    for k in range(4):
+        for c in range(2):
+            part = (x - k + 4) % 4 * 2 + (core if c == 0 else 1 - core)
+            begin = part * PART // RUN * RUN
+            cell = line + (part_start(part) - begin)
+            ok = (cell == lane) & (cell >= part * PART - begin) & (cell < part * PART - begin + PART)
+            put = jnp.where(ok, 1.0, 0.0).astype(jnp.bfloat16)
+            cols = pl.ds(pl.multiple_of(begin, RUN), 384)
+            basis[:WIN, cols] += jnp.dot(refs[k][c], put, preferred_element_type=jnp.float32)
+    line = lax.broadcasted_iota(jnp.int32, (TALL, 256), 0)
+    lane = lax.broadcasted_iota(jnp.int32, (TALL, 256), 1)
+    for g in range(K // ROWS + 1):
+        begin = g * ROWS // RUN * RUN
+        ok = (line + (g * ROWS - begin) == lane) & (line < ROWS) & (line + g * ROWS < K)
+        put = jnp.where(ok, 1.0, 0.0).astype(jnp.bfloat16)
+        cross[:, begin : begin + 256] += jnp.dot(back_ref[g], put, preferred_element_type=jnp.float32)
+    shift = (TALL - (first - row_start(first))) % TALL
+    width = 1792
+    row = first + lax.broadcasted_iota(jnp.int32, (TALL, 1), 0)
+    left = jnp.where(row < K, pltpu.roll(basis[...], shift, 0), cross[...])
+    base = K // RUN * RUN
+    right = pltpu.roll(
+        jnp.concatenate([rows_ref[...], jnp.zeros((TALL, RUN), jnp.float32)], axis=1), K - base, 1
+    )
+    zero, one = scale_ref[0:1, 0:1], scale_ref[1:2, 0:1]
+    of_row = jnp.where(row < K, 1.0, jnp.where(row < K + SUBJ, zero, one))
+    col = lax.broadcasted_iota(jnp.int32, (1, width), 1)
+    of_col = jnp.where(col < K, 1.0, jnp.where(col < K + SUBJ, zero, one))
+    out_ref[:, :base] = (left[:, :base] * (of_row * of_col[:, :base]) / masked)[:ROWS]
+    edge = jnp.concatenate([left[:, base:], jnp.zeros((TALL, width - left.shape[1]), jnp.float32)], axis=1)
+    values = jnp.where(col[:, base:] < K, edge, right)
+    out_ref[:, base:] = (values * (of_row * of_col[:, base:]) / masked)[:ROWS, : KX - base]
+
+
+def rotate_kernel(scale_ref, base_ref, turn_ref, cen_ref, out_ref):
+    first = jnp.dot(turn_ref[:, :SUBJ], cen_ref[0], preferred_element_type=jnp.float32)
+    second = jnp.dot(turn_ref[:, SUBJ:], cen_ref[1], preferred_element_type=jnp.float32)
+    out_ref[...] = (base_ref[...] + scale_ref[0:1, 0:1] * first + scale_ref[1:2, 0:1] * second).astype(out_ref.dtype)
 
 
 def copies(value, axis, count):
@@ -176,13 +365,14 @@
     per_device = subspace.shape[1]
     slab = ("x", "core")
     masked = per_device * 8 * GRP
-    slab_at = lax.axis_index("x") * 2 + lax.axis_index("core")
-    core = lax.axis_index("core")
-    grp = lax.axis_index("grp")
     bf16 = jnp.bfloat16
     f32 = jnp.float32
+    like = jax.ShapeDtypeStruct
     swap = [(0, 1), (1, 0)]
-
+    turns = [[(i, (i + k) % 4) for i in range(4)] for k in range(4)]
+    at = jnp.stack([lax.axis_index("x"), lax.axis_index("core"), lax.axis_index("grp")]).astype(jnp.int32)
+
+    slab_at = lax.axis_index("x") * 2 + lax.axis_index("core")
     tiles = mask_index.reshape(-1, RUN)[:, 0] // RUN - slab_at * (depth * extent // RUN)
     up = [(i, i + 1) for i in range(7)]
     down = [(i + 1, i) for i in range(7)]
@@ -197,86 +387,112 @@
     quarter = GRP // 4
     low = (rim[:quarter] + from_low).astype(bf16)
     high = (rim[quarter:] + from_high).astype(bf16)
-    regrouped = lax.all_to_all(jnp.concatenate([low, mid, high]), "grp", 0, 0, tiled=True)
-
-    across = (((1,), (1,)), ((), ()))
-    col_starts = window_starts(150, 8, 160, K)
-    starts = jnp.array(col_starts, jnp.int32)
-
-    def some_rows(which):
-        return jnp.concatenate(
-            [lax.dynamic_slice_in_dim(subspace, starts[2 * x + which], 160, 0) for x in range(4)]
-        )
-
-    other_ss = lax.dot_general(some_rows(1 - core), subspace, across, preferred_element_type=f32).astype(bf16)
+    placed = jnp.concatenate([low, mid, high])
+    regrouped = lax.all_to_all(placed, "grp", 0, 0, tiled=True)
+
+    at_ss, _ = lax.optimization_barrier((at, to_down))
+    left = pltpu.VMEM((4 * WIDE, per_device), bf16)
+    other_ss = pl.pallas_call(
+        basis_other_kernel,
+        out_shape=like((4 * WIDE, K), bf16),
+        in_specs=[smem(), *vmem(1)],
+        out_specs=vmem(1)[0],
+        scratch_shapes=[left],
+        compiler_params=params(24),
+        name="basis_other",
+    )(at_ss, subspace)
     got_ss = lax.ppermute(other_ss, "core", swap)
-    own_ss = lax.dot_general(some_rows(core), subspace, across, preferred_element_type=f32)
-    pair_ss = (own_ss + got_ss.astype(f32)).astype(bf16).reshape(4, 160, K)
-    slab_ss = jnp.sum(lax.all_to_all(pair_ss, "x", 0, 0, tiled=True).astype(f32), axis=0)
-    row_starts = window_starts(ROWS, GRP, WIN, KX + 0)
-    tall = jnp.pad(slab_ss.astype(bf16).T, ((0, KX - K), (0, 0)))
-    by_row = jnp.stack([tall[a : a + WIN] for a in row_starts])
+    parts = pl.pallas_call(
+        basis_own_kernel,
+        out_shape=[like((WIDE, K), bf16)] * 4,
+        in_specs=[smem(), *vmem(2)],
+        out_specs=vmem(4),
+        scratch_shapes=[left],
+        compiler_params=params(24),
+        name="basis_own",
+    )(at_ss, subspace, got_ss)
+    parts = [parts[0]] + [lax.ppermute(parts[k], "x", turns[k]) for k in range(1, 4)]
+    by_row = pl.pallas_call(
+        basis_rows_kernel,
+        out_shape=like((GRP, WIN, WIDE), bf16),
+        in_specs=vmem(4),
+        out_specs=vmem(1)[0],
+        scratch_shapes=[pltpu.VMEM((256, 1408), f32)],
+        compiler_params=params(16),
+        name="basis_rows",
+    )(*parts)
     grp_ss = jnp.sum(lax.all_to_all(by_row, "grp", 0, 0, tiled=True).astype(f32), axis=0).astype(bf16)
-    all_ss = copies(grp_ss, slab, 8)
-    rows_ss = jnp.concatenate(
-        [all_ss[p][:, 150 * p - col_starts[p] : 150 * p - col_starts[p] + 150] for p in range(8)], axis=1
+    pair_ss = jnp.stack([grp_ss, lax.ppermute(grp_ss, "core", swap)])
+    all_ss = [pair_ss] + [lax.ppermute(pair_ss, "x", turns[k]) for k in range(1, 4)]
+
+    rotation_b, _ = lax.optimization_barrier((rotation, placed))
+    contract = (((0,), (0,)), ((), ()))
+    from_basis = lax.optimization_barrier(
+        lax.dot_general(rotation_b[:K], subspace, contract, preferred_element_type=f32)
     )
-
-    contract = (((0,), (0,)), ((), ()))
-    from_basis = lax.dot_general(rotation[:K], subspace, contract, preferred_element_type=f32)
-
-    halves = regrouped.astype(f32).reshape(2, SUBJ, per_device)
-    centered = (halves - jnp.mean(halves, axis=1, keepdims=True)).astype(bf16)
-    wide = centered.astype(f32)
-    partial_power = jnp.sum(wide * wide, axis=(1, 2))
-    power = jnp.sum(copies(partial_power[None], ("x", "core", "grp"), 8 * GRP), axis=(0, 1))
-    scales = lax.rsqrt(power / (masked * SUBJ) + epsilon)
-
-    def data_columns(which):
-        mine = lax.dynamic_index_in_dim(centered, which, 0, keepdims=False)
-        return jnp.concatenate(
-            [
-                lax.dot_general(subspace, mine, across, preferred_element_type=f32),
-                lax.dot_general(centered.reshape(2 * SUBJ, per_device), mine, across, preferred_element_type=f32),
-            ]
-        )
-
-    got_c = lax.ppermute(data_columns(1 - core).astype(bf16), "core", swap)
-    pair_c = (data_columns(core) + got_c.astype(f32)).astype(bf16)
-    by_row_c = jnp.stack([pair_c[a : a + WIN] for a in row_starts])
-    grp_c = jnp.sum(lax.all_to_all(by_row_c, "grp", 0, 0, tiled=True).astype(f32), axis=0).astype(bf16)
-    all_c = copies(grp_c, slab, 8).astype(f32).reshape(4, 2, WIN, SUBJ)
-    sum_c = jnp.sum(all_c, axis=0)
-    first_row = grp * ROWS
-    offset = first_row - jnp.array(row_starts, jnp.int32)[grp]
-    rows_c = lax.dynamic_slice_in_dim(jnp.concatenate([sum_c[0], sum_c[1]], axis=1), offset, ROWS, 0)
-
-    first_data = K // ROWS
-    data_devices = GRP - first_data
-    wanted = np.zeros((data_devices, ROWS, 2 * SUBJ), np.float32)
-    for d in range(data_devices):
-        for i in range(ROWS):
-            at = (first_data + d) * ROWS + i - K
-            if at >= 0:
-                wanted[d, i, at] = 1.0
-    turned = lax.dot_general(
-        jnp.asarray(wanted).astype(bf16), rows_c.astype(bf16), (((2,), (1,)), ((), ())), preferred_element_type=f32
-    ).astype(bf16)
-    turned = jnp.concatenate([jnp.zeros((first_data, ROWS, ROWS), bf16), turned])
+    turn = lax.optimization_barrier(rotation_b[K:].T)
+
+    centered, other_c, own_c, power = pl.pallas_call(
+        columns_kernel,
+        out_shape=[like((2, SUBJ, per_device), bf16), like((KX, SUBJ), bf16), like((KX, SUBJ), f32), like((8, RUN), f32)],
+        in_specs=[smem(), *vmem(2)],
+        out_specs=vmem(4),
+        compiler_params=params(24),
+        name="columns",
+    )(at, regrouped, subspace)
+    got_c = lax.ppermute(other_c, "core", swap)
+    by_row_c = pl.pallas_call(
+        windows_kernel,
+        out_shape=like((GRP, TALL, SUBJ), bf16),
+        in_specs=vmem(3),
+        out_specs=vmem(1)[0],
+        scratch_shapes=[pltpu.VMEM((KX, SUBJ), f32)],
+        compiler_params=params(16),
+        name="windows",
+    )(own_c, got_c, power)
+    sum_c = pl.pallas_call(
+        total_kernel,
+        out_shape=like((8, TALL, SUBJ), bf16),
+        in_specs=vmem(1),
+        out_specs=vmem(1)[0],
+        compiler_params=params(16),
+        name="total",
+    )(lax.all_to_all(by_row_c, "grp", 0, 0, tiled=True))
+    rows_c, scales, turned = pl.pallas_call(
+        functools.partial(finish_kernel, float(masked * SUBJ)),
+        out_shape=[like((TALL, 2 * SUBJ), f32), like((8, RUN), f32), like((GRP, TALL, TALL), bf16)],
+        in_specs=[smem(), *vmem(1)],
+        out_specs=vmem(3),
+        compiler_params=params(16),
+        name="finish",
+    )(at, lax.all_to_all(sum_c, slab, 0, 0, tiled=True))
+
     back = lax.all_to_all(turned, "grp", 0, 0, tiled=True)
-    rows_t = jnp.transpose(back[: first_data + 1], (1, 0, 2)).reshape(ROWS, (first_data + 1) * ROWS)[:, :K]
-    rows_ss = lax.dynamic_slice_in_dim(rows_ss, offset, ROWS, 0)
-    row_number = first_row + lax.broadcasted_iota(jnp.int32, (ROWS, 1), 0)
-    left = jnp.where(row_number < K, rows_ss.astype(f32), rows_t.astype(f32))
-    owned = jnp.concatenate([left, rows_c], axis=1)
-
-    row_scale = jnp.concatenate([jnp.ones((K,), f32), jnp.repeat(scales, SUBJ)])
-    owned_scale = lax.dynamic_slice_in_dim(row_scale, first_row, ROWS, 0)
-    gram_rows = owned * (owned_scale[:, None] * row_scale[None, :]) / masked
-
-    from_first = lax.dot_general(rotation[K : K + SUBJ], centered[0], contract, preferred_element_type=f32)
-    from_second = lax.dot_general(rotation[K + SUBJ :], centered[1], contract, preferred_element_type=f32)
-    new_subspace = (from_basis + scales[0] * from_first + scales[1] * from_second).astype(bf16)
+    gram_rows = pl.pallas_call(
+        functools.partial(assemble_kernel, float(masked)),
+        out_shape=like((ROWS, KX), f32),
+        in_specs=[smem(), *vmem(7)],
+        out_specs=vmem(1)[0],
+        scratch_shapes=[pltpu.VMEM((TALL, 1408), f32), pltpu.VMEM((TALL, 1408), f32)],
+        compiler_params=params(16),
+        name="assemble",
+    )(at, back, rows_c, scales, *all_ss)
+
+    tile = 256
+    new_subspace = pl.pallas_call(
+        rotate_kernel,
+        out_shape=like((K, per_device), bf16),
+        grid=(per_device // tile,),
+        in_specs=[
+            pl.BlockSpec((8, RUN), lambda i: (0, 0)),
+            pl.BlockSpec((K, tile), lambda i: (0, i)),
+            pl.BlockSpec((K, 2 * SUBJ), lambda i: (0, 0)),
+            pl.BlockSpec((2, SUBJ, tile), lambda i: (0, 0, i)),
+        ],
+        out_specs=pl.BlockSpec((K, tile), lambda i: (0, i)),
+        compiler_params=params(24),
+        name="rotate",
+    )(scales, from_basis, turn, centered)
     return (gram_rows, new_subspace)
 
 

time: 267 us -> 190 us (0.71)
  matrix products: 51.9 us -> 10.7 us
  Pallas kernels: 17.6 us -> 52 us
  local copies, waits for them, and re-layouts: 42 us -> 19.1 us
  waiting for transfers between devices: 51.7 us -> 31.3 us
  starting transfers between devices: 73.4 us -> 55.7 us
  between operations: 16.6 us -> 0.86 us
  blocking collectives: 0 us -> 15.6 us
  other arithmetic: 12.3 us -> 3.56 us
    dot_general x10 -> x1, matrix products: 51.9 us -> 10.7 us  [body(): lax.dot_general(rotation_b[:K], subspace, contract, preferred_element_typ...]
    all_to_all x7 -> x3, starting transfers between devices: 50.6 us -> 13.8 us  [the longest x1 6.43 us: body(): lax.all_to_all(sum_c, slab, 0, 0, tiled=True)]
    pallas_call x0 -> x9, Pallas kernels: none -> 33.4 us  [the longest x1 7.56 us: body(): pl.pallas_call(basis_own_kernel, out_shape=[like((WIDE, K), bf16)] * 4, i...]
    all_to_all x7 -> x3, waiting for transfers between devices: 42.6 us -> 18.6 us  [the longest x1 15.6 us: body(): lax.all_to_all(by_row_c, 'grp', 0, 0, tiled=True)]
    ppermute x1 -> x8, starting transfers between devices: 0.01 us -> 19.9 us  [the longest x3 9.49 us: body(): lax.ppermute(parts[k], 'x', turns[k])]
    all_to_all x0 -> x1, blocking collectives: none -> 15.6 us  [copies(): lax.all_to_all(jnp.broadcast_to(value[None], (count, *value.shape)), axis...]
    unnamed x51 -> x20, local copies, waits for them, and re-layouts: 27.2 us -> 14.6 us
    all_to_all x1, waiting for transfers between devices: 0.01 us -> 11.6 us  [body(): lax.all_to_all(by_row, 'grp', 0, 0, tiled=True).astype(f32)]
  transfers between devices with their start and end apart: 15 -> 18, of which waited for: 7 -> 5; matrix products, arithmetic and copies ran while one was open for 31% -> 9% of each run, Pallas kernels for 0% -> 16%
where the time goes in v2:
time: 190 us; the launch traced here: 189 us
  starting transfers between devices  55.7 us (29%)
  Pallas kernels  52 us (27%)
  waiting for transfers between devices  31.3 us (16%)
  local copies, waits for them, and re-layouts  19.1 us (10%)
  blocking collectives  15.6 us (8%)
  matrix products  10.7 us (6%)
  other arithmetic  3.56 us (2%)
    pallas_call x1, Pallas kernels, smooth(): pl.pallas_call(functools.partial(smooth_kernel, depth), out_shape=[jax.Sh...  18.6 us
    all_to_all x1, waiting for transfers between devices, body(): lax.all_to_all(by_row_c, 'grp', 0, 0, tiled=True)  15.6 us
    all_to_all x1, blocking collectives, copies(): lax.all_to_all(jnp.broadcast_to(value[None], (count, *value.shape)), axis...  15.6 us
    unnamed x20, local copies, waits for them, and re-layouts  14.6 us
    all_to_all x1, waiting for transfers between devices, body(): lax.all_to_all(by_row, 'grp', 0, 0, tiled=True).astype(f32)  11.6 us
    dot_general x1, matrix products, body(): lax.dot_general(rotation_b[:K], subspace, contract, preferred_element_typ...  10.7 us
    ppermute x3, starting transfers between devices, body(): lax.ppermute(parts[k], 'x', turns[k])  9.49 us
    pallas_call x1, Pallas kernels, body(): pl.pallas_call(basis_own_kernel, out_shape=[like((WIDE, K), bf16)] * 4, i...  7.56 us
  transfers between devices with their start and end apart: 18, of which 5 were waited for; matrix products, arithmetic and copies ran while one was open for 9% of the time, Pallas kernels for 16%

profile of v2, /device:TPU:0, one launch (start us, length us, event | category | flops | bytes accessed | tf_op | source)
XLA Modules:
  0.0 188.7 jit_solution(2348873684962994466)
XLA Ops:
  0.6 0.8 slice_reduce_fusion.1
  1.5 1.3 collective-permute-start.1
  2.8 3.0 %collective-permute-start = (s32[14]{0:T(128)S(1)}, s32[14]{0:T(128)S(1)}, u32[]{:S(2)}, u32[]{:S(2)}) collective-permute-start(s32[14]{0:T(128)S(1)} %fusion.2), channel_id=1, source_target_pairs={{0,16},{16,32},{32,48},{48,64},{64,80},{80,96},{96,112},{1,17},{17... | collective-permute-start | bytes 176 | tf_op jit(solution)/shard_map/ppermute | solution.py:379
  5.8 0.8 collective-permute-done
  6.6 15.6 %all_to_all.30 = s32[16,3,14]{2,1,0:T(4,128)S(1)} all-to-all(s32[16,3,14]{2,1,0:T(4,128)S(1)} %broadcast_in_dim.2), channel_id=1, replica_groups=mesh['x'=4,'core'=2,'grp'=16] {'grp'}, dimensions={0} | all-to-all | bytes 5376 | tf_op jit(solution)/shard_map/all_to_all | solution.py:359
  22.6 1.4 copy-done.8
  24.0 0.7 copy-done.9
  24.7 18.6 %smooth.1 = (bf16[8,32,1792]{2,1,0:T(8,128)(2,1)S(1)}, f32[8,32,1792]{2,1,0:T(8,128)S(1)}, f32[4,32,1792]{2,1,0:T(8,128)}, f32[4,32,1792]{2,1,0:T(8,128)}) custom-call(s32[224]{0:T(256)S(1)} %reshape_squeeze.9.own_ref, s32[112]{0:T(128)S(1)} %pad_add_fusion.2.near_ref, f32[64]{0:T(128)S(1)} %copy-done.9, bf16[3,1024,256]{2,1,0:T(8,128)(2,1)S(1)} %copy-done.8, ...), custom_call_target="tpu_custom_call" | custom-call | tf_op jit(solution)/shard_map/smooth/pallas_call | solution.py:148
  43.3 2.6 %collective-permute-start.2 = (f32[4,32,1792]{2,1,0:T(8,128)}, f32[4,32,1792]{2,1,0:T(8,128)}, u32[]{:S(2)}, u32[]{:S(2)}) collective-permute-start(f32[4,32,1792]{2,1,0:T(8,128)} %get-tuple-element.20), channel_id=1, source_target_pairs={{0,16},{16,32},{32,48},{48,64},{64,80},{80,96},{96,112},{1,17},{17... | collective-permute-start | bytes 2752520 | tf_op jit(solution)/shard_map/ppermute | solution.py:385
  45.8 1.3 collective-permute-start.3
  47.2 2.2 %copy-done = bf16[1200,1792]{1,0:T(8,128)(2,1)S(1)} copy-done((bf16[1200,1792]{1,0:T(8,128)(2,1)S(1)}, bf16[1200,1792]{1,0:T(8,128)(2,1)}, u32[]{:S(2)}) %copy-start) | copy-done | bytes 4300824
  49.4 5.2 %basis_other.1 = bf16[704,1200]{1,0:T(8,128)(2,1)} custom-call(s32[3]{0:T(128)S(1)} %pad_add_fusion.1.at_ref, bf16[1200,1792]{1,0:T(8,128)(2,1)S(1)} %copy-done), custom_call_target="tpu_custom_call" | custom-call | tf_op jit(solution)/shard_map/basis_other/pallas_call | solution.py:395
  54.6 3.3 %collective-permute-start.5 = (bf16[704,1200]{1,0:T(8,128)(2,1)}, bf16[704,1200]{1,0:T(8,128)(2,1)}, u32[]{:S(2)}, u32[]{:S(2)}) collective-permute-start(bf16[704,1200]{1,0:T(8,128)(2,1)} %basis_other.1), channel_id=1, source_target_pairs={{0,16},{16,0},{1,17},{17,1},{2,18},{18,2},{3,19},{19,3},{4,20},{20... | collective-permute-start | bytes 5068808 | tf_op jit(solution)/shard_map/ppermute | solution.py:404
  57.9 1.8 add_convert_fusion.1
  59.7 1.4 pad_maximum_fusion
  61.1 3.7 %all-to-all-start.1 = ((bf16[16,32,1792]{2,1,0:T(8,128)(2,1)}), bf16[16,32,1792]{2,1,0:T(8,128)(2,1)S(1)}, u32[]{:S(2)}, u32[]{:S(2)}) async-start(bf16[16,32,1792]{2,1,0:T(8,128)(2,1)} %pad_maximum_fusion), calls=%async_computation.1 | async-start | bytes 3670016 | tf_op jit(solution)/shard_map/all_to_all | solution.py:391
  64.9 2.2 %copy-done.1 = bf16[1200,1792]{1,0:T(8,128)(2,1)S(1)} copy-done((bf16[1200,1792]{1,0:T(8,128)(2,1)S(1)}, bf16[1200,1792]{1,0:T(8,128)(2,1)}, u32[]{:S(2)}) %copy-start.1) | copy-done | bytes 4300824
  67.1 7.6 %basis_own.1 = (bf16[176,1200]{1,0:T(8,128)(2,1)S(1)}, bf16[176,1200]{1,0:T(8,128)(2,1)}, bf16[176,1200]{1,0:T(8,128)(2,1)}, bf16[176,1200]{1,0:T(8,128)(2,1)}) custom-call(s32[3]{0:T(128)S(1)} %pad_add_fusion.1.at_ref, bf16[1200,1792]{1,0:T(8,128)(2,1)S(1)} %copy-done.1, bf16[704,1200]{1,0:T(8,128)(2,1)} %collective-permute-done.5.got_ref), custom_call_target="tpu_custom_call" | custom-call | tf_op jit(solution)/shard_map/basis_own/pallas_call | solution.py:405
  74.6 5.3 %collective-permute-start.6 = (bf16[176,1200]{1,0:T(8,128)(2,1)}, bf16[176,1200]{1,0:T(8,128)(2,1)S(1)}, u32[]{:S(2)}, u32[]{:S(2)}) collective-permute-start(bf16[176,1200]{1,0:T(8,128)(2,1)} %get-tuple-element.31), channel_id=1, source_target_pairs={{0,32},{32,64},{64,96},{96,0},{1,33},{33,65},{65,97},{97,1},{2,34}... | collective-permute-start | bytes 1267208 | tf_op jit(solution)/shard_map/ppermute | solution.py:414
  80.0 3.0 %collective-permute-start.7 = (bf16[176,1200]{1,0:T(8,128)(2,1)}, bf16[176,1200]{1,0:T(8,128)(2,1)S(1)}, u32[]{:S(2)}, u32[]{:S(2)}) collective-permute-start(bf16[176,1200]{1,0:T(8,128)(2,1)} %get-tuple-element.32), channel_id=1, source_target_pairs={{0,64},{32,96},{64,0},{96,32},{1,65},{33,97},{65,1},{97,33},{2,66}... | collective-permute-start | bytes 1267208 | tf_op jit(solution)/shard_map/ppermute | solution.py:414
  82.9 1.2 collective-permute-start.8
  84.1 3.0 %all-to-all-done.1.got_ref = bf16[16,32,1792]{2,1,0:T(8,128)(2,1)S(1)} async-done(((bf16[16,32,1792]{2,1,0:T(8,128)(2,1)}), bf16[16,32,1792]{2,1,0:T(8,128)(2,1)S(1)}, u32[]{:S(2)}, u32[]{:S(2)}) %all-to-all-start.1) | async-done | bytes 1835040 | tf_op jit(solution)/shard_map/all_to_all | solution.py:391
  87.1 2.2 %copy-done.2 = bf16[1200,1792]{1,0:T(8,128)(2,1)S(1)} copy-done((bf16[1200,1792]{1,0:T(8,128)(2,1)S(1)}, bf16[1200,1792]{1,0:T(8,128)(2,1)}, u32[]{:S(2)}) %copy-start.2) | copy-done | bytes 4300824
  89.3 6.2 %columns.1 = (bf16[2,256,1792]{2,1,0:T(8,128)(2,1)S(1)}, bf16[1712,256]{1,0:T(8,128)(2,1)}, f32[1712,256]{1,0:T(8,128)S(1)}, f32[8,128]{1,0:T(8,128)S(1)}) custom-call(s32[3]{0:T(128)S(1)} %pad_add_fusion.1.at_ref, bf16[16,32,1792]{2,1,0:T(8,128)(2,1)S(1)} %all-to-all-done.1.got_ref, bf16[1200,1792]{1,0:T(8,128)(2,1)S(1)} %copy-done.2), custom_call_target="tpu_custom_call" | custom-call | tf_op jit(solution)/shard_map/columns/pallas_call | solution.py:435
  95.5 1.2 copy-done.4
  96.8 1.2 copy-done.6
  98.0 5.3 %collective-permute-start.4 = (bf16[1712,256]{1,0:T(8,128)(2,1)}, bf16[1712,256]{1,0:T(8,128)(2,1)}, u32[]{:S(2)}, u32[]{:S(2)}) collective-permute-start(bf16[1712,256]{1,0:T(8,128)(2,1)} %get-tuple-element.24), channel_id=1, source_target_pairs={{0,16},{16,0},{1,17},{17,1},{2,18},{18,2},{3,19},{19,3},{4,20},{20... | collective-permute-start | bytes 2629640 | tf_op jit(solution)/shard_map/ppermute | solution.py:443
  103.3 0.3 collective-permute-done.7.c_ref
  103.6 1.4 basis_rows.1
  105.0 1.2 copy.9
  106.3 6.9 %all-to-all-start.5 = ((bf16[16,120,176]{1,2,0:T(8,128)(2,1)}), bf16[16,120,176]{1,2,0:T(8,128)(2,1)S(1)}, u32[]{:S(2)}, u32[]{:S(2)}) async-start(bf16[16,120,176]{1,2,0:T(8,128)(2,1)} %copy.9), calls=%async_computation.5 | async-start | bytes 1441792 | tf_op jit(solution)/shard_map/all_to_all | solution.py:424
  113.2 2.3 %windows.1 = bf16[16,128,256]{2,1,0:T(8,128)(2,1)} custom-call(f32[1712,256]{1,0:T(8,128)S(1)} %copy-done.7, bf16[1712,256]{1,0:T(8,128)(2,1)} %collective-permute-done.4.got_ref, f32[8,128]{1,0:T(8,128)S(1)} %get-tuple-element.25.power_ref), custom_call_target="tpu_custom_call" | custom-call | tf_op jit(solution)/shard_map/windows/pallas_call | solution.py:444
  115.5 11.6 %all-to-all-done.5 = bf16[16,120,176]{1,2,0:T(8,128)(2,1)S(1)} async-done(((bf16[16,120,176]{1,2,0:T(8,128)(2,1)}), bf16[16,120,176]{1,2,0:T(8,128)(2,1)S(1)}, u32[]{:S(2)}, u32[]{:S(2)}) %all-to-all-start.5) | async-done | bytes 675872 | tf_op jit(solution)/shard_map/all_to_all | solution.py:424
  127.1 3.7 %all-to-all-start.2 = ((bf16[16,128,256]{2,1,0:T(8,128)(2,1)}), bf16[16,128,256]{2,1,0:T(8,128)(2,1)S(1)}, u32[]{:S(2)}, u32[]{:S(2)}) async-start(bf16[16,128,256]{2,1,0:T(8,128)(2,1)} %windows.1), calls=%async_computation.2 | async-start | bytes 2097152 | tf_op jit(solution)/shard_map/all_to_all | solution.py:460
  130.8 0.2 reduce_sum.12
  131.1 15.6 %all-to-all-done.2.got_ref = bf16[16,128,256]{2,1,0:T(8,128)(2,1)S(1)} async-done(((bf16[16,128,256]{2,1,0:T(8,128)(2,1)}), bf16[16,128,256]{2,1,0:T(8,128)(2,1)S(1)}, u32[]{:S(2)}, u32[]{:S(2)}) %all-to-all-start.2) | async-done | bytes 1048608 | tf_op jit(solution)/shard_map/all_to_all | solution.py:460
  146.7 0.9 total.1
  147.7 6.4 %all-to-all-start.3 = ((bf16[8,128,256]{2,1,0:T(8,128)(2,1)}), bf16[8,128,256]{2,1,0:T(8,128)(2,1)S(1)}, u32[]{:S(2)}, u32[]{:S(2)}) async-start(bf16[8,128,256]{2,1,0:T(8,128)(2,1)} %total.1), calls=%async_computation.3 | async-start | bytes 1048576 | tf_op jit(solution)/shard_map/all_to_all | solution.py:468
  154.1 10.7 %fusion.base_ref = f32[1200,1792]{1,0:T(8,128)} fusion(bf16[1200,1792]{1,0:T(8,128)(2,1)} %sub_ref.5, bf16[1712,1200]{0,1:T(8,128)(2,1)} %param.9), kind=kOutput, calls=%fused_computation | convolution fusion | flops 5160960000 | bytes 15974400 | tf_op jit(solution)/shard_map/dot_general | solution.py:431
  164.8 3.3 %collective-permute-start.12 = (bf16[2,120,176]{2,1,0:T(8,128)(2,1)S(1)}, bf16[2,120,176]{2,1,0:T(8,128)(2,1)S(1)}, u32[]{:S(2)}, u32[]{:S(2)}) collective-permute-start(bf16[2,120,176]{2,1,0:T(8,128)(2,1)S(1)} %pad_maximum_fusion.1.refs_0_), channel_id=1, source_target_pairs={{0,96},{32,0},{64,32},{96,64},{1,97},{33,1},{65,33},{97,65},{2,98}... | collective-permute-start | bytes 253448 | tf_op jit(solution)/shard_map/ppermute | solution.py:426
  168.1 0.9 collective-permute-start.11
  168.9 0.9 collective-permute-start.10
  169.8 1.8 finish.1
  171.6 3.7 %all-to-all-start.4 = ((bf16[16,128,128]{2,1,0:T(8,128)(2,1)}), bf16[16,128,128]{2,1,0:T(8,128)(2,1)S(1)}, u32[]{:S(2)}, u32[]{:S(2)}) async-start(bf16[16,128,128]{2,1,0:T(8,128)(2,1)} %get-tuple-element.26), calls=%async_computation.4 | async-start | bytes 1048576 | tf_op jit(solution)/shard_map/all_to_all | solution.py:470
  175.3 2.0 %slice_bitcast_fusion.turn_ref = bf16[1200,512]{1,0:T(8,128)(2,1)S(1)} fusion(bf16[1712,1200]{0,1:T(8,128)(2,1)} %param.9), kind=kLoop, calls=%fused_computation.3 | loop fusion | bytes 2457600 | tf_op jit(solution)/shard_map/transpose | solution.py:433
  177.3 3.4 %copy-done.3 = f32[1200,1792]{1,0:T(8,128)S(1)} copy-done((f32[1200,1792]{1,0:T(8,128)S(1)}, f32[1200,1792]{1,0:T(8,128)}, u32[]{:S(2)}) %copy-start.3) | copy-done | bytes 8601624
  180.7 5.7 %rotate.1 = bf16[1200,1792]{1,0:T(8,128)(2,1)} custom-call(f32[8,128]{1,0:T(8,128)S(1)} %get-tuple-element.28.scale_ref, f32[1200,1792]{1,0:T(8,128)S(1)} %copy-done.3, bf16[1200,512]{1,0:T(8,128)(2,1)S(1)} %slice_bitcast_fusion.turn_ref, bf16[2,256,1792]{2,1,0:T(8,128)(2,1)S(1)} %copy-done.5), custom_call_target="tpu_custom_call" | custom-call | tf_op jit(solution)/shard_map/rotate/pallas_call | solution.py:482
  186.5 2.2 %assemble.1 = f32[107,1712]{1,0:T(8,128)} custom-call(s32[3]{0:T(128)S(1)} %pad_add_fusion.1.at_ref, bf16[16,128,128]{2,1,0:T(8,128)(2,1)S(1)} %all-to-all-done.4.back_ref, f32[128,512]{1,0:T(8,128)S(1)} %get-tuple-element.27.rows_ref, f32[8,128]{1,0:T(8,128)S(1)} %get-tuple-element.28.scale_ref, bf16[2,120,176]{2,1,0:T(8,128)(2,1)S(1)} %pad_maximum_fusion.1.refs_0_, ...), custom_call_target="tpu_custom_call" | custom-call | tf_op jit(solution)/shard_map/assemble/pallas_call | solution.py:471
  (39 shorter events, 0.8 us)
Async XLA Ops:
  1.5 4.4 %collective-permute-start.1 = (s32[14]{0:T(128)S(1)}, s32[14]{0:T(128)S(1)}, u32[]{:S(2)}, u32[]{:S(2)}) collective-permute-start(s32[14]{0:T(128)S(1)} %fusion.2), channel_id=1, source_target_pairs={{16,0},{32,16},{48,32},{64,48},{80,64},{96,80},{112,96},{17,1},{33... | collective-permute-start | bytes 176 | tf_op jit(solution)/shard_map/ppermute | solution.py:379
  2.8 3.8 %collective-permute-start = (s32[14]{0:T(128)S(1)}, s32[14]{0:T(128)S(1)}, u32[]{:S(2)}, u32[]{:S(2)}) collective-permute-start(s32[14]{0:T(128)S(1)} %fusion.2), channel_id=1, source_target_pairs={{0,16},{16,32},{32,48},{48,64},{64,80},{80,96},{96,112},{1,17},{17... | collective-permute-start | bytes 176 | tf_op jit(solution)/shard_map/ppermute | solution.py:379
  22.6 1.4 copy-start.8
  24.0 0.7 copy-start.9
  43.3 14.6 %collective-permute-start.2 = (f32[4,32,1792]{2,1,0:T(8,128)}, f32[4,32,1792]{2,1,0:T(8,128)}, u32[]{:S(2)}, u32[]{:S(2)}) collective-permute-start(f32[4,32,1792]{2,1,0:T(8,128)} %get-tuple-element.20), channel_id=1, source_target_pairs={{0,16},{16,32},{32,48},{48,64},{64,80},{80,96},{96,112},{1,17},{17... | collective-permute-start | bytes 2752520 | tf_op jit(solution)/shard_map/ppermute | solution.py:385
  45.8 12.1 %collective-permute-start.3 = (f32[4,32,1792]{2,1,0:T(8,128)}, f32[4,32,1792]{2,1,0:T(8,128)}, u32[]{:S(2)}, u32[]{:S(2)}) collective-permute-start(f32[4,32,1792]{2,1,0:T(8,128)} %get-tuple-element.22), channel_id=1, source_target_pairs={{16,0},{32,16},{48,32},{64,48},{80,64},{96,80},{112,96},{17,1},{33... | collective-permute-start | bytes 2752520 | tf_op jit(solution)/shard_map/ppermute | solution.py:386
  47.2 2.2 %copy-start = (bf16[1200,1792]{1,0:T(8,128)(2,1)S(1)}, bf16[1200,1792]{1,0:T(8,128)(2,1)}, u32[]{:S(2)}) copy-start(bf16[1200,1792]{1,0:T(8,128)(2,1)} %sub_ref.5) | copy-start | bytes 12902404
  54.6 10.2 %collective-permute-start.5 = (bf16[704,1200]{1,0:T(8,128)(2,1)}, bf16[704,1200]{1,0:T(8,128)(2,1)}, u32[]{:S(2)}, u32[]{:S(2)}) collective-permute-start(bf16[704,1200]{1,0:T(8,128)(2,1)} %basis_other.1), channel_id=1, source_target_pairs={{0,16},{16,0},{1,17},{17,1},{2,18},{18,2},{3,19},{19,3},{4,20},{20... | collective-permute-start | bytes 5068808 | tf_op jit(solution)/shard_map/ppermute | solution.py:404
  61.1 26.0 %all-to-all-start.1 = ((bf16[16,32,1792]{2,1,0:T(8,128)(2,1)}), bf16[16,32,1792]{2,1,0:T(8,128)(2,1)S(1)}, u32[]{:S(2)}, u32[]{:S(2)}) async-start(bf16[16,32,1792]{2,1,0:T(8,128)(2,1)} %pad_maximum_fusion), calls=%async_computation.1 | async-start | bytes 3670016 | tf_op jit(solution)/shard_map/all_to_all | solution.py:391
  64.8 2.2 %copy-start.1 = (bf16[1200,1792]{1,0:T(8,128)(2,1)S(1)}, bf16[1200,1792]{1,0:T(8,128)(2,1)}, u32[]{:S(2)}) copy-start(bf16[1200,1792]{1,0:T(8,128)(2,1)} %sub_ref.5) | copy-start | bytes 12902404
  74.6 28.6 %collective-permute-start.6 = (bf16[176,1200]{1,0:T(8,128)(2,1)}, bf16[176,1200]{1,0:T(8,128)(2,1)S(1)}, u32[]{:S(2)}, u32[]{:S(2)}) collective-permute-start(bf16[176,1200]{1,0:T(8,128)(2,1)} %get-tuple-element.31), channel_id=1, source_target_pairs={{0,32},{32,64},{64,96},{96,0},{1,33},{33,65},{65,97},{97,1},{2,34}... | collective-permute-start | bytes 1267208 | tf_op jit(solution)/shard_map/ppermute | solution.py:414
  80.0 23.6 %collective-permute-start.7 = (bf16[176,1200]{1,0:T(8,128)(2,1)}, bf16[176,1200]{1,0:T(8,128)(2,1)S(1)}, u32[]{:S(2)}, u32[]{:S(2)}) collective-permute-start(bf16[176,1200]{1,0:T(8,128)(2,1)} %get-tuple-element.32), channel_id=1, source_target_pairs={{0,64},{32,96},{64,0},{96,32},{1,65},{33,97},{65,1},{97,33},{2,66}... | collective-permute-start | bytes 1267208 | tf_op jit(solution)/shard_map/ppermute | solution.py:414
  82.9 20.7 %collective-permute-start.8 = (bf16[176,1200]{1,0:T(8,128)(2,1)}, bf16[176,1200]{1,0:T(8,128)(2,1)}, u32[]{:S(2)}, u32[]{:S(2)}) collective-permute-start(bf16[176,1200]{1,0:T(8,128)(2,1)} %get-tuple-element.33), channel_id=1, source_target_pairs={{0,96},{32,0},{64,32},{96,64},{1,97},{33,1},{65,33},{97,65},{2,98}... | collective-permute-start | bytes 1267208 | tf_op jit(solution)/shard_map/ppermute | solution.py:414
  87.1 2.2 %copy-start.2 = (bf16[1200,1792]{1,0:T(8,128)(2,1)S(1)}, bf16[1200,1792]{1,0:T(8,128)(2,1)}, u32[]{:S(2)}) copy-start(bf16[1200,1792]{1,0:T(8,128)(2,1)} %sub_ref.5) | copy-start | bytes 12902404
  95.5 1.2 copy-start.4
  96.8 1.2 copy-start.6
  98.0 15.1 %collective-permute-start.4 = (bf16[1712,256]{1,0:T(8,128)(2,1)}, bf16[1712,256]{1,0:T(8,128)(2,1)}, u32[]{:S(2)}, u32[]{:S(2)}) collective-permute-start(bf16[1712,256]{1,0:T(8,128)(2,1)} %get-tuple-element.24), channel_id=1, source_target_pairs={{0,16},{16,0},{1,17},{17,1},{2,18},{18,2},{3,19},{19,3},{4,20},{20... | collective-permute-start | bytes 2629640 | tf_op jit(solution)/shard_map/ppermute | solution.py:443
  105.0 8.2 %copy-start.7 = (f32[1712,256]{1,0:T(8,128)S(1)}, f32[1712,256]{1,0:T(8,128)}, u32[]{:S(2)}) copy-start(f32[1712,256]{1,0:T(8,128)} %copy-done.6) | copy-start | bytes 5259268
  106.3 20.8 %all-to-all-start.5 = ((bf16[16,120,176]{1,2,0:T(8,128)(2,1)}), bf16[16,120,176]{1,2,0:T(8,128)(2,1)S(1)}, u32[]{:S(2)}, u32[]{:S(2)}) async-start(bf16[16,120,176]{1,2,0:T(8,128)(2,1)} %copy.9), calls=%async_computation.5 | async-start | bytes 1441792 | tf_op jit(solution)/shard_map/all_to_all | solution.py:424
  127.1 19.6 %all-to-all-start.2 = ((bf16[16,128,256]{2,1,0:T(8,128)(2,1)}), bf16[16,128,256]{2,1,0:T(8,128)(2,1)S(1)}, u32[]{:S(2)}, u32[]{:S(2)}) async-start(bf16[16,128,256]{2,1,0:T(8,128)(2,1)} %windows.1), calls=%async_computation.2 | async-start | bytes 2097152 | tf_op jit(solution)/shard_map/all_to_all | solution.py:460
  131.0 33.7 %collective-permute-start.9 = (bf16[120,176]{1,0:T(8,128)(2,1)S(1)}, bf16[120,176]{1,0:T(8,128)(2,1)S(1)}, u32[]{:S(2)}, u32[]{:S(2)}) collective-permute-start(bf16[120,176]{1,0:T(8,128)(2,1)S(1)} %copy.10), channel_id=1, source_target_pairs={{0,16},{16,0},{1,17},{17,1},{2,18},{18,2},{3,19},{19,3},{4,20},{20... | collective-permute-start | bytes 126728 | tf_op jit(solution)/shard_map/ppermute | solution.py:425
  147.7 22.1 %all-to-all-start.3 = ((bf16[8,128,256]{2,1,0:T(8,128)(2,1)}), bf16[8,128,256]{2,1,0:T(8,128)(2,1)S(1)}, u32[]{:S(2)}, u32[]{:S(2)}) async-start(bf16[8,128,256]{2,1,0:T(8,128)(2,1)} %total.1), calls=%async_computation.3 | async-start | bytes 1048576 | tf_op jit(solution)/shard_map/all_to_all | solution.py:468
  164.8 21.7 %collective-permute-start.12 = (bf16[2,120,176]{2,1,0:T(8,128)(2,1)S(1)}, bf16[2,120,176]{2,1,0:T(8,128)(2,1)S(1)}, u32[]{:S(2)}, u32[]{:S(2)}) collective-permute-start(bf16[2,120,176]{2,1,0:T(8,128)(2,1)S(1)} %pad_maximum_fusion.1.refs_0_), channel_id=1, source_target_pairs={{0,96},{32,0},{64,32},{96,64},{1,97},{33,1},{65,33},{97,65},{2,98}... | collective-permute-start | bytes 253448 | tf_op jit(solution)/shard_map/ppermute | solution.py:426
  168.1 18.4 %collective-permute-start.11 = (bf16[2,120,176]{2,1,0:T(8,128)(2,1)S(1)}, bf16[2,120,176]{2,1,0:T(8,128)(2,1)S(1)}, u32[]{:S(2)}, u32[]{:S(2)}) collective-permute-start(bf16[2,120,176]{2,1,0:T(8,128)(2,1)S(1)} %pad_maximum_fusion.1.refs_0_), channel_id=1, source_target_pairs={{0,64},{32,96},{64,0},{96,32},{1,65},{33,97},{65,1},{97,33},{2,66}... | collective-permute-start | bytes 253448 | tf_op jit(solution)/shard_map/ppermute | solution.py:426
  168.9 17.5 %collective-permute-start.10 = (bf16[2,120,176]{2,1,0:T(8,128)(2,1)S(1)}, bf16[2,120,176]{2,1,0:T(8,128)(2,1)S(1)}, u32[]{:S(2)}, u32[]{:S(2)}) collective-permute-start(bf16[2,120,176]{2,1,0:T(8,128)(2,1)S(1)} %pad_maximum_fusion.1.refs_0_), channel_id=1, source_target_pairs={{0,32},{32,64},{64,96},{96,0},{1,33},{33,65},{65,97},{97,1},{2,34}... | collective-permute-start | bytes 253448 | tf_op jit(solution)/shard_map/ppermute | solution.py:426
  171.6 5.7 %copy-start.5 = (bf16[2,256,1792]{2,1,0:T(8,128)(2,1)S(1)}, bf16[2,256,1792]{2,1,0:T(8,128)(2,1)}, u32[]{:S(2)}) copy-start(bf16[2,256,1792]{2,1,0:T(8,128)(2,1)} %copy-done.4) | copy-start | bytes 5505028
  171.6 14.9 %all-to-all-start.4 = ((bf16[16,128,128]{2,1,0:T(8,128)(2,1)}), bf16[16,128,128]{2,1,0:T(8,128)(2,1)S(1)}, u32[]{:S(2)}, u32[]{:S(2)}) async-start(bf16[16,128,128]{2,1,0:T(8,128)(2,1)} %get-tuple-element.26), calls=%async_computation.4 | async-start | bytes 1048576 | tf_op jit(solution)/shard_map/all_to_all | solution.py:470
  177.3 3.4 %copy-start.3 = (f32[1200,1792]{1,0:T(8,128)S(1)}, f32[1200,1792]{1,0:T(8,128)}, u32[]{:S(2)}) copy-start(f32[1200,1792]{1,0:T(8,128)} %fusion.base_ref) | copy-start | bytes 25804804

commit v3 on v2

--- a/solution.py
+++ b/solution.py
@@ -21,6 +21,7 @@
 TALL = 128
 PART = 150
 WIDE = 176
+SHARE = 152
 LEAD = 384
 BLOCK = 256
 PHASES = 3
@@ -63,7 +64,7 @@
     return table
 
 
-def smooth_kernel(depth, own_ref, near_ref, tab_ref, mat_ref, raw_ref, mid_ref, rim_ref, up_ref, down_ref, pad, planar, sems):
+def smooth_kernel(depth, own_ref, near_ref, tab_ref, mat_ref, raw_ref, all_ref, rim_ref, up_ref, down_ref, pad, planar, mid_ref, sems, mid_sem):
     frames = raw_ref.shape[1]
     extent = raw_ref.shape[2]
     step = PHASES * BLOCK
@@ -128,14 +129,17 @@
         for j in range(per):
             cols = slice(j * RUN, (j + 1) * RUN)
             at = g * per + j
-            up_ref[g, :, cols] = some(near_ref[at], depth - RAD, RAD, -depth)
-            down_ref[g, :, cols] = some(near_ref[GRP // 4 * per + at], 0, RAD, depth)
+            up_ref[g, :, cols] = some(near_ref[at], depth - RAD, RAD, -depth).astype(up_ref.dtype)
+            down_ref[g, :, cols] = some(near_ref[GRP // 4 * per + at], 0, RAD, depth).astype(down_ref.dtype)
             rim_ref[g, :, cols] = some(own_ref[at], 0, 2 * RAD, 0)
             rim_ref[GRP // 4 + g, :, cols] = some(own_ref[GRP * 3 // 4 * per + at], depth - 2 * RAD, 2 * RAD, 0)
         return carry
 
+    lax.fori_loop(0, GRP // 2, middle, 0)
+    keep = pltpu.make_async_copy(mid_ref, all_ref.at[GRP // 4 : GRP * 3 // 4], mid_sem)
+    keep.start()
     lax.fori_loop(0, GRP // 4, rims, 0)
-    lax.fori_loop(0, GRP // 2, middle, 0)
+    keep.wait()
 
 
 def smooth(own, near, raw):
@@ -148,17 +152,19 @@
     return pl.pallas_call(
         functools.partial(smooth_kernel, depth),
         out_shape=[
-            jax.ShapeDtypeStruct(half, jnp.bfloat16),
+            jax.ShapeDtypeStruct((GRP, frames, per_device), jnp.bfloat16),
             jax.ShapeDtypeStruct(half, jnp.float32),
-            jax.ShapeDtypeStruct(quarter, jnp.float32),
-            jax.ShapeDtypeStruct(quarter, jnp.float32),
+            jax.ShapeDtypeStruct(quarter, jnp.bfloat16),
+            jax.ShapeDtypeStruct(quarter, jnp.bfloat16),
         ],
         in_specs=[smem, smem, smem, vmem, pl.BlockSpec(memory_space=pl.ANY)],
-        out_specs=[vmem] * 4,
+        out_specs=[pl.BlockSpec(memory_space=pltpu.HBM), vmem, vmem, vmem],
         scratch_shapes=[
             pltpu.VMEM((depth, frames, extent + 2 * LEAD), jnp.bfloat16),
             pltpu.VMEM((depth, frames, extent), jnp.float32),
+            pltpu.VMEM(half, jnp.bfloat16),
             pltpu.SemaphoreType.DMA((extent // (PHASES * BLOCK),)),
+            pltpu.SemaphoreType.DMA,
         ],
         compiler_params=pltpu.CompilerParams(vmem_limit_bytes=48 * 1024 * 1024),
         name="smooth",
@@ -188,43 +194,87 @@
     return pltpu.CompilerParams(vmem_limit_bytes=mib * 1024 * 1024)
 
 
-def gather_parts(x, which, sub_ref, left):
+def hbm():
+    return pl.BlockSpec(memory_space=pltpu.HBM)
+
+
+PIECE = 400
+PIECES = K // PIECE
+
+
+def basis_copies(x, which, sub_ref, left, right, sems):
+    made = []
     for k in range(4):
         start = pl.multiple_of(part_start((x + k) % 4 * 2 + which), 16)
-        left[k * WIDE : (k + 1) * WIDE, :] = sub_ref[pl.ds(start, WIDE), :]
-
-
-def basis_other_kernel(at_ref, sub_ref, out_ref, left):
-    gather_parts(at_ref[0], 1 - at_ref[1], sub_ref, left)
-    out_ref[...] = lax.dot_general(left[...], sub_ref[...], NT, preferred_element_type=jnp.float32).astype(out_ref.dtype)
+        made.append(
+            pltpu.make_async_copy(sub_ref.at[pl.ds(start, WIDE)], left.at[k * WIDE : (k + 1) * WIDE], sems.at[k])
+        )
+    for i in range(PIECES):
+        rows = slice(i * PIECE, (i + 1) * PIECE)
+        made.append(pltpu.make_async_copy(sub_ref.at[rows], right.at[rows], sems.at[4 + i]))
+    for copy in made:
+        copy.start()
+    return made
+
+
+def basis_other_kernel(at_ref, sub_ref, out_ref, left, right, sems):
+    made = basis_copies(at_ref[0], 1 - at_ref[1], sub_ref, left, right, sems)
+    for copy in made:
+        copy.wait()
+    out_ref[...] = lax.dot_general(left[...], right[...], NT, preferred_element_type=jnp.float32).astype(out_ref.dtype)
 
 
 def basis_own_kernel(at_ref, sub_ref, got_ref, *refs):
-    left = refs[-1]
-    gather_parts(at_ref[0], at_ref[1], sub_ref, left)
+    left, right, sems = refs[-3:]
+    made = basis_copies(at_ref[0], at_ref[1], sub_ref, left, right, sems)
+    for copy in made:
+        copy.wait()
     for k in range(4):
         rows = slice(k * WIDE, (k + 1) * WIDE)
-        made = lax.dot_general(left[rows, :], sub_ref[...], NT, preferred_element_type=jnp.float32)
-        refs[k][...] = (made + got_ref[rows, :].astype(jnp.float32)).astype(refs[k].dtype)
-
-
-def basis_rows_kernel(a_ref, b_ref, c_ref, d_ref, out_ref, flat):
-    flat[...] = jnp.zeros_like(flat)
+        part = lax.dot_general(left[rows, :], right[...], NT, preferred_element_type=jnp.float32)
+        refs[k][...] = (part + got_ref[rows, :].astype(jnp.float32)).astype(refs[k].dtype)
+
+
+def basis_rows_kernel(at_ref, a_ref, b_ref, c_ref, d_ref, out_ref, flat):
+    part = at_ref[0] * 2 + at_ref[1]
     total = a_ref[...].astype(jnp.float32) + b_ref[...].astype(jnp.float32)
-    flat[:WIDE, :K] = total + c_ref[...].astype(jnp.float32) + d_ref[...].astype(jnp.float32)
-    turned = flat[...].T
+    total = total + c_ref[...].astype(jnp.float32) + d_ref[...].astype(jnp.float32)
+    flat[:, K // RUN * RUN :] = jnp.zeros((flat.shape[0], flat.shape[1] - K // RUN * RUN), jnp.float32)
+    flat[:, :K] = total
+    shift = (WIDE - (part * PART - part_start(part))) % WIDE
+    narrow = pltpu.roll(flat[...], shift, 0)[:SHARE].astype(jnp.bfloat16)
+    line = lax.broadcasted_iota(jnp.int32, (256, RUN), 0)
+    lane = lax.broadcasted_iota(jnp.int32, (256, RUN), 1)
     for g in range(GRP):
-        first = row_start(g * ROWS)
-        if first + WIN <= turned.shape[0]:
-            out_ref[g] = turned[first : first + WIN, :WIDE].astype(out_ref.dtype)
+        begin = g * ROWS // RUN * RUN
+        if g * ROWS < K:
+            pick = jnp.where((line == lane + (g * ROWS - begin)) & (lane < ROWS), 1.0, 0.0).astype(jnp.bfloat16)
+            out_ref[g] = jnp.dot(narrow[:, begin : begin + 256], pick, preferred_element_type=jnp.float32).astype(
+                out_ref.dtype
+            )
         else:
-            out_ref[g] = jnp.zeros((WIN, WIDE), out_ref.dtype)
-
-
-def columns_kernel(at_ref, got_ref, sub_ref, cen_ref, other_ref, own_ref, power_ref):
+            out_ref[g] = jnp.zeros((SHARE, RUN), out_ref.dtype)
+
+
+def rim_kernel(rim_ref, low_ref, high_ref, all_ref, out_ref, made, sems):
+    del all_ref
+    quarter = GRP // 4
+    made[:quarter] = (rim_ref[:quarter] + low_ref[...].astype(jnp.float32)).astype(made.dtype)
+    first = pltpu.make_async_copy(made.at[:quarter], out_ref.at[:quarter], sems.at[0])
+    first.start()
+    made[quarter:] = (rim_ref[quarter:] + high_ref[...].astype(jnp.float32)).astype(made.dtype)
+    second = pltpu.make_async_copy(made.at[quarter:], out_ref.at[3 * quarter :], sems.at[1])
+    second.start()
+    first.wait()
+    second.wait()
+
+
+def columns_kernel(at_ref, got_ref, basis_ref, cen_out, other_ref, own_out, power_ref, sub_ref, cen_ref, own_ref, sems):
     per_device = sub_ref.shape[1]
     core = at_ref[1]
     each = GRP // 2
+    fetch = pltpu.make_async_copy(basis_ref, sub_ref, sems.at[0])
+    fetch.start()
 
     def centre(i, sums):
         cols = pl.ds(pl.multiple_of(i * RUN, RUN), RUN)
@@ -240,12 +290,15 @@
 
     zero = jnp.zeros((8, RUN), jnp.float32)
     sums = lax.fori_loop(0, per_device // RUN, centre, (zero, zero))
+    keep = pltpu.make_async_copy(cen_ref, cen_out, sems.at[1])
+    keep.start()
     line = lax.broadcasted_iota(jnp.int32, (8, RUN), 0)
     first = jnp.sum(sums[0], keepdims=True)
     second = jnp.sum(sums[1], keepdims=True)
     power_ref[...] = jnp.where(line == 0, first, jnp.where(line == 1, second, 0.0))
 
-    for which, out in ((1 - core, other_ref), (core, own_ref)):
+    fetch.wait()
+    for which, out in ((core, own_ref), (1 - core, other_ref)):
         right = cen_ref[which]
         for lo in range(0, K, 400):
             out[lo : lo + 400, :] = lax.dot_general(
@@ -256,47 +309,72 @@
             out[lo : lo + SUBJ, :] = lax.dot_general(
                 cen_ref[s], right, NT, preferred_element_type=jnp.float32
             ).astype(out.dtype)
-
-
-def write_power(power, out_ref, at):
+        if out is own_ref:
+            leave = pltpu.make_async_copy(own_ref, own_out, sems.at[2])
+            leave.start()
+    leave.wait()
+    keep.wait()
+
+
+def write_power(power, put):
     high = power.astype(jnp.bfloat16)
-    low = (power - high.astype(jnp.float32)).astype(jnp.bfloat16)
-    out_ref[at, WIN:, :RUN] = high
-    out_ref[at, WIN:, RUN:] = low
-
-
-def windows_kernel(own_ref, got_ref, power_ref, out_ref, whole):
-    whole[...] = own_ref[...] + got_ref[...].astype(jnp.float32)
+    put(slice(WIN, TALL), high)
+    put(slice(TALL + WIN, 2 * TALL), (power - high.astype(jnp.float32)).astype(jnp.bfloat16))
+
+
+def windows_kernel(own_ref, got_ref, power_ref, basis_ref, out_ref, whole, sem):
+    fetch = pltpu.make_async_copy(own_ref, whole, sem)
+    fetch.start()
+    for g in range(GRP):
+        out_ref[g, 2 * TALL :, :] = basis_ref[g]
+
+        def put(rows, value, g=g):
+            out_ref[g, rows, :] = value
+
+        write_power(power_ref[...], put)
+    fetch.wait()
+    whole[...] = whole[...] + got_ref[...].astype(jnp.float32)
     for g in range(GRP):
         first = row_start(g * ROWS)
-        out_ref[g, :WIN, :] = whole[first : first + WIN, :].astype(out_ref.dtype)
-        write_power(power_ref[...], out_ref, g)
+        for half in range(2):
+            out_ref[g, half * TALL : half * TALL + WIN, :] = whole[
+                first : first + WIN, half * RUN : (half + 1) * RUN
+            ].astype(out_ref.dtype)
 
 
 def total_kernel(got_ref, out_ref):
     total = got_ref[0].astype(jnp.float32)
     for g in range(1, GRP):
         total = total + got_ref[g].astype(jnp.float32)
-    power = total[WIN:, :RUN] + total[WIN:, RUN:]
-    rows = total[:WIN].astype(out_ref.dtype)
-    for p in range(8):
-        out_ref[p, :WIN, :] = rows
-        write_power(power, out_ref, p)
-
-
-def finish_kernel(count, at_ref, got_ref, rows_ref, scale_ref, turned_ref):
-    halves = []
-    power = jnp.zeros((8, RUN), jnp.float32)
-    for c in range(2):
-        total = got_ref[c].astype(jnp.float32)
-        for x in range(1, 4):
-            total = total + got_ref[2 * x + c].astype(jnp.float32)
-        power = power + total[WIN:, :RUN] + total[WIN:, RUN:]
-        halves.append(total)
-    scale_ref[...] = lax.rsqrt(power / count + epsilon)
+    out_ref[...] = total.astype(out_ref.dtype)
+
+    def put(rows, value):
+        out_ref[rows, :] = value
+
+    write_power(total[WIN:TALL] + total[TALL + WIN : 2 * TALL], put)
+
+
+def slab_kernel(a_ref, b_ref, c_ref, d_ref, sum_ref, parts_ref):
+    refs = (a_ref, b_ref, c_ref, d_ref)
+    total = refs[0][: 2 * TALL].astype(jnp.float32)
+    for ref in refs[1:]:
+        total = total + ref[: 2 * TALL].astype(jnp.float32)
+    sum_ref[...] = total
+    for k in range(4):
+        parts_ref[k] = refs[k][2 * TALL :]
+
+
+def finish_kernel(count, at_ref, own_ref, got_ref, rows_ref, scale_ref, turned_ref):
+    own, got = own_ref[...], got_ref[...]
+    both = own + got
+    scale_ref[...] = lax.rsqrt((both[WIN:TALL] + both[TALL + WIN :]) / count + epsilon)
+    is_first = at_ref[1] == 0
+    zero = jnp.where(is_first, own, got)
+    one = jnp.where(is_first, got, own)
+    rows = jnp.concatenate([zero[:TALL], zero[TALL:], one[:TALL], one[TALL:]], axis=1)
     first = at_ref[2] * ROWS
     shift = (TALL - (first - row_start(first))) % TALL
-    rows = pltpu.roll(jnp.concatenate(halves, axis=1), shift, 0)
+    rows = pltpu.roll(rows, shift, 0)
     rows_ref[...] = rows
     narrow = rows.astype(jnp.bfloat16)
     turned_ref[: K // ROWS] = jnp.zeros((K // ROWS, TALL, TALL), turned_ref.dtype)
@@ -307,23 +385,22 @@
         turned_ref[g] = lax.dot_general(pick, narrow, NT, preferred_element_type=jnp.float32).astype(turned_ref.dtype)
 
 
-def assemble_kernel(masked, at_ref, back_ref, rows_ref, scale_ref, *refs):
-    out_ref, basis, cross = refs[-3:]
+def assemble_kernel(masked, at_ref, back_ref, rows_ref, scale_ref, own_ref, got_ref, out_ref, basis, cross):
     x, core, grp = at_ref[0], at_ref[1], at_ref[2]
     first = grp * ROWS
     basis[...] = jnp.zeros_like(basis)
     cross[...] = jnp.zeros_like(cross)
-    line = lax.broadcasted_iota(jnp.int32, (WIDE, 384), 0)
-    lane = lax.broadcasted_iota(jnp.int32, (WIDE, 384), 1)
+    line = lax.broadcasted_iota(jnp.int32, (SHARE, 384), 0)
+    lane = lax.broadcasted_iota(jnp.int32, (SHARE, 384), 1)
     for k in range(4):
-        for c in range(2):
-            part = (x - k + 4) % 4 * 2 + (core if c == 0 else 1 - core)
+        for ref, which in ((own_ref, core), (got_ref, 1 - core)):
+            part = (x - k + 4) % 4 * 2 + which
             begin = part * PART // RUN * RUN
-            cell = line + (part_start(part) - begin)
-            ok = (cell == lane) & (cell >= part * PART - begin) & (cell < part * PART - begin + PART)
-            put = jnp.where(ok, 1.0, 0.0).astype(jnp.bfloat16)
+            put = jnp.where((line + (part * PART - begin) == lane) & (line < PART), 1.0, 0.0).astype(jnp.bfloat16)
             cols = pl.ds(pl.multiple_of(begin, RUN), 384)
-            basis[:WIN, cols] += jnp.dot(refs[k][c], put, preferred_element_type=jnp.float32)
+            basis[:, cols] += lax.dot_general(
+                ref[k], put, (((0,), (0,)), ((), ())), preferred_element_type=jnp.float32
+            )
     line = lax.broadcasted_iota(jnp.int32, (TALL, 256), 0)
     lane = lax.broadcasted_iota(jnp.int32, (TALL, 256), 1)
     for g in range(K // ROWS + 1):
@@ -331,10 +408,9 @@
         ok = (line + (g * ROWS - begin) == lane) & (line < ROWS) & (line + g * ROWS < K)
         put = jnp.where(ok, 1.0, 0.0).astype(jnp.bfloat16)
         cross[:, begin : begin + 256] += jnp.dot(back_ref[g], put, preferred_element_type=jnp.float32)
-    shift = (TALL - (first - row_start(first))) % TALL
     width = 1792
     row = first + lax.broadcasted_iota(jnp.int32, (TALL, 1), 0)
-    left = jnp.where(row < K, pltpu.roll(basis[...], shift, 0), cross[...])
+    left = jnp.where(row < K, basis[...], cross[...])
     base = K // RUN * RUN
     right = pltpu.roll(
         jnp.concatenate([rows_ref[...], jnp.zeros((TALL, RUN), jnp.float32)], axis=1), K - base, 1
@@ -349,10 +425,27 @@
     out_ref[:, base:] = (values * (of_row * of_col[:, base:]) / masked)[:ROWS, : KX - base]
 
 
-def rotate_kernel(scale_ref, base_ref, turn_ref, cen_ref, out_ref):
+def rotate_kernel(tile, scale_ref, base_ref, turn_ref, cen_ref, out_ref, held, sems):
+    step = pl.program_id(0)
+    steps = pl.num_programs(0)
+
+    def fetch(i):
+        cols = pl.ds(pl.multiple_of(i * tile, tile), tile)
+        return pltpu.make_async_copy(base_ref.at[:, cols], held.at[i % 2], sems.at[i % 2])
+
+    @pl.when(step == 0)
+    def _():
+        fetch(step).start()
+
+    @pl.when(step + 1 < steps)
+    def _():
+        fetch(step + 1).start()
+
     first = jnp.dot(turn_ref[:, :SUBJ], cen_ref[0], preferred_element_type=jnp.float32)
     second = jnp.dot(turn_ref[:, SUBJ:], cen_ref[1], preferred_element_type=jnp.float32)
-    out_ref[...] = (base_ref[...] + scale_ref[0:1, 0:1] * first + scale_ref[1:2, 0:1] * second).astype(out_ref.dtype)
+    fetch(step).wait()
+    base = held[step % 2]
+    out_ref[...] = (base + scale_ref[0:1, 0:1] * first + scale_ref[1:2, 0:1] * second).astype(out_ref.dtype)
 
 
 def copies(value, axis, count):
@@ -381,23 +474,27 @@
     own = every[:, 0].reshape(-1)
     near = jnp.concatenate([every[: GRP // 4, 2].reshape(-1), every[3 * GRP // 4 :, 1].reshape(-1)])
 
-    mid, rim, to_up, to_down = smooth(own, near, jnp.transpose(raw_frames, (1, 0, 2)))
-    from_low = lax.ppermute(to_up, slab, up)
-    from_high = lax.ppermute(to_down, slab, down)
-    quarter = GRP // 4
-    low = (rim[:quarter] + from_low).astype(bf16)
-    high = (rim[quarter:] + from_high).astype(bf16)
-    placed = jnp.concatenate([low, mid, high])
+    middles, rim, to_up, to_down = smooth(own, near, jnp.transpose(raw_frames, (1, 0, 2)))
+    placed = pl.pallas_call(
+        rim_kernel,
+        out_shape=like(middles.shape, bf16),
+        in_specs=[*vmem(3), hbm()],
+        out_specs=hbm(),
+        scratch_shapes=[pltpu.VMEM(rim.shape, bf16), pltpu.SemaphoreType.DMA((2,))],
+        input_output_aliases={3: 0},
+        compiler_params=params(16),
+        name="rim",
+    )(rim, lax.ppermute(to_up, slab, up), lax.ppermute(to_down, slab, down), middles)
     regrouped = lax.all_to_all(placed, "grp", 0, 0, tiled=True)
 
     at_ss, _ = lax.optimization_barrier((at, to_down))
-    left = pltpu.VMEM((4 * WIDE, per_device), bf16)
+    held = [pltpu.VMEM((4 * WIDE, per_device), bf16), pltpu.VMEM((K, per_device), bf16), pltpu.SemaphoreType.DMA((4 + PIECES,))]
     other_ss = pl.pallas_call(
         basis_other_kernel,
         out_shape=like((4 * WIDE, K), bf16),
-        in_specs=[smem(), *vmem(1)],
+        in_specs=[smem(), hbm()],
         out_specs=vmem(1)[0],
-        scratch_shapes=[left],
+        scratch_shapes=held,
         compiler_params=params(24),
         name="basis_other",
     )(at_ss, subspace)
@@ -405,91 +502,102 @@
     parts = pl.pallas_call(
         basis_own_kernel,
         out_shape=[like((WIDE, K), bf16)] * 4,
-        in_specs=[smem(), *vmem(2)],
+        in_specs=[smem(), hbm(), *vmem(1)],
         out_specs=vmem(4),
-        scratch_shapes=[left],
+        scratch_shapes=held,
         compiler_params=params(24),
         name="basis_own",
     )(at_ss, subspace, got_ss)
     parts = [parts[0]] + [lax.ppermute(parts[k], "x", turns[k]) for k in range(1, 4)]
     by_row = pl.pallas_call(
         basis_rows_kernel,
-        out_shape=like((GRP, WIN, WIDE), bf16),
-        in_specs=vmem(4),
+        out_shape=like((GRP, SHARE, RUN), bf16),
+        in_specs=[smem(), *vmem(4)],
         out_specs=vmem(1)[0],
-        scratch_shapes=[pltpu.VMEM((256, 1408), f32)],
+        scratch_shapes=[pltpu.VMEM((WIDE, 1408), f32)],
         compiler_params=params(16),
         name="basis_rows",
-    )(*parts)
-    grp_ss = jnp.sum(lax.all_to_all(by_row, "grp", 0, 0, tiled=True).astype(f32), axis=0).astype(bf16)
-    pair_ss = jnp.stack([grp_ss, lax.ppermute(grp_ss, "core", swap)])
-    all_ss = [pair_ss] + [lax.ppermute(pair_ss, "x", turns[k]) for k in range(1, 4)]
-
-    rotation_b, _ = lax.optimization_barrier((rotation, placed))
-    contract = (((0,), (0,)), ((), ()))
-    from_basis = lax.optimization_barrier(
-        lax.dot_general(rotation_b[:K], subspace, contract, preferred_element_type=f32)
-    )
-    turn = lax.optimization_barrier(rotation_b[K:].T)
+    )(at, *parts)
 
     centered, other_c, own_c, power = pl.pallas_call(
         columns_kernel,
         out_shape=[like((2, SUBJ, per_device), bf16), like((KX, SUBJ), bf16), like((KX, SUBJ), f32), like((8, RUN), f32)],
-        in_specs=[smem(), *vmem(2)],
-        out_specs=vmem(4),
+        in_specs=[smem(), *vmem(1), hbm()],
+        out_specs=[hbm(), *vmem(1), hbm(), *vmem(1)],
+        scratch_shapes=[
+            pltpu.VMEM((K, per_device), bf16),
+            pltpu.VMEM((2, SUBJ, per_device), bf16),
+            pltpu.VMEM((KX, SUBJ), f32),
+            pltpu.SemaphoreType.DMA((3,)),
+        ],
         compiler_params=params(24),
         name="columns",
     )(at, regrouped, subspace)
-    got_c = lax.ppermute(other_c, "core", swap)
-    by_row_c = pl.pallas_call(
+    sent = pl.pallas_call(
         windows_kernel,
-        out_shape=like((GRP, TALL, SUBJ), bf16),
-        in_specs=vmem(3),
+        out_shape=like((GRP, 2 * TALL + SHARE, RUN), bf16),
+        in_specs=[hbm(), *vmem(3)],
         out_specs=vmem(1)[0],
-        scratch_shapes=[pltpu.VMEM((KX, SUBJ), f32)],
+        scratch_shapes=[pltpu.VMEM((KX, SUBJ), f32), pltpu.SemaphoreType.DMA],
         compiler_params=params(16),
         name="windows",
-    )(own_c, got_c, power)
-    sum_c = pl.pallas_call(
+    )(own_c, lax.ppermute(other_c, "core", swap), power, by_row)
+    summed = lax.all_to_all(sent, "grp", 0, 0, tiled=True)
+
+    rotation_b, _ = lax.optimization_barrier((rotation, sent))
+    contract = (((0,), (0,)), ((), ()))
+    from_basis = lax.dot_general(rotation_b[:K], subspace, contract, preferred_element_type=f32)
+    summed, from_basis, turn = lax.optimization_barrier((summed, from_basis, rotation_b[K:].T))
+
+    total = pl.pallas_call(
         total_kernel,
-        out_shape=like((8, TALL, SUBJ), bf16),
+        out_shape=like((2 * TALL + SHARE, RUN), bf16),
         in_specs=vmem(1),
         out_specs=vmem(1)[0],
         compiler_params=params(16),
         name="total",
-    )(lax.all_to_all(by_row_c, "grp", 0, 0, tiled=True))
+    )(summed)
+    sum_c, parts_ss = pl.pallas_call(
+        slab_kernel,
+        out_shape=[like((2 * TALL, RUN), f32), like((4, SHARE, RUN), bf16)],
+        in_specs=vmem(4),
+        out_specs=vmem(2),
+        compiler_params=params(16),
+        name="slab",
+    )(total, *[lax.ppermute(total, "x", turns[k]) for k in range(1, 4)])
     rows_c, scales, turned = pl.pallas_call(
         functools.partial(finish_kernel, float(masked * SUBJ)),
         out_shape=[like((TALL, 2 * SUBJ), f32), like((8, RUN), f32), like((GRP, TALL, TALL), bf16)],
-        in_specs=[smem(), *vmem(1)],
+        in_specs=[smem(), *vmem(2)],
         out_specs=vmem(3),
         compiler_params=params(16),
         name="finish",
-    )(at, lax.all_to_all(sum_c, slab, 0, 0, tiled=True))
+    )(at, sum_c, lax.ppermute(sum_c, "core", swap))
 
     back = lax.all_to_all(turned, "grp", 0, 0, tiled=True)
     gram_rows = pl.pallas_call(
         functools.partial(assemble_kernel, float(masked)),
         out_shape=like((ROWS, KX), f32),
-        in_specs=[smem(), *vmem(7)],
+        in_specs=[smem(), *vmem(5)],
         out_specs=vmem(1)[0],
         scratch_shapes=[pltpu.VMEM((TALL, 1408), f32), pltpu.VMEM((TALL, 1408), f32)],
         compiler_params=params(16),
         name="assemble",
-    )(at, back, rows_c, scales, *all_ss)
+    )(at, back, rows_c, scales, parts_ss, lax.ppermute(parts_ss, "core", swap))
 
     tile = 256
     new_subspace = pl.pallas_call(
-        rotate_kernel,
+        functools.partial(rotate_kernel, tile),
         out_shape=like((K, per_device), bf16),
         grid=(per_device // tile,),
         in_specs=[
             pl.BlockSpec((8, RUN), lambda i: (0, 0)),
-            pl.BlockSpec((K, tile), lambda i: (0, i)),
+            hbm(),
             pl.BlockSpec((K, 2 * SUBJ), lambda i: (0, 0)),
             pl.BlockSpec((2, SUBJ, tile), lambda i: (0, 0, i)),
         ],
         out_specs=pl.BlockSpec((K, tile), lambda i: (0, i)),
+        scratch_shapes=[pltpu.VMEM((2, K, tile), f32), pltpu.SemaphoreType.DMA((2,))],
         compiler_params=params(24),
         name="rotate",
     )(scales, from_basis, turn, centered)

time: 190 us -> 198 us (1.042)
  waiting for transfers between devices: 31.3 us -> 47.1 us
  starting transfers between devices: 55.7 us -> 48.7 us
  Pallas kernels: 52 us -> 56.3 us
  other arithmetic: 3.56 us -> 0.19 us
  local copies, waits for them, and re-layouts: 19.1 us -> 17 us
    ppermute x3, waiting for transfers between devices: 0.32 us -> 17.5 us  [body(): lax.ppermute(parts[k], 'x', turns[k])]
    all_to_all x3 -> x1, waiting for transfers between devices: 27.2 us -> 11.9 us  [body(): summed = lax.all_to_all(sent, 'grp', 0, 0, tiled=True)]
    all_to_all x3 -> x1, starting transfers between devices: 17 us -> 4.54 us  [body(): summed = lax.all_to_all(sent, 'grp', 0, 0, tiled=True)]
    ppermute x7 -> x8, waiting for transfers between devices: 0.02 us -> 10.5 us  [the longest x1 5.41 us: body(): lax.ppermute(to_down, slab, down)]
    all_to_all x1, waiting for transfers between devices: 3 us -> 6.4 us  [body(): regrouped = lax.all_to_all(placed, 'grp', 0, 0, tiled=True)]
    ppermute x1, starting transfers between devices: 3.29 us -> 6.67 us  [body(): got_ss = lax.ppermute(other_ss, 'core', swap)]
    pallas_call x4 -> x6, Pallas kernels: 10.4 us -> 12.8 us  [the longest x1 8.38 us: body(): pl.pallas_call(functools.partial(rotate_kernel, tile), out_shape=like((K,...]
    ppermute x3, starting transfers between devices: 9.49 us -> 11.6 us  [body(): lax.ppermute(parts[k], 'x', turns[k])]
  transfers between devices with their start and end apart: 18 -> 17, of which waited for: 5 -> 11; matrix products, arithmetic and copies ran while one was open for 9% -> 6% of each run, Pallas kernels for 16% -> 16%
where the time goes in v3:
time: 198 us; the launch traced here: 196 us
  Pallas kernels  56.3 us (28%)
  starting transfers between devices  48.7 us (25%)
  waiting for transfers between devices  47.1 us (24%)
  local copies, waits for them, and re-layouts  17 us (9%)
  blocking collectives  15.6 us (8%)
  matrix products  10.7 us (5%)
    pallas_call x1, Pallas kernels, smooth(): pl.pallas_call(functools.partial(smooth_kernel, depth), out_shape=[jax.Sh...  17.7 us
    ppermute x3, waiting for transfers between devices, body(): lax.ppermute(parts[k], 'x', turns[k])  17.5 us
    all_to_all x1, blocking collectives, copies(): lax.all_to_all(jnp.broadcast_to(value[None], (count, *value.shape)), axis...  15.6 us
    unnamed x16, local copies, waits for them, and re-layouts  13.9 us
    all_to_all x1, waiting for transfers between devices, body(): summed = lax.all_to_all(sent, 'grp', 0, 0, tiled=True)  11.9 us
    ppermute x3, starting transfers between devices, body(): lax.ppermute(parts[k], 'x', turns[k])  11.6 us
    dot_general x1, matrix products, body(): lax.dot_general(rotation_b[:K], subspace, contract, preferred_element_typ...  10.7 us
    pallas_call x1, Pallas kernels, body(): pl.pallas_call(functools.partial(rotate_kernel, tile), out_shape=like((K,...  8.38 us
  transfers between devices with their start and end apart: 17, of which 11 were waited for; matrix products, arithmetic and copies ran while one was open for 6% of the time, Pallas kernels for 16%

profile of v3, /device:TPU:0, one launch (start us, length us, event | category | flops | bytes accessed | tf_op | source)
XLA Modules:
  0.0 196.3 jit_solution(14691569512957201840)
XLA Ops:
  0.6 0.8 slice_reduce_fusion.1
  1.5 1.3 collective-permute-start.1
  2.8 3.0 %collective-permute-start = (s32[14]{0:T(128)S(1)}, s32[14]{0:T(128)S(1)}, u32[]{:S(2)}, u32[]{:S(2)}) collective-permute-start(s32[14]{0:T(128)S(1)} %fusion.2), channel_id=1, source_target_pairs={{0,16},{16,32},{32,48},{48,64},{64,80},{80,96},{96,112},{1,17},{17... | collective-permute-start | bytes 176 | tf_op jit(solution)/shard_map/ppermute | solution.py:472
  5.8 0.8 collective-permute-done
  6.6 15.6 %all_to_all.20 = s32[16,3,14]{2,1,0:T(4,128)S(1)} all-to-all(s32[16,3,14]{2,1,0:T(4,128)S(1)} %broadcast_in_dim.2), channel_id=1, replica_groups=mesh['x'=4,'core'=2,'grp'=16] {'grp'}, dimensions={0} | all-to-all | bytes 5376 | tf_op jit(solution)/shard_map/all_to_all | solution.py:452
  22.6 1.4 copy-done.6
  24.0 0.7 copy-done.7
  24.7 17.7 %smooth.1 = (bf16[16,32,1792]{2,1,0:T(8,128)(2,1)S(1)}, f32[8,32,1792]{2,1,0:T(8,128)S(1)}, bf16[4,32,1792]{2,1,0:T(8,128)(2,1)S(1)}, bf16[4,32,1792]{2,1,0:T(8,128)(2,1)S(1)}) custom-call(s32[224]{0:T(256)S(1)} %reshape_squeeze.9.own_ref, s32[112]{0:T(128)S(1)} %pad_add_fusion.2.near_ref, f32[64]{0:T(128)S(1)} %copy-done.7, ...), custom_call_target="tpu_custom_call" | custom-call | tf_op jit(solution)/shard_map/smooth/pallas_call | solution.py:152
  42.3 1.6 collective-permute-start.2
  43.9 1.3 collective-permute-start.3
  45.3 5.4 %collective-permute-done.3.high_ref = bf16[4,32,1792]{2,1,0:T(8,128)(2,1)S(1)} collective-permute-done((bf16[4,32,1792]{2,1,0:T(8,128)(2,1)S(1)}, bf16[4,32,1792]{2,1,0:T(8,128)(2,1)S(1)}, u32[]{:S(2)}, u32[]{:S(2)}) %collective-permute-start.3) | collective-permute-done | bytes 458784 | tf_op jit(solution)/shard_map/ppermute | solution.py:487
  50.7 0.7 rim.1
  51.5 1.2 copy-done.3
  52.7 3.7 %all-to-all-start.1 = ((bf16[16,32,1792]{2,1,0:T(8,128)(2,1)}), bf16[16,32,1792]{2,1,0:T(8,128)(2,1)S(1)}, u32[]{:S(2)}, u32[]{:S(2)}) async-start(bf16[16,32,1792]{2,1,0:T(8,128)(2,1)} %copy-done.3), calls=%async_computation.1 | async-start | bytes 3670016 | tf_op jit(solution)/shard_map/all_to_all | solution.py:488
  56.5 2.2 %copy-done = bf16[1200,1792]{1,0:T(8,128)(2,1)S(1)} copy-done((bf16[1200,1792]{1,0:T(8,128)(2,1)S(1)}, bf16[1200,1792]{1,0:T(8,128)(2,1)}, u32[]{:S(2)}) %copy-start) | copy-done | bytes 4300824
  58.7 6.8 %basis_other.1 = bf16[704,1200]{1,0:T(8,128)(2,1)} custom-call(s32[3]{0:T(128)S(1)} %pad_add_fusion.1.at_ref, bf16[1200,1792]{1,0:T(8,128)(2,1)S(1)} %copy-done), custom_call_target="tpu_custom_call" | custom-call | tf_op jit(solution)/shard_map/basis_other/pallas_call | solution.py:492
  65.5 6.7 %collective-permute-start.5 = (bf16[704,1200]{1,0:T(8,128)(2,1)}, bf16[704,1200]{1,0:T(8,128)(2,1)}, u32[]{:S(2)}, u32[]{:S(2)}) collective-permute-start(bf16[704,1200]{1,0:T(8,128)(2,1)} %basis_other.1), channel_id=1, source_target_pairs={{0,16},{16,0},{1,17},{17,1},{2,18},{18,2},{3,19},{19,3},{4,20},{20... | collective-permute-start | bytes 5068808 | tf_op jit(solution)/shard_map/ppermute | solution.py:501
  72.2 6.4 %all-to-all-done.1.got_ref = bf16[16,32,1792]{2,1,0:T(8,128)(2,1)S(1)} async-done(((bf16[16,32,1792]{2,1,0:T(8,128)(2,1)}), bf16[16,32,1792]{2,1,0:T(8,128)(2,1)S(1)}, u32[]{:S(2)}, u32[]{:S(2)}) %all-to-all-start.1) | async-done | bytes 1835040 | tf_op jit(solution)/shard_map/all_to_all | solution.py:488
  78.6 2.2 %copy-done.1 = bf16[1200,1792]{1,0:T(8,128)(2,1)S(1)} copy-done((bf16[1200,1792]{1,0:T(8,128)(2,1)S(1)}, bf16[1200,1792]{1,0:T(8,128)(2,1)}, u32[]{:S(2)}) %copy-start.1) | copy-done | bytes 4300824
  80.8 6.9 %columns.1 = (bf16[2,256,1792]{2,1,0:T(8,128)(2,1)S(1)}, bf16[1712,256]{1,0:T(8,128)(2,1)S(1)}, f32[1712,256]{1,0:T(8,128)S(1)}, f32[8,128]{1,0:T(8,128)S(1)}) custom-call(s32[3]{0:T(128)S(1)} %pad_add_fusion.1.at_ref, bf16[16,32,1792]{2,1,0:T(8,128)(2,1)S(1)} %all-to-all-done.1.got_ref, bf16[1200,1792]{1,0:T(8,128)(2,1)S(1)} %copy-done.1), custom_call_target="tpu_custom_call" | custom-call | tf_op jit(solution)/shard_map/columns/pallas_call | solution.py:522
  87.7 1.2 copy-done.4
  88.9 5.3 %collective-permute-start.4 = (bf16[1712,256]{1,0:T(8,128)(2,1)S(1)}, bf16[1712,256]{1,0:T(8,128)(2,1)S(1)}, u32[]{:S(2)}, u32[]{:S(2)}) collective-permute-start(bf16[1712,256]{1,0:T(8,128)(2,1)S(1)} %get-tuple-element.29), channel_id=1, source_target_pairs={{0,16},{16,0},{1,17},{17,1},{2,18},{18,2},{3,19},{19,3},{4,20},{20... | collective-permute-start | bytes 2629640 | tf_op jit(solution)/shard_map/ppermute | solution.py:544
  94.2 8.3 %basis_own.1 = (bf16[176,1200]{1,0:T(8,128)(2,1)S(1)}, bf16[176,1200]{1,0:T(8,128)(2,1)S(1)}, bf16[176,1200]{1,0:T(8,128)(2,1)S(1)}, bf16[176,1200]{1,0:T(8,128)(2,1)S(1)}) custom-call(s32[3]{0:T(128)S(1)} %pad_add_fusion.1.at_ref, bf16[1200,1792]{1,0:T(8,128)(2,1)S(1)} %copy-done.1, bf16[704,1200]{1,0:T(8,128)(2,1)} %collective-permute-done.5.got_ref), custom_call_target="tpu_custom_call" | custom-call | tf_op jit(solution)/shard_map/basis_own/pallas_call | solution.py:502
  102.5 7.6 %collective-permute-start.6 = (bf16[176,1200]{1,0:T(8,128)(2,1)S(1)}, bf16[176,1200]{1,0:T(8,128)(2,1)S(1)}, u32[]{:S(2)}, u32[]{:S(2)}) collective-permute-start(bf16[176,1200]{1,0:T(8,128)(2,1)S(1)} %get-tuple-element.33), channel_id=1, source_target_pairs={{0,32},{32,64},{64,96},{96,0},{1,33},{33,65},{65,97},{97,1},{2,34}... | collective-permute-start | bytes 1267208 | tf_op jit(solution)/shard_map/ppermute | solution.py:511
  110.1 1.7 collective-permute-start.7
  111.8 2.4 %collective-permute-start.8 = (bf16[176,1200]{1,0:T(8,128)(2,1)S(1)}, bf16[176,1200]{1,0:T(8,128)(2,1)S(1)}, u32[]{:S(2)}, u32[]{:S(2)}) collective-permute-start(bf16[176,1200]{1,0:T(8,128)(2,1)S(1)} %get-tuple-element.35), channel_id=1, source_target_pairs={{0,96},{32,0},{64,32},{96,64},{1,97},{33,1},{65,33},{97,65},{2,98}... | collective-permute-start | bytes 1267208 | tf_op jit(solution)/shard_map/ppermute | solution.py:511
  114.1 6.7 %collective-permute-done.6.b_ref = bf16[176,1200]{1,0:T(8,128)(2,1)S(1)} collective-permute-done((bf16[176,1200]{1,0:T(8,128)(2,1)S(1)}, bf16[176,1200]{1,0:T(8,128)(2,1)S(1)}, u32[]{:S(2)}, u32[]{:S(2)}) %collective-permute-start.6) | collective-permute-done | bytes 422432 | tf_op jit(solution)/shard_map/ppermute | solution.py:511
  120.8 10.8 %collective-permute-done.7.c_ref = bf16[176,1200]{1,0:T(8,128)(2,1)S(1)} collective-permute-done((bf16[176,1200]{1,0:T(8,128)(2,1)S(1)}, bf16[176,1200]{1,0:T(8,128)(2,1)S(1)}, u32[]{:S(2)}, u32[]{:S(2)}) %collective-permute-start.7) | collective-permute-done | bytes 422432 | tf_op jit(solution)/shard_map/ppermute | solution.py:511
  131.6 1.5 basis_rows.1.basis_ref
  133.2 1.9 windows.1
  135.1 4.5 %all-to-all-start.2 = ((bf16[16,408,128]{2,1,0:T(8,128)(2,1)}), bf16[16,408,128]{2,1,0:T(8,128)(2,1)S(1)}, u32[]{:S(2)}, u32[]{:S(2)}) async-start(bf16[16,408,128]{2,1,0:T(8,128)(2,1)} %windows.1), calls=%async_computation.2 | async-start | bytes 3342336 | tf_op jit(solution)/shard_map/all_to_all | solution.py:545
  139.7 2.0 %slice_bitcast_fusion.turn_ref = bf16[1200,512]{1,0:T(8,128)(2,1)S(1)} fusion(bf16[1712,1200]{0,1:T(8,128)(2,1)} %param.9), kind=kLoop, calls=%fused_computation.2 | loop fusion | bytes 2457600 | tf_op jit(solution)/shard_map/transpose | solution.py:550
  141.6 10.7 %fusion.base_ref = f32[1200,1792]{1,0:T(8,128)} fusion(bf16[1200,1792]{1,0:T(8,128)(2,1)} %sub_ref.3, bf16[1712,1200]{0,1:T(8,128)(2,1)} %param.9), kind=kOutput, calls=%fused_computation | convolution fusion | flops 5160960000 | bytes 15974400 | tf_op jit(solution)/shard_map/dot_general | solution.py:549
  152.3 11.9 %all-to-all-done.2.got_ref = bf16[16,408,128]{2,1,0:T(8,128)(2,1)S(1)} async-done(((bf16[16,408,128]{2,1,0:T(8,128)(2,1)}), bf16[16,408,128]{2,1,0:T(8,128)(2,1)S(1)}, u32[]{:S(2)}, u32[]{:S(2)}) %all-to-all-start.2) | async-done | bytes 1671200 | tf_op jit(solution)/shard_map/all_to_all | solution.py:545
  164.2 0.2 total.1.a_ref
  164.4 0.9 collective-permute-start.9
  165.3 3.8 %collective-permute-start.10 = (bf16[408,128]{1,0:T(8,128)(2,1)S(1)}, bf16[408,128]{1,0:T(8,128)(2,1)S(1)}, u32[]{:S(2)}, u32[]{:S(2)}) collective-permute-start(bf16[408,128]{1,0:T(8,128)(2,1)S(1)} %total.1.a_ref), channel_id=1, source_target_pairs={{0,64},{32,96},{64,0},{96,32},{1,65},{33,97},{65,1},{97,33},{2,66}... | collective-permute-start | bytes 313352 | tf_op jit(solution)/shard_map/ppermute | solution.py:567
  169.1 1.0 collective-permute-start.11
  170.1 0.2 collective-permute-done.9.b_ref
  170.4 2.6 %collective-permute-done.10.c_ref = bf16[408,128]{1,0:T(8,128)(2,1)S(1)} collective-permute-done((bf16[408,128]{1,0:T(8,128)(2,1)S(1)}, bf16[408,128]{1,0:T(8,128)(2,1)S(1)}, u32[]{:S(2)}, u32[]{:S(2)}) %collective-permute-start.10) | collective-permute-done | bytes 104480 | tf_op jit(solution)/shard_map/ppermute | solution.py:567
  172.9 0.9 collective-permute-done.11.d_ref
  174.0 1.3 collective-permute-done.12.got_ref
  175.3 1.7 finish.1
  177.0 3.7 %all-to-all-start.3 = ((bf16[16,128,128]{2,1,0:T(8,128)(2,1)}), bf16[16,128,128]{2,1,0:T(8,128)(2,1)S(1)}, u32[]{:S(2)}, u32[]{:S(2)}) async-start(bf16[16,128,128]{2,1,0:T(8,128)(2,1)} %get-tuple-element.39), calls=%async_computation.3 | async-start | bytes 1048576 | tf_op jit(solution)/shard_map/all_to_all | solution.py:577
  180.8 3.4 %copy-done.2 = f32[1200,1792]{1,0:T(8,128)S(1)} copy-done((f32[1200,1792]{1,0:T(8,128)S(1)}, f32[1200,1792]{1,0:T(8,128)}, u32[]{:S(2)}) %copy-start.2) | copy-done | bytes 8601624
  184.3 1.5 copy-done.5
  185.8 8.4 %rotate.1 = bf16[1200,1792]{1,0:T(8,128)(2,1)} custom-call(f32[8,128]{1,0:T(8,128)S(1)} %get-tuple-element.41.scale_ref, f32[1200,1792]{1,0:T(8,128)S(1)} %copy-done.2, bf16[1200,512]{1,0:T(8,128)(2,1)S(1)} %slice_bitcast_fusion.turn_ref, bf16[2,256,1792]{2,1,0:T(8,128)(2,1)S(1)} %copy-done.5), custom_call_target="tpu_custom_call" | custom-call | tf_op jit(solution)/shard_map/rotate/pallas_call | solution.py:589
  194.2 2.1 %assemble.1 = f32[107,1712]{1,0:T(8,128)} custom-call(s32[3]{0:T(128)S(1)} %pad_add_fusion.1.at_ref, bf16[16,128,128]{2,1,0:T(8,128)(2,1)S(1)} %all-to-all-done.3.back_ref, f32[128,512]{1,0:T(8,128)S(1)} %get-tuple-element.40.rows_ref, f32[8,128]{1,0:T(8,128)S(1)} %get-tuple-element.41.scale_ref, bf16[4,152,128]{2,1,0:T(8,128)(2,1)S(1)} %get-tuple-element.42.own_ref, ...), custom_call_target="tpu_custom_call" | custom-call | tf_op jit(solution)/shard_map/assemble/pallas_call | solution.py:578
  (29 shorter events, 0.9 us)
Async XLA Ops:
  1.5 4.4 %collective-permute-start.1 = (s32[14]{0:T(128)S(1)}, s32[14]{0:T(128)S(1)}, u32[]{:S(2)}, u32[]{:S(2)}) collective-permute-start(s32[14]{0:T(128)S(1)} %fusion.2), channel_id=1, source_target_pairs={{16,0},{32,16},{48,32},{64,48},{80,64},{96,80},{112,96},{17,1},{33... | collective-permute-start | bytes 176 | tf_op jit(solution)/shard_map/ppermute | solution.py:472
  2.8 3.8 %collective-permute-start = (s32[14]{0:T(128)S(1)}, s32[14]{0:T(128)S(1)}, u32[]{:S(2)}, u32[]{:S(2)}) collective-permute-start(s32[14]{0:T(128)S(1)} %fusion.2), channel_id=1, source_target_pairs={{0,16},{16,32},{32,48},{48,64},{64,80},{80,96},{96,112},{1,17},{17... | collective-permute-start | bytes 176 | tf_op jit(solution)/shard_map/ppermute | solution.py:472
  22.6 1.4 copy-start.6
  24.0 0.7 copy-start.7
  42.3 3.0 %collective-permute-start.2 = (bf16[4,32,1792]{2,1,0:T(8,128)(2,1)S(1)}, bf16[4,32,1792]{2,1,0:T(8,128)(2,1)S(1)}, u32[]{:S(2)}, u32[]{:S(2)}) collective-permute-start(bf16[4,32,1792]{2,1,0:T(8,128)(2,1)S(1)} %get-tuple-element.25), channel_id=1, source_target_pairs={{0,16},{16,32},{32,48},{48,64},{64,80},{80,96},{96,112},{1,17},{17... | collective-permute-start | bytes 1376264 | tf_op jit(solution)/shard_map/ppermute | solution.py:487
  43.9 6.8 %collective-permute-start.3 = (bf16[4,32,1792]{2,1,0:T(8,128)(2,1)S(1)}, bf16[4,32,1792]{2,1,0:T(8,128)(2,1)S(1)}, u32[]{:S(2)}, u32[]{:S(2)}) collective-permute-start(bf16[4,32,1792]{2,1,0:T(8,128)(2,1)S(1)} %get-tuple-element.26), channel_id=1, source_target_pairs={{16,0},{32,16},{48,32},{64,48},{80,64},{96,80},{112,96},{17,1},{33... | collective-permute-start | bytes 1376264 | tf_op jit(solution)/shard_map/ppermute | solution.py:487
  51.5 1.2 copy-start.3
  52.7 25.9 %all-to-all-start.1 = ((bf16[16,32,1792]{2,1,0:T(8,128)(2,1)}), bf16[16,32,1792]{2,1,0:T(8,128)(2,1)S(1)}, u32[]{:S(2)}, u32[]{:S(2)}) async-start(bf16[16,32,1792]{2,1,0:T(8,128)(2,1)} %copy-done.3), calls=%async_computation.1 | async-start | bytes 3670016 | tf_op jit(solution)/shard_map/all_to_all | solution.py:488
  56.5 2.2 %copy-start = (bf16[1200,1792]{1,0:T(8,128)(2,1)S(1)}, bf16[1200,1792]{1,0:T(8,128)(2,1)}, u32[]{:S(2)}) copy-start(bf16[1200,1792]{1,0:T(8,128)(2,1)} %sub_ref.3) | copy-start | bytes 12902404
  65.5 28.7 %collective-permute-start.5 = (bf16[704,1200]{1,0:T(8,128)(2,1)}, bf16[704,1200]{1,0:T(8,128)(2,1)}, u32[]{:S(2)}, u32[]{:S(2)}) collective-permute-start(bf16[704,1200]{1,0:T(8,128)(2,1)} %basis_other.1), channel_id=1, source_target_pairs={{0,16},{16,0},{1,17},{17,1},{2,18},{18,2},{3,19},{19,3},{4,20},{20... | collective-permute-start | bytes 5068808 | tf_op jit(solution)/shard_map/ppermute | solution.py:501
  78.6 2.2 %copy-start.1 = (bf16[1200,1792]{1,0:T(8,128)(2,1)S(1)}, bf16[1200,1792]{1,0:T(8,128)(2,1)}, u32[]{:S(2)}) copy-start(bf16[1200,1792]{1,0:T(8,128)(2,1)} %sub_ref.3) | copy-start | bytes 12902404
  87.7 1.2 copy-start.4
  88.9 44.2 %collective-permute-start.4 = (bf16[1712,256]{1,0:T(8,128)(2,1)S(1)}, bf16[1712,256]{1,0:T(8,128)(2,1)S(1)}, u32[]{:S(2)}, u32[]{:S(2)}) collective-permute-start(bf16[1712,256]{1,0:T(8,128)(2,1)S(1)} %get-tuple-element.29), channel_id=1, source_target_pairs={{0,16},{16,0},{1,17},{17,1},{2,18},{18,2},{3,19},{19,3},{4,20},{20... | collective-permute-start | bytes 2629640 | tf_op jit(solution)/shard_map/ppermute | solution.py:544
  102.5 18.3 %collective-permute-start.6 = (bf16[176,1200]{1,0:T(8,128)(2,1)S(1)}, bf16[176,1200]{1,0:T(8,128)(2,1)S(1)}, u32[]{:S(2)}, u32[]{:S(2)}) collective-permute-start(bf16[176,1200]{1,0:T(8,128)(2,1)S(1)} %get-tuple-element.33), channel_id=1, source_target_pairs={{0,32},{32,64},{64,96},{96,0},{1,33},{33,65},{65,97},{97,1},{2,34}... | collective-permute-start | bytes 1267208 | tf_op jit(solution)/shard_map/ppermute | solution.py:511
  110.1 21.6 %collective-permute-start.7 = (bf16[176,1200]{1,0:T(8,128)(2,1)S(1)}, bf16[176,1200]{1,0:T(8,128)(2,1)S(1)}, u32[]{:S(2)}, u32[]{:S(2)}) collective-permute-start(bf16[176,1200]{1,0:T(8,128)(2,1)S(1)} %get-tuple-element.34), channel_id=1, source_target_pairs={{0,64},{32,96},{64,0},{96,32},{1,65},{33,97},{65,1},{97,33},{2,66}... | collective-permute-start | bytes 1267208 | tf_op jit(solution)/shard_map/ppermute | solution.py:511
  111.8 19.9 %collective-permute-start.8 = (bf16[176,1200]{1,0:T(8,128)(2,1)S(1)}, bf16[176,1200]{1,0:T(8,128)(2,1)S(1)}, u32[]{:S(2)}, u32[]{:S(2)}) collective-permute-start(bf16[176,1200]{1,0:T(8,128)(2,1)S(1)} %get-tuple-element.35), channel_id=1, source_target_pairs={{0,96},{32,0},{64,32},{96,64},{1,97},{33,1},{65,33},{97,65},{2,98}... | collective-permute-start | bytes 1267208 | tf_op jit(solution)/shard_map/ppermute | solution.py:511
  135.1 29.0 %all-to-all-start.2 = ((bf16[16,408,128]{2,1,0:T(8,128)(2,1)}), bf16[16,408,128]{2,1,0:T(8,128)(2,1)S(1)}, u32[]{:S(2)}, u32[]{:S(2)}) async-start(bf16[16,408,128]{2,1,0:T(8,128)(2,1)} %windows.1), calls=%async_computation.2 | async-start | bytes 3342336 | tf_op jit(solution)/shard_map/all_to_all | solution.py:545
  164.4 6.0 %collective-permute-start.9 = (bf16[408,128]{1,0:T(8,128)(2,1)S(1)}, bf16[408,128]{1,0:T(8,128)(2,1)S(1)}, u32[]{:S(2)}, u32[]{:S(2)}) collective-permute-start(bf16[408,128]{1,0:T(8,128)(2,1)S(1)} %total.1.a_ref), channel_id=1, source_target_pairs={{0,32},{32,64},{64,96},{96,0},{1,33},{33,65},{65,97},{97,1},{2,34}... | collective-permute-start | bytes 313352 | tf_op jit(solution)/shard_map/ppermute | solution.py:567
  165.3 7.6 %collective-permute-start.10 = (bf16[408,128]{1,0:T(8,128)(2,1)S(1)}, bf16[408,128]{1,0:T(8,128)(2,1)S(1)}, u32[]{:S(2)}, u32[]{:S(2)}) collective-permute-start(bf16[408,128]{1,0:T(8,128)(2,1)S(1)} %total.1.a_ref), channel_id=1, source_target_pairs={{0,64},{32,96},{64,0},{96,32},{1,65},{33,97},{65,1},{97,33},{2,66}... | collective-permute-start | bytes 313352 | tf_op jit(solution)/shard_map/ppermute | solution.py:567
  169.1 4.7 %collective-permute-start.11 = (bf16[408,128]{1,0:T(8,128)(2,1)S(1)}, bf16[408,128]{1,0:T(8,128)(2,1)S(1)}, u32[]{:S(2)}, u32[]{:S(2)}) collective-permute-start(bf16[408,128]{1,0:T(8,128)(2,1)S(1)} %total.1.a_ref), channel_id=1, source_target_pairs={{0,96},{32,0},{64,32},{96,64},{1,97},{33,1},{65,33},{97,65},{2,98}... | collective-permute-start | bytes 313352 | tf_op jit(solution)/shard_map/ppermute | solution.py:567
  173.9 1.4 collective-permute-start.12
  177.0 17.2 %all-to-all-start.3 = ((bf16[16,128,128]{2,1,0:T(8,128)(2,1)}), bf16[16,128,128]{2,1,0:T(8,128)(2,1)S(1)}, u32[]{:S(2)}, u32[]{:S(2)}) async-start(bf16[16,128,128]{2,1,0:T(8,128)(2,1)} %get-tuple-element.39), calls=%async_computation.3 | async-start | bytes 1048576 | tf_op jit(solution)/shard_map/all_to_all | solution.py:577
  180.7 13.5 %collective-permute-start.13 = (bf16[4,152,128]{2,1,0:T(8,128)(2,1)S(1)}, bf16[4,152,128]{2,1,0:T(8,128)(2,1)S(1)}, u32[]{:S(2)}, u32[]{:S(2)}) collective-permute-start(bf16[4,152,128]{2,1,0:T(8,128)(2,1)S(1)} %get-tuple-element.42.own_ref), channel_id=1, source_target_pairs={{0,16},{16,0},{1,17},{17,1},{2,18},{18,2},{3,19},{19,3},{4,20},{20... | collective-permute-start | bytes 466952 | tf_op jit(solution)/shard_map/ppermute | solution.py:586
  180.8 3.4 %copy-start.2 = (f32[1200,1792]{1,0:T(8,128)S(1)}, f32[1200,1792]{1,0:T(8,128)}, u32[]{:S(2)}) copy-start(f32[1200,1792]{1,0:T(8,128)} %fusion.base_ref) | copy-start | bytes 25804804
  184.3 1.5 copy-start.5

commit v4 on v3

--- a/solution.py
+++ b/solution.py
@@ -22,6 +22,7 @@
 PART = 150
 WIDE = 176
 SHARE = 152
+BIG = 56
 LEAD = 384
 BLOCK = 256
 PHASES = 3
@@ -64,7 +65,7 @@
     return table
 
 
-def smooth_kernel(depth, own_ref, near_ref, tab_ref, mat_ref, raw_ref, all_ref, rim_ref, up_ref, down_ref, pad, planar, mid_ref, sems, mid_sem):
+def smooth_kernel(depth, own_ref, near_ref, tab_ref, taps_ref, raw_ref, all_ref, rim_ref, up_ref, down_ref, pad, planar, mid_ref, mat_ref, sems, mid_sem, mat_sem):
     frames = raw_ref.shape[1]
     extent = raw_ref.shape[2]
     step = PHASES * BLOCK
@@ -78,11 +79,14 @@
             sems.at[i],
         )
 
+    plan = pltpu.make_async_copy(taps_ref, mat_ref, mat_sem)
+    plan.start()
     for i in range(steps):
         fetch(i).start()
     edge = jnp.zeros((depth, frames, LEAD), pad.dtype)
     pad[:, :, :LEAD] = edge
     pad[:, :, LEAD + extent :] = edge
+    plan.wait()
     fetch(0).wait()
 
     def block(i, carry):
@@ -157,16 +161,18 @@
             jax.ShapeDtypeStruct(quarter, jnp.bfloat16),
             jax.ShapeDtypeStruct(quarter, jnp.bfloat16),
         ],
-        in_specs=[smem, smem, smem, vmem, pl.BlockSpec(memory_space=pl.ANY)],
+        in_specs=[smem, smem, smem, pl.BlockSpec(memory_space=pltpu.HBM), pl.BlockSpec(memory_space=pltpu.HBM)],
         out_specs=[pl.BlockSpec(memory_space=pltpu.HBM), vmem, vmem, vmem],
         scratch_shapes=[
             pltpu.VMEM((depth, frames, extent + 2 * LEAD), jnp.bfloat16),
             pltpu.VMEM((depth, frames, extent), jnp.float32),
             pltpu.VMEM(half, jnp.bfloat16),
+            pltpu.VMEM((PHASES, LEAD + BLOCK + LEAD, BLOCK), jnp.bfloat16),
             pltpu.SemaphoreType.DMA((extent // (PHASES * BLOCK),)),
             pltpu.SemaphoreType.DMA,
+            pltpu.SemaphoreType.DMA,
         ],
-        compiler_params=pltpu.CompilerParams(vmem_limit_bytes=48 * 1024 * 1024),
+        compiler_params=pltpu.CompilerParams(vmem_limit_bytes=59 * 1024 * 1024),
         name="smooth",
     )(own, near, jnp.asarray(depth_table()), jnp.asarray(plane_matrix()).astype(jnp.bfloat16), raw)
 
@@ -198,8 +204,8 @@
     return pl.BlockSpec(memory_space=pltpu.HBM)
 
 
-PIECE = 400
-PIECES = K // PIECE
+PIECES = ((0, 512), (512, 1024), (1024, K))
+HALF = WIDE // 2
 
 
 def basis_copies(x, which, sub_ref, left, right, sems):
@@ -209,8 +215,8 @@
         made.append(
             pltpu.make_async_copy(sub_ref.at[pl.ds(start, WIDE)], left.at[k * WIDE : (k + 1) * WIDE], sems.at[k])
         )
-    for i in range(PIECES):
-        rows = slice(i * PIECE, (i + 1) * PIECE)
+    for i, (lo, hi) in enumerate(PIECES):
+        rows = slice(lo, hi)
         made.append(pltpu.make_async_copy(sub_ref.at[rows], right.at[rows], sems.at[4 + i]))
     for copy in made:
         copy.start()
@@ -219,26 +225,39 @@
 
 def basis_other_kernel(at_ref, sub_ref, out_ref, left, right, sems):
     made = basis_copies(at_ref[0], 1 - at_ref[1], sub_ref, left, right, sems)
-    for copy in made:
+    for copy in made[:4]:
         copy.wait()
-    out_ref[...] = lax.dot_general(left[...], right[...], NT, preferred_element_type=jnp.float32).astype(out_ref.dtype)
-
-
-def basis_own_kernel(at_ref, sub_ref, got_ref, *refs):
-    left, right, sems = refs[-3:]
+    for i, (lo, hi) in enumerate(PIECES):
+        made[4 + i].wait()
+        out_ref[:, lo:hi] = lax.dot_general(
+            left[...], right[lo:hi, :], NT, preferred_element_type=jnp.float32
+        ).astype(out_ref.dtype)
+
+
+def basis_own_kernel(at_ref, sub_ref, got_ref, own_ref, next_ref, far_ref, back_ref, left, right, sems):
     made = basis_copies(at_ref[0], at_ref[1], sub_ref, left, right, sems)
-    for copy in made:
+    for copy in made[:4]:
         copy.wait()
-    for k in range(4):
-        rows = slice(k * WIDE, (k + 1) * WIDE)
-        part = lax.dot_general(left[rows, :], right[...], NT, preferred_element_type=jnp.float32)
-        refs[k][...] = (part + got_ref[rows, :].astype(jnp.float32)).astype(refs[k].dtype)
-
-
-def basis_rows_kernel(at_ref, a_ref, b_ref, c_ref, d_ref, out_ref, flat):
+    for i, (lo, hi) in enumerate(PIECES):
+        made[4 + i].wait()
+        part = lax.dot_general(left[...], right[lo:hi, :], NT, preferred_element_type=jnp.float32)
+        part = (part + got_ref[:, lo:hi].astype(jnp.float32)).astype(own_ref.dtype)
+        own_ref[:, lo:hi] = part[:WIDE]
+        next_ref[:, lo:hi] = part[WIDE : 2 * WIDE]
+        far_ref[:, :, lo:hi] = part[2 * WIDE : 3 * WIDE].reshape(2, HALF, hi - lo)
+        back_ref[:, lo:hi] = part[3 * WIDE :]
+
+
+def basis_relay_kernel(next_ref, back_ref, low_ref, high_ref, next_out, back_out):
+    next_out[:HALF] = (next_ref[:HALF].astype(jnp.float32) + low_ref[...].astype(jnp.float32)).astype(next_out.dtype)
+    next_out[HALF:] = next_ref[HALF:]
+    back_out[:HALF] = back_ref[:HALF]
+    back_out[HALF:] = (back_ref[HALF:].astype(jnp.float32) + high_ref[...].astype(jnp.float32)).astype(back_out.dtype)
+
+
+def basis_rows_kernel(at_ref, a_ref, b_ref, c_ref, out_ref, flat):
     part = at_ref[0] * 2 + at_ref[1]
-    total = a_ref[...].astype(jnp.float32) + b_ref[...].astype(jnp.float32)
-    total = total + c_ref[...].astype(jnp.float32) + d_ref[...].astype(jnp.float32)
+    total = a_ref[...].astype(jnp.float32) + b_ref[...].astype(jnp.float32) + c_ref[...].astype(jnp.float32)
     flat[:, K // RUN * RUN :] = jnp.zeros((flat.shape[0], flat.shape[1] - K // RUN * RUN), jnp.float32)
     flat[:, :K] = total
     shift = (WIDE - (part * PART - part_start(part))) % WIDE
@@ -342,11 +361,12 @@
             ].astype(out_ref.dtype)
 
 
-def total_kernel(got_ref, out_ref):
+def total_kernel(got_ref, out_ref, share_ref):
     total = got_ref[0].astype(jnp.float32)
     for g in range(1, GRP):
         total = total + got_ref[g].astype(jnp.float32)
-    out_ref[...] = total.astype(out_ref.dtype)
+    out_ref[...] = total[: 2 * TALL].astype(out_ref.dtype)
+    share_ref[...] = total[2 * TALL :].astype(share_ref.dtype)
 
     def put(rows, value):
         out_ref[rows, :] = value
@@ -354,14 +374,9 @@
     write_power(total[WIN:TALL] + total[TALL + WIN : 2 * TALL], put)
 
 
-def slab_kernel(a_ref, b_ref, c_ref, d_ref, sum_ref, parts_ref):
-    refs = (a_ref, b_ref, c_ref, d_ref)
-    total = refs[0][: 2 * TALL].astype(jnp.float32)
-    for ref in refs[1:]:
-        total = total + ref[: 2 * TALL].astype(jnp.float32)
-    sum_ref[...] = total
-    for k in range(4):
-        parts_ref[k] = refs[k][2 * TALL :]
+def slab_kernel(a_ref, b_ref, c_ref, d_ref, sum_ref):
+    total = a_ref[...].astype(jnp.float32) + b_ref[...].astype(jnp.float32)
+    sum_ref[...] = total + c_ref[...].astype(jnp.float32) + d_ref[...].astype(jnp.float32)
 
 
 def finish_kernel(count, at_ref, own_ref, got_ref, rows_ref, scale_ref, turned_ref):
@@ -385,21 +400,22 @@
         turned_ref[g] = lax.dot_general(pick, narrow, NT, preferred_element_type=jnp.float32).astype(turned_ref.dtype)
 
 
-def assemble_kernel(masked, at_ref, back_ref, rows_ref, scale_ref, own_ref, got_ref, out_ref, basis, cross):
+def assemble_kernel(masked, at_ref, back_ref, rows_ref, scale_ref, zero_ref, one_ref, two_ref, three_ref, out_ref, basis, cross):
     x, core, grp = at_ref[0], at_ref[1], at_ref[2]
     first = grp * ROWS
+    shares = (zero_ref, one_ref, two_ref, three_ref)
     basis[...] = jnp.zeros_like(basis)
     cross[...] = jnp.zeros_like(cross)
     line = lax.broadcasted_iota(jnp.int32, (SHARE, 384), 0)
     lane = lax.broadcasted_iota(jnp.int32, (SHARE, 384), 1)
     for k in range(4):
-        for ref, which in ((own_ref, core), (got_ref, 1 - core)):
+        for c, which in ((0, core), (1, 1 - core)):
             part = (x - k + 4) % 4 * 2 + which
             begin = part * PART // RUN * RUN
             put = jnp.where((line + (part * PART - begin) == lane) & (line < PART), 1.0, 0.0).astype(jnp.bfloat16)
             cols = pl.ds(pl.multiple_of(begin, RUN), 384)
             basis[:, cols] += lax.dot_general(
-                ref[k], put, (((0,), (0,)), ((), ())), preferred_element_type=jnp.float32
+                shares[k][c], put, (((0,), (0,)), ((), ())), preferred_element_type=jnp.float32
             )
     line = lax.broadcasted_iota(jnp.int32, (TALL, 256), 0)
     lane = lax.broadcasted_iota(jnp.int32, (TALL, 256), 1)
@@ -475,6 +491,24 @@
     near = jnp.concatenate([every[: GRP // 4, 2].reshape(-1), every[3 * GRP // 4 :, 1].reshape(-1)])
 
     middles, rim, to_up, to_down = smooth(own, near, jnp.transpose(raw_frames, (1, 0, 2)))
+    at_ss, _ = lax.optimization_barrier((at, to_down))
+    held = [
+        pltpu.VMEM((4 * WIDE, per_device), bf16),
+        pltpu.VMEM((K, per_device), bf16),
+        pltpu.SemaphoreType.DMA((4 + len(PIECES),)),
+    ]
+    other_ss = pl.pallas_call(
+        basis_other_kernel,
+        out_shape=like((4 * WIDE, K), bf16),
+        in_specs=[smem(), hbm()],
+        out_specs=vmem(1)[0],
+        scratch_shapes=held,
+        compiler_params=params(BIG),
+        name="basis_other",
+    )(at_ss, subspace)
+    from_low, from_high, other_ss = lax.optimization_barrier(
+        (lax.ppermute(to_up, slab, up), lax.ppermute(to_down, slab, down), other_ss)
+    )
     placed = pl.pallas_call(
         rim_kernel,
         out_shape=like(middles.shape, bf16),
@@ -484,40 +518,38 @@
         input_output_aliases={3: 0},
         compiler_params=params(16),
         name="rim",
-    )(rim, lax.ppermute(to_up, slab, up), lax.ppermute(to_down, slab, down), middles)
+    )(rim, from_low, from_high, middles)
     regrouped = lax.all_to_all(placed, "grp", 0, 0, tiled=True)
 
-    at_ss, _ = lax.optimization_barrier((at, to_down))
-    held = [pltpu.VMEM((4 * WIDE, per_device), bf16), pltpu.VMEM((K, per_device), bf16), pltpu.SemaphoreType.DMA((4 + PIECES,))]
-    other_ss = pl.pallas_call(
-        basis_other_kernel,
-        out_shape=like((4 * WIDE, K), bf16),
-        in_specs=[smem(), hbm()],
-        out_specs=vmem(1)[0],
-        scratch_shapes=held,
-        compiler_params=params(24),
-        name="basis_other",
-    )(at_ss, subspace)
     got_ss = lax.ppermute(other_ss, "core", swap)
-    parts = pl.pallas_call(
+    own_ss, next_ss, far_ss, back_ss = pl.pallas_call(
         basis_own_kernel,
-        out_shape=[like((WIDE, K), bf16)] * 4,
+        out_shape=[like((WIDE, K), bf16), like((WIDE, K), bf16), like((2, HALF, K), bf16), like((WIDE, K), bf16)],
         in_specs=[smem(), hbm(), *vmem(1)],
         out_specs=vmem(4),
         scratch_shapes=held,
-        compiler_params=params(24),
+        compiler_params=params(BIG),
         name="basis_own",
     )(at_ss, subspace, got_ss)
-    parts = [parts[0]] + [lax.ppermute(parts[k], "x", turns[k]) for k in range(1, 4)]
+    ahead, behind = turns[1], turns[3]
+    next_ss, back_ss = pl.pallas_call(
+        basis_relay_kernel,
+        out_shape=[like((WIDE, K), bf16)] * 2,
+        in_specs=vmem(4),
+        out_specs=vmem(2),
+        compiler_params=params(16),
+        name="basis_relay",
+    )(next_ss, back_ss, lax.ppermute(far_ss[0], "x", ahead), lax.ppermute(far_ss[1], "x", behind))
+    regrouped, next_ss, back_ss = lax.optimization_barrier((regrouped, next_ss, back_ss))
     by_row = pl.pallas_call(
         basis_rows_kernel,
         out_shape=like((GRP, SHARE, RUN), bf16),
-        in_specs=[smem(), *vmem(4)],
+        in_specs=[smem(), *vmem(3)],
         out_specs=vmem(1)[0],
         scratch_shapes=[pltpu.VMEM((WIDE, 1408), f32)],
         compiler_params=params(16),
         name="basis_rows",
-    )(at, *parts)
+    )(at, own_ss, lax.ppermute(next_ss, "x", ahead), lax.ppermute(back_ss, "x", behind))
 
     centered, other_c, own_c, power = pl.pallas_call(
         columns_kernel,
@@ -530,7 +562,7 @@
             pltpu.VMEM((KX, SUBJ), f32),
             pltpu.SemaphoreType.DMA((3,)),
         ],
-        compiler_params=params(24),
+        compiler_params=params(47),
         name="columns",
     )(at, regrouped, subspace)
     sent = pl.pallas_call(
@@ -549,22 +581,23 @@
     from_basis = lax.dot_general(rotation_b[:K], subspace, contract, preferred_element_type=f32)
     summed, from_basis, turn = lax.optimization_barrier((summed, from_basis, rotation_b[K:].T))
 
-    total = pl.pallas_call(
+    total, share = pl.pallas_call(
         total_kernel,
-        out_shape=like((2 * TALL + SHARE, RUN), bf16),
+        out_shape=[like((2 * TALL, RUN), bf16), like((SHARE, RUN), bf16)],
         in_specs=vmem(1),
-        out_specs=vmem(1)[0],
+        out_specs=vmem(2),
         compiler_params=params(16),
         name="total",
     )(summed)
-    sum_c, parts_ss = pl.pallas_call(
+    sum_c = pl.pallas_call(
         slab_kernel,
-        out_shape=[like((2 * TALL, RUN), f32), like((4, SHARE, RUN), bf16)],
+        out_shape=like((2 * TALL, RUN), f32),
         in_specs=vmem(4),
-        out_specs=vmem(2),
+        out_specs=vmem(1)[0],
         compiler_params=params(16),
         name="slab",
     )(total, *[lax.ppermute(total, "x", turns[k]) for k in range(1, 4)])
+    share = jnp.stack([share, lax.ppermute(share, "core", swap)])
     rows_c, scales, turned = pl.pallas_call(
         functools.partial(finish_kernel, float(masked * SUBJ)),
         out_shape=[like((TALL, 2 * SUBJ), f32), like((8, RUN), f32), like((GRP, TALL, TALL), bf16)],
@@ -575,15 +608,16 @@
     )(at, sum_c, lax.ppermute(sum_c, "core", swap))
 
     back = lax.all_to_all(turned, "grp", 0, 0, tiled=True)
+    share, _ = lax.optimization_barrier((share, turned))
     gram_rows = pl.pallas_call(
         functools.partial(assemble_kernel, float(masked)),
         out_shape=like((ROWS, KX), f32),
-        in_specs=[smem(), *vmem(5)],
+        in_specs=[smem(), *vmem(7)],
         out_specs=vmem(1)[0],
         scratch_shapes=[pltpu.VMEM((TALL, 1408), f32), pltpu.VMEM((TALL, 1408), f32)],
         compiler_params=params(16),
         name="assemble",
-    )(at, back, rows_c, scales, parts_ss, lax.ppermute(parts_ss, "core", swap))
+    )(at, back, rows_c, scales, share, *[lax.ppermute(share, "x", turns[k]) for k in range(1, 4)])
 
     tile = 256
     new_subspace = pl.pallas_call(
@@ -598,7 +632,7 @@
         ],
         out_specs=pl.BlockSpec((K, tile), lambda i: (0, i)),
         scratch_shapes=[pltpu.VMEM((2, K, tile), f32), pltpu.SemaphoreType.DMA((2,))],
-        compiler_params=params(24),
+        compiler_params=params(BIG),
         name="rotate",
     )(scales, from_basis, turn, centered)
     return (gram_rows, new_subspace)

time: 198 us -> 188 us (0.949)
  Pallas kernels: 56.3 us -> 67.6 us
  starting transfers between devices: 48.7 us -> 40.1 us
  waiting for transfers between devices: 47.1 us -> 40 us
  local copies, waits for them, and re-layouts: 17 us -> 10.9 us
    unnamed x16 -> x20, local copies, waits for them, and re-layouts: 13.9 us -> 5.13 us
    ppermute x1, waiting for transfers between devices: 5.41 us -> 0.01 us  [body(): lax.ppermute(to_down, slab, down)]
    ppermute x1, starting transfers between devices: 5.28 us -> 0.01 us  [body(): lax.ppermute(other_c, 'core', swap)]
    pallas_call x1, Pallas kernels: 17.7 us -> 21.8 us  [smooth(): pl.pallas_call(functools.partial(smooth_kernel, depth), out_shape=[jax.Sh...]
    pallas_call x1, Pallas kernels: 6.78 us -> 9.37 us  [body(): pl.pallas_call(basis_other_kernel, out_shape=like((4 * WIDE, K), bf16), i...]
    pallas_call x3 -> x4, Pallas kernels: 8.57 us -> 11 us  [the longest x1 10.6 us: body(): pl.pallas_call(basis_own_kernel, out_shape=[like((WIDE, K), bf16), like((...]
    pallas_call x1, Pallas kernels: 8.38 us -> 10.6 us  [body(): pl.pallas_call(functools.partial(rotate_kernel, tile), out_shape=like((K,...]
    ppermute x4 -> x8, starting transfers between devices: 11.7 us -> 10.8 us  [the longest x3 4.21 us: body(): lax.ppermute(share, 'x', turns[k])]
  transfers between devices with their start and end apart: 17 -> 21, of which waited for: 11 -> 11; matrix products, arithmetic and copies ran while one was open for 6% -> 8% of each run, Pallas kernels for 16% -> 18%
where the time goes in v4:
time: 188 us; the launch traced here: 187 us
  Pallas kernels  67.6 us (36%)
  starting transfers between devices  40.1 us (21%)
  waiting for transfers between devices  40 us (21%)
  blocking collectives  15.6 us (8%)
  local copies, waits for them, and re-layouts  10.9 us (6%)
  matrix products  10.7 us (6%)
    pallas_call x1, Pallas kernels, smooth(): pl.pallas_call(functools.partial(smooth_kernel, depth), out_shape=[jax.Sh...  21.8 us
    all_to_all x1, blocking collectives, copies(): lax.all_to_all(jnp.broadcast_to(value[None], (count, *value.shape)), axis...  15.6 us
    all_to_all x1, waiting for transfers between devices, body(): summed = lax.all_to_all(sent, 'grp', 0, 0, tiled=True)  11.5 us
    ppermute x1, waiting for transfers between devices, body(): lax.ppermute(next_ss, 'x', ahead)  10.7 us
    dot_general x1, matrix products, body(): lax.dot_general(rotation_b[:K], subspace, contract, preferred_element_typ...  10.7 us
    pallas_call x1, Pallas kernels, body(): pl.pallas_call(basis_own_kernel, out_shape=[like((WIDE, K), bf16), like((...  10.6 us
    pallas_call x1, Pallas kernels, body(): pl.pallas_call(functools.partial(rotate_kernel, tile), out_shape=like((K,...  10.6 us
    pallas_call x1, Pallas kernels, body(): pl.pallas_call(basis_other_kernel, out_shape=like((4 * WIDE, K), bf16), i...  9.37 us
  transfers between devices with their start and end apart: 21, of which 11 were waited for; matrix products, arithmetic and copies ran while one was open for 8% of the time, Pallas kernels for 18%

profile of v4, /device:TPU:0, one launch (start us, length us, event | category | flops | bytes accessed | tf_op | source)
XLA Modules:
  0.0 187.0 jit_solution(3155690287066405736)
XLA Ops:
  0.6 0.8 slice_reduce_fusion.1
  1.5 1.3 collective-permute-start.1
  2.8 3.0 %collective-permute-start = (s32[14]{0:T(128)S(1)}, s32[14]{0:T(128)S(1)}, u32[]{:S(2)}, u32[]{:S(2)}) collective-permute-start(s32[14]{0:T(128)S(1)} %fusion.2), channel_id=1, source_target_pairs={{0,16},{16,32},{32,48},{48,64},{64,80},{80,96},{96,112},{1,17},{17... | collective-permute-start | bytes 176 | tf_op jit(solution)/shard_map/ppermute | solution.py:488
  5.8 0.8 collective-permute-done
  6.6 15.6 %all_to_all.20 = s32[16,3,14]{2,1,0:T(4,128)S(1)} all-to-all(s32[16,3,14]{2,1,0:T(4,128)S(1)} %broadcast_in_dim.2), channel_id=1, replica_groups=mesh['x'=4,'core'=2,'grp'=16] {'grp'}, dimensions={0} | all-to-all | bytes 5376 | tf_op jit(solution)/shard_map/all_to_all | solution.py:468
  22.2 0.7 reshape_squeeze.9.own_ref
  23.7 21.8 %smooth.1 = (bf16[16,32,1792]{2,1,0:T(8,128)(2,1)}, f32[8,32,1792]{2,1,0:T(8,128)}, bf16[4,32,1792]{2,1,0:T(8,128)(2,1)}, bf16[4,32,1792]{2,1,0:T(8,128)(2,1)}) custom-call(s32[224]{0:T(256)} %reshape_squeeze.9.own_ref, s32[112]{0:T(128)} %pad_add_fusion.2.near_ref, f32[64]{0:T(128)} %constant.39.clone.tab_ref, bf16[3,1024,256]{2,1,0:T(8,128)(2,1)} %constant.42.taps_ref, ...), custom_call_target="tpu_custom_call" | custom-call | tf_op jit(solution)/shard_map/smooth/pallas_call | solution.py:156
  45.4 1.7 collective-permute-start.2
  47.2 1.3 collective-permute-start.3
  48.5 0.6 pad_add_fusion.1.at_ref
  49.1 9.4 %basis_other.1 = bf16[704,1200]{1,0:T(8,128)(2,1)} custom-call(s32[3]{0:T(128)} %pad_add_fusion.1.at_ref, bf16[1200,1792]{1,0:T(8,128)(2,1)} %basis_ref.1), custom_call_target="tpu_custom_call" | custom-call | tf_op jit(solution)/shard_map/basis_other/pallas_call | solution.py:500
  58.5 4.9 %collective-permute-start.4 = (bf16[704,1200]{1,0:T(8,128)(2,1)}, bf16[704,1200]{1,0:T(8,128)(2,1)}, u32[]{:S(2)}, u32[]{:S(2)}) collective-permute-start(bf16[704,1200]{1,0:T(8,128)(2,1)} %basis_other.1), channel_id=1, source_target_pairs={{0,16},{16,0},{1,17},{17,1},{2,18},{18,2},{3,19},{19,3},{4,20},{20... | collective-permute-start | bytes 5068808 | tf_op jit(solution)/shard_map/ppermute | solution.py:524
  63.4 0.7 rim.1
  64.1 1.2 copy-done.1
  65.4 3.7 %all-to-all-start.1 = ((bf16[16,32,1792]{2,1,0:T(8,128)(2,1)}), bf16[16,32,1792]{2,1,0:T(8,128)(2,1)S(1)}, u32[]{:S(2)}, u32[]{:S(2)}) async-start(bf16[16,32,1792]{2,1,0:T(8,128)(2,1)} %copy-done.1), calls=%async_computation.1 | async-start | bytes 3670016 | tf_op jit(solution)/shard_map/all_to_all | solution.py:522
  69.1 10.6 %basis_own.1 = (bf16[176,1200]{1,0:T(8,128)(2,1)}, bf16[176,1200]{1,0:T(8,128)(2,1)}, bf16[2,88,1200]{2,1,0:T(8,128)(2,1)}, bf16[176,1200]{1,0:T(8,128)(2,1)}) custom-call(s32[3]{0:T(128)} %pad_add_fusion.1.at_ref, bf16[1200,1792]{1,0:T(8,128)(2,1)} %basis_ref.1, bf16[704,1200]{1,0:T(8,128)(2,1)} %collective-permute-done.4.got_ref), custom_call_target="tpu_custom_call" | custom-call | tf_op jit(solution)/shard_map/basis_own/pallas_call | solution.py:525
  79.7 1.1 slice_bitcast_fusion.1
  80.8 1.7 collective-permute-start.5
  82.5 1.6 collective-permute-start.6
  84.1 5.0 %collective-permute-done.5.low_ref = bf16[88,1200]{1,0:T(8,128)(2,1)S(1)} collective-permute-done((bf16[88,1200]{1,0:T(8,128)(2,1)S(1)}, bf16[88,1200]{1,0:T(8,128)(2,1)S(1)}, u32[]{:S(2)}, u32[]{:S(2)}) %collective-permute-start.5) | collective-permute-done | bytes 211232 | tf_op jit(solution)/shard_map/ppermute | solution.py:542
  89.1 1.0 copy-done.5
  90.1 1.0 copy-done.6
  91.2 5.9 %all-to-all-done.1.got_ref = bf16[16,32,1792]{2,1,0:T(8,128)(2,1)S(1)} async-done(((bf16[16,32,1792]{2,1,0:T(8,128)(2,1)}), bf16[16,32,1792]{2,1,0:T(8,128)(2,1)S(1)}, u32[]{:S(2)}, u32[]{:S(2)}) %all-to-all-start.1) | async-done | bytes 1835040 | tf_op jit(solution)/shard_map/all_to_all | solution.py:522
  97.2 6.9 %columns.1 = (bf16[2,256,1792]{2,1,0:T(8,128)(2,1)S(1)}, bf16[1712,256]{1,0:T(8,128)(2,1)S(1)}, f32[1712,256]{1,0:T(8,128)S(1)}, f32[8,128]{1,0:T(8,128)S(1)}) custom-call(s32[3]{0:T(128)S(1)} %copy-done.7, bf16[16,32,1792]{2,1,0:T(8,128)(2,1)S(1)} %all-to-all-done.1.got_ref, bf16[1200,1792]{1,0:T(8,128)(2,1)} %basis_ref.1), custom_call_target="tpu_custom_call" | custom-call | tf_op jit(solution)/shard_map/columns/pallas_call | solution.py:554
  104.1 1.3 copy-done.3
  105.4 1.6 collective-permute-start.8
  106.9 1.7 collective-permute-start.9
  108.6 10.7 %collective-permute-done.8.b_ref = bf16[176,1200]{1,0:T(8,128)(2,1)S(1)} collective-permute-done((bf16[176,1200]{1,0:T(8,128)(2,1)S(1)}, bf16[176,1200]{1,0:T(8,128)(2,1)S(1)}, u32[]{:S(2)}, u32[]{:S(2)}) %collective-permute-start.8) | collective-permute-done | bytes 422432 | tf_op jit(solution)/shard_map/ppermute | solution.py:552
  119.4 1.5 basis_rows.1.basis_ref
  120.9 1.9 %windows.1 = bf16[16,408,128]{2,1,0:T(8,128)(2,1)} custom-call(f32[1712,256]{1,0:T(8,128)S(1)} %get-tuple-element.47.own_ref, bf16[1712,256]{1,0:T(8,128)(2,1)S(1)} %collective-permute-done.7.got_ref, f32[8,128]{1,0:T(8,128)S(1)} %get-tuple-element.49.power_ref, bf16[16,152,128]{2,1,0:T(8,128)(2,1)S(1)} %basis_rows.1.basis_ref), custom_call_target="tpu_custom_call" | custom-call | tf_op jit(solution)/shard_map/windows/pallas_call | solution.py:568
  122.8 4.5 %all-to-all-start.2 = ((bf16[16,408,128]{2,1,0:T(8,128)(2,1)}), bf16[16,408,128]{2,1,0:T(8,128)(2,1)S(1)}, u32[]{:S(2)}, u32[]{:S(2)}) async-start(bf16[16,408,128]{2,1,0:T(8,128)(2,1)} %windows.1), calls=%async_computation.2 | async-start | bytes 3342336 | tf_op jit(solution)/shard_map/all_to_all | solution.py:577
  127.3 3.0 %slice_bitcast_fusion.turn_ref = bf16[1200,512]{1,0:T(8,128)(2,1)} fusion(bf16[1712,1200]{0,1:T(8,128)(2,1)} %param.9), kind=kLoop, calls=%fused_computation.2 | loop fusion | bytes 2457600 | tf_op jit(solution)/shard_map/transpose | solution.py:582
  130.3 10.7 %fusion.base_ref = f32[1200,1792]{1,0:T(8,128)} fusion(bf16[1200,1792]{1,0:T(8,128)(2,1)} %basis_ref.1, bf16[1712,1200]{0,1:T(8,128)(2,1)} %param.9), kind=kOutput, calls=%fused_computation | convolution fusion | flops 5160960000 | bytes 15974400 | tf_op jit(solution)/shard_map/dot_general | solution.py:581
  140.9 11.5 %all-to-all-done.2.got_ref = bf16[16,408,128]{2,1,0:T(8,128)(2,1)S(1)} async-done(((bf16[16,408,128]{2,1,0:T(8,128)(2,1)}), bf16[16,408,128]{2,1,0:T(8,128)(2,1)S(1)}, u32[]{:S(2)}, u32[]{:S(2)}) %all-to-all-start.2) | async-done | bytes 1671200 | tf_op jit(solution)/shard_map/all_to_all | solution.py:577
  152.7 0.7 collective-permute-start.10
  153.4 3.3 %collective-permute-start.11 = (bf16[256,128]{1,0:T(8,128)(2,1)S(1)}, bf16[256,128]{1,0:T(8,128)(2,1)S(1)}, u32[]{:S(2)}, u32[]{:S(2)}) collective-permute-start(bf16[256,128]{1,0:T(8,128)(2,1)S(1)} %get-tuple-element.55.a_ref), channel_id=1, source_target_pairs={{0,64},{32,96},{64,0},{96,32},{1,65},{33,97},{65,1},{97,33},{2,66}... | collective-permute-start | bytes 196616 | tf_op jit(solution)/shard_map/ppermute | solution.py:599
  156.7 0.9 collective-permute-start.12
  157.6 0.7 collective-permute-done.10.b_ref
  158.3 1.4 collective-permute-done.11.c_ref
  159.6 1.3 collective-permute-done.12.d_ref
  161.1 1.3 collective-permute-done.13.got_ref
  162.4 1.7 finish.1
  164.8 3.9 %all-to-all-start.3 = ((bf16[16,128,128]{2,1,0:T(8,128)(2,1)}), bf16[16,128,128]{2,1,0:T(8,128)(2,1)S(1)}, u32[]{:S(2)}, u32[]{:S(2)}) async-start(bf16[16,128,128]{2,1,0:T(8,128)(2,1)} %get-tuple-element.56), calls=%async_computation.3 | async-start | bytes 1048576 | tf_op jit(solution)/shard_map/all_to_all | solution.py:610
  168.8 1.2 collective-permute-done.14
  170.1 3.1 %collective-permute-start.16 = (bf16[2,152,128]{2,1,0:T(8,128)(2,1)S(1)}, bf16[2,152,128]{2,1,0:T(8,128)(2,1)S(1)}, u32[]{:S(2)}, u32[]{:S(2)}) collective-permute-start(bf16[2,152,128]{2,1,0:T(8,128)(2,1)S(1)} %pad_maximum_fusion.zero_ref), channel_id=1, source_target_pairs={{0,64},{32,96},{64,0},{96,32},{1,65},{33,97},{65,1},{97,33},{2,66}... | collective-permute-start | bytes 233480 | tf_op jit(solution)/shard_map/ppermute | solution.py:620
  173.3 0.9 collective-permute-start.17
  174.2 10.6 %rotate.1 = bf16[1200,1792]{1,0:T(8,128)(2,1)} custom-call(f32[8,128]{1,0:T(8,128)} %copy-done.8, f32[1200,1792]{1,0:T(8,128)} %fusion.base_ref, bf16[1200,512]{1,0:T(8,128)(2,1)} %slice_bitcast_fusion.turn_ref, bf16[2,256,1792]{2,1,0:T(8,128)(2,1)} %copy-done.3), custom_call_target="tpu_custom_call" | custom-call | tf_op jit(solution)/shard_map/rotate/pallas_call | solution.py:623
  184.8 2.1 %assemble.1 = f32[107,1712]{1,0:T(8,128)} custom-call(s32[3]{0:T(128)S(1)} %copy-done.7, bf16[16,128,128]{2,1,0:T(8,128)(2,1)S(1)} %all-to-all-done.3.back_ref, f32[128,512]{1,0:T(8,128)S(1)} %get-tuple-element.57.rows_ref, f32[8,128]{1,0:T(8,128)S(1)} %copy-done.9, bf16[2,152,128]{2,1,0:T(8,128)(2,1)S(1)} %pad_maximum_fusion.zero_ref, ...), custom_call_target="tpu_custom_call" | custom-call | tf_op jit(solution)/shard_map/assemble/pallas_call | solution.py:612
  (44 shorter events, 2.3 us)
Async XLA Ops:
  1.5 4.4 %collective-permute-start.1 = (s32[14]{0:T(128)S(1)}, s32[14]{0:T(128)S(1)}, u32[]{:S(2)}, u32[]{:S(2)}) collective-permute-start(s32[14]{0:T(128)S(1)} %fusion.2), channel_id=1, source_target_pairs={{16,0},{32,16},{48,32},{64,48},{80,64},{96,80},{112,96},{17,1},{33... | collective-permute-start | bytes 176 | tf_op jit(solution)/shard_map/ppermute | solution.py:488
  2.8 3.8 %collective-permute-start = (s32[14]{0:T(128)S(1)}, s32[14]{0:T(128)S(1)}, u32[]{:S(2)}, u32[]{:S(2)}) collective-permute-start(s32[14]{0:T(128)S(1)} %fusion.2), channel_id=1, source_target_pairs={{0,16},{16,32},{32,48},{48,64},{64,80},{80,96},{96,112},{1,17},{17... | collective-permute-start | bytes 176 | tf_op jit(solution)/shard_map/ppermute | solution.py:488
  45.4 18.0 %copy-start = (bf16[16,32,1792]{2,1,0:T(8,128)(2,1)S(1)}, bf16[16,32,1792]{2,1,0:T(8,128)(2,1)}, u32[]{:S(2)}) copy-start(bf16[16,32,1792]{2,1,0:T(8,128)(2,1)} %get-tuple-element.39.all_ref) | copy-start | bytes 5505028
  45.4 13.1 %collective-permute-start.2 = (bf16[4,32,1792]{2,1,0:T(8,128)(2,1)}, bf16[4,32,1792]{2,1,0:T(8,128)(2,1)S(1)}, u32[]{:S(2)}, u32[]{:S(2)}) collective-permute-start(bf16[4,32,1792]{2,1,0:T(8,128)(2,1)} %get-tuple-element.34), channel_id=1, source_target_pairs={{0,16},{16,32},{32,48},{48,64},{64,80},{80,96},{96,112},{1,17},{17... | collective-permute-start | bytes 1376264 | tf_op jit(solution)/shard_map/ppermute | solution.py:510
  47.2 11.3 %collective-permute-start.3 = (bf16[4,32,1792]{2,1,0:T(8,128)(2,1)}, bf16[4,32,1792]{2,1,0:T(8,128)(2,1)S(1)}, u32[]{:S(2)}, u32[]{:S(2)}) collective-permute-start(bf16[4,32,1792]{2,1,0:T(8,128)(2,1)} %get-tuple-element.35), channel_id=1, source_target_pairs={{16,0},{32,16},{48,32},{64,48},{80,64},{96,80},{112,96},{17,1},{33... | collective-permute-start | bytes 1376264 | tf_op jit(solution)/shard_map/ppermute | solution.py:510
  48.5 14.9 %copy-start.2 = (f32[8,32,1792]{2,1,0:T(8,128)S(1)}, f32[8,32,1792]{2,1,0:T(8,128)}, u32[]{:S(2)}) copy-start(f32[8,32,1792]{2,1,0:T(8,128)} %get-tuple-element.33.rim_ref) | copy-start | bytes 5505028
  58.5 10.6 %collective-permute-start.4 = (bf16[704,1200]{1,0:T(8,128)(2,1)}, bf16[704,1200]{1,0:T(8,128)(2,1)}, u32[]{:S(2)}, u32[]{:S(2)}) collective-permute-start(bf16[704,1200]{1,0:T(8,128)(2,1)} %basis_other.1), channel_id=1, source_target_pairs={{0,16},{16,0},{1,17},{17,1},{2,18},{18,2},{3,19},{19,3},{4,20},{20... | collective-permute-start | bytes 5068808 | tf_op jit(solution)/shard_map/ppermute | solution.py:524
  64.1 1.2 copy-start.1
  65.4 31.8 %all-to-all-start.1 = ((bf16[16,32,1792]{2,1,0:T(8,128)(2,1)}), bf16[16,32,1792]{2,1,0:T(8,128)(2,1)S(1)}, u32[]{:S(2)}, u32[]{:S(2)}) async-start(bf16[16,32,1792]{2,1,0:T(8,128)(2,1)} %copy-done.1), calls=%async_computation.1 | async-start | bytes 3670016 | tf_op jit(solution)/shard_map/all_to_all | solution.py:522
  69.1 28.1 %copy-start.7 = (s32[3]{0:T(128)S(1)}, s32[3]{0:T(128)}, u32[]{:S(2)}) copy-start(s32[3]{0:T(128)} %pad_add_fusion.1.at_ref) | copy-start | bytes 40
  80.8 8.3 %collective-permute-start.5 = (bf16[88,1200]{1,0:T(8,128)(2,1)S(1)}, bf16[88,1200]{1,0:T(8,128)(2,1)S(1)}, u32[]{:S(2)}, u32[]{:S(2)}) collective-permute-start(bf16[88,1200]{1,0:T(8,128)(2,1)S(1)} %get-tuple-element.67), channel_id=1, source_target_pairs={{0,32},{32,64},{64,96},{96,0},{1,33},{33,65},{65,97},{97,1},{2,34}... | collective-permute-start | bytes 633608 | tf_op jit(solution)/shard_map/ppermute | solution.py:542
  82.5 6.6 %collective-permute-start.6 = (bf16[88,1200]{1,0:T(8,128)(2,1)S(1)}, bf16[88,1200]{1,0:T(8,128)(2,1)S(1)}, u32[]{:S(2)}, u32[]{:S(2)}) collective-permute-start(bf16[88,1200]{1,0:T(8,128)(2,1)S(1)} %get-tuple-element.66), channel_id=1, source_target_pairs={{0,96},{32,0},{64,32},{96,64},{1,97},{33,1},{65,33},{97,65},{2,98}... | collective-permute-start | bytes 633608 | tf_op jit(solution)/shard_map/ppermute | solution.py:542
  89.1 1.0 copy-start.5
  90.1 1.0 copy-start.6
  91.2 28.2 %copy-start.4 = (bf16[176,1200]{1,0:T(8,128)(2,1)S(1)}, bf16[176,1200]{1,0:T(8,128)(2,1)}, u32[]{:S(2)}) copy-start(bf16[176,1200]{1,0:T(8,128)(2,1)} %get-tuple-element.50.a_ref) | copy-start | bytes 1267204
  104.1 1.3 copy-start.3
  105.4 15.5 %collective-permute-start.7 = (bf16[1712,256]{1,0:T(8,128)(2,1)S(1)}, bf16[1712,256]{1,0:T(8,128)(2,1)S(1)}, u32[]{:S(2)}, u32[]{:S(2)}) collective-permute-start(bf16[1712,256]{1,0:T(8,128)(2,1)S(1)} %get-tuple-element.48), channel_id=1, source_target_pairs={{0,16},{16,0},{1,17},{17,1},{2,18},{18,2},{3,19},{19,3},{4,20},{20... | collective-permute-start | bytes 2629640 | tf_op jit(solution)/shard_map/ppermute | solution.py:576
  105.4 14.0 %collective-permute-start.8 = (bf16[176,1200]{1,0:T(8,128)(2,1)S(1)}, bf16[176,1200]{1,0:T(8,128)(2,1)S(1)}, u32[]{:S(2)}, u32[]{:S(2)}) collective-permute-start(bf16[176,1200]{1,0:T(8,128)(2,1)S(1)} %get-tuple-element.51), channel_id=1, source_target_pairs={{0,32},{32,64},{64,96},{96,0},{1,33},{33,65},{65,97},{97,1},{2,34}... | collective-permute-start | bytes 1267208 | tf_op jit(solution)/shard_map/ppermute | solution.py:552
  106.9 12.5 %collective-permute-start.9 = (bf16[176,1200]{1,0:T(8,128)(2,1)S(1)}, bf16[176,1200]{1,0:T(8,128)(2,1)S(1)}, u32[]{:S(2)}, u32[]{:S(2)}) collective-permute-start(bf16[176,1200]{1,0:T(8,128)(2,1)S(1)} %get-tuple-element.52), channel_id=1, source_target_pairs={{0,96},{32,0},{64,32},{96,64},{1,97},{33,1},{65,33},{97,65},{2,98}... | collective-permute-start | bytes 1267208 | tf_op jit(solution)/shard_map/ppermute | solution.py:552
  122.8 29.7 %all-to-all-start.2 = ((bf16[16,408,128]{2,1,0:T(8,128)(2,1)}), bf16[16,408,128]{2,1,0:T(8,128)(2,1)S(1)}, u32[]{:S(2)}, u32[]{:S(2)}) async-start(bf16[16,408,128]{2,1,0:T(8,128)(2,1)} %windows.1), calls=%async_computation.2 | async-start | bytes 3342336 | tf_op jit(solution)/shard_map/all_to_all | solution.py:577
  152.7 5.5 %collective-permute-start.10 = (bf16[256,128]{1,0:T(8,128)(2,1)S(1)}, bf16[256,128]{1,0:T(8,128)(2,1)S(1)}, u32[]{:S(2)}, u32[]{:S(2)}) collective-permute-start(bf16[256,128]{1,0:T(8,128)(2,1)S(1)} %get-tuple-element.55.a_ref), channel_id=1, source_target_pairs={{0,32},{32,64},{64,96},{96,0},{1,33},{33,65},{65,97},{97,1},{2,34}... | collective-permute-start | bytes 196616 | tf_op jit(solution)/shard_map/ppermute | solution.py:599
  153.4 6.2 %collective-permute-start.11 = (bf16[256,128]{1,0:T(8,128)(2,1)S(1)}, bf16[256,128]{1,0:T(8,128)(2,1)S(1)}, u32[]{:S(2)}, u32[]{:S(2)}) collective-permute-start(bf16[256,128]{1,0:T(8,128)(2,1)S(1)} %get-tuple-element.55.a_ref), channel_id=1, source_target_pairs={{0,64},{32,96},{64,0},{96,32},{1,65},{33,97},{65,1},{97,33},{2,66}... | collective-permute-start | bytes 196616 | tf_op jit(solution)/shard_map/ppermute | solution.py:599
  156.7 4.3 %collective-permute-start.12 = (bf16[256,128]{1,0:T(8,128)(2,1)S(1)}, bf16[256,128]{1,0:T(8,128)(2,1)S(1)}, u32[]{:S(2)}, u32[]{:S(2)}) collective-permute-start(bf16[256,128]{1,0:T(8,128)(2,1)S(1)} %get-tuple-element.55.a_ref), channel_id=1, source_target_pairs={{0,96},{32,0},{64,32},{96,64},{1,97},{33,1},{65,33},{97,65},{2,98}... | collective-permute-start | bytes 196616 | tf_op jit(solution)/shard_map/ppermute | solution.py:599
  161.0 1.4 collective-permute-start.13
  164.2 0.6 copy-start.8
  164.8 20.1 %all-to-all-start.3 = ((bf16[16,128,128]{2,1,0:T(8,128)(2,1)}), bf16[16,128,128]{2,1,0:T(8,128)(2,1)S(1)}, u32[]{:S(2)}, u32[]{:S(2)}) async-start(bf16[16,128,128]{2,1,0:T(8,128)(2,1)} %get-tuple-element.56), calls=%async_computation.3 | async-start | bytes 1048576 | tf_op jit(solution)/shard_map/all_to_all | solution.py:610
  168.7 1.3 collective-permute-start.14
  170.0 14.8 %collective-permute-start.15 = (bf16[2,152,128]{2,1,0:T(8,128)(2,1)S(1)}, bf16[2,152,128]{2,1,0:T(8,128)(2,1)S(1)}, u32[]{:S(2)}, u32[]{:S(2)}) collective-permute-start(bf16[2,152,128]{2,1,0:T(8,128)(2,1)S(1)} %pad_maximum_fusion.zero_ref), channel_id=1, source_target_pairs={{0,32},{32,64},{64,96},{96,0},{1,33},{33,65},{65,97},{97,1},{2,34}... | collective-permute-start | bytes 233480 | tf_op jit(solution)/shard_map/ppermute | solution.py:620
  170.1 14.7 %collective-permute-start.16 = (bf16[2,152,128]{2,1,0:T(8,128)(2,1)S(1)}, bf16[2,152,128]{2,1,0:T(8,128)(2,1)S(1)}, u32[]{:S(2)}, u32[]{:S(2)}) collective-permute-start(bf16[2,152,128]{2,1,0:T(8,128)(2,1)S(1)} %pad_maximum_fusion.zero_ref), channel_id=1, source_target_pairs={{0,64},{32,96},{64,0},{96,32},{1,65},{33,97},{65,1},{97,33},{2,66}... | collective-permute-start | bytes 233480 | tf_op jit(solution)/shard_map/ppermute | solution.py:620
  173.3 11.5 %collective-permute-start.17 = (bf16[2,152,128]{2,1,0:T(8,128)(2,1)S(1)}, bf16[2,152,128]{2,1,0:T(8,128)(2,1)S(1)}, u32[]{:S(2)}, u32[]{:S(2)}) collective-permute-start(bf16[2,152,128]{2,1,0:T(8,128)(2,1)S(1)} %pad_maximum_fusion.zero_ref), channel_id=1, source_target_pairs={{0,96},{32,0},{64,32},{96,64},{1,97},{33,1},{65,33},{97,65},{2,98}... | collective-permute-start | bytes 233480 | tf_op jit(solution)/shard_map/ppermute | solution.py:620
  174.2 10.7 %copy-start.9 = (f32[8,128]{1,0:T(8,128)S(1)}, f32[8,128]{1,0:T(8,128)}, u32[]{:S(2)}) copy-start(f32[8,128]{1,0:T(8,128)} %copy-done.8) | copy-start | bytes 12292

commit v5 on v4

--- a/solution.py
+++ b/solution.py
@@ -65,12 +65,10 @@
     return table
 
 
-def smooth_kernel(depth, own_ref, near_ref, tab_ref, taps_ref, raw_ref, all_ref, rim_ref, up_ref, down_ref, pad, planar, mid_ref, mat_ref, sems, mid_sem, mat_sem):
-    frames = raw_ref.shape[1]
-    extent = raw_ref.shape[2]
+def planes_kernel(taps_ref, raw_ref, planar, pad, mat_ref, made, sems, mat_sem, out_sems):
+    depth, frames, extent = raw_ref.shape
     step = PHASES * BLOCK
     steps = extent // step
-    tiles = extent // RUN
 
     def fetch(i):
         return pltpu.make_async_copy(
@@ -78,6 +76,10 @@
             pad.at[:, :, pl.ds(LEAD + i * step, step)],
             sems.at[i],
         )
+
+    def leave(i):
+        slot = i % 2
+        return pltpu.make_async_copy(made.at[slot], planar.at[:, :, pl.ds(i * step, step)], out_sems.at[slot])
 
     plan = pltpu.make_async_copy(taps_ref, mat_ref, mat_sem)
     plan.start()
@@ -94,15 +96,36 @@
         def _():
             fetch(i + 1).wait()
 
+        @pl.when(i >= 2)
+        def _():
+            leave(i - 2).wait()
+
         for phase in range(PHASES):
             start = pl.multiple_of(i * step + phase * BLOCK, BLOCK)
             cells = pad[:, :, pl.ds(start, LEAD + BLOCK + LEAD)].reshape(depth * frames, LEAD + BLOCK + LEAD)
             out = jnp.dot(cells, mat_ref[phase], preferred_element_type=jnp.float32)
-            planar[:, :, pl.ds(start, BLOCK)] = out.reshape(depth, frames, BLOCK)
+            made[i % 2, :, :, phase * BLOCK : (phase + 1) * BLOCK] = out.reshape(depth, frames, BLOCK)
+        leave(i).start()
         return carry
 
     lax.fori_loop(0, steps, block, 0)
-
+    leave(steps - 2).wait()
+    leave(steps - 1).wait()
+
+
+def depth_kernel(own_ref, near_ref, tab_ref, made_ref, all_ref, rim_ref, up_ref, down_ref, planar, mid_ref, sems, mid_sem):
+    depth, _, extent = planar.shape
+
+    def fetch(q):
+        return pltpu.make_async_copy(made_ref.at[q], planar.at[q], sems.at[q])
+
+    def more(q, carry):
+        fetch(q).wait()
+        return carry
+
+    for q in range(depth):
+        fetch(q).start()
+    tiles = extent // RUN
     taps = tap_weights()
 
     def place(tile):
@@ -111,14 +134,16 @@
 
     per = mid_ref.shape[2] // RUN
 
-    def middle(g, carry):
+    def middle(g, have):
+        last = own_ref[(g + GRP // 4) * per + per - 1] // tiles + RAD + 1
+        lax.fori_loop(have, last, more, 0)
         for j in range(per):
             plane, lane = place(own_ref[(g + GRP // 4) * per + j])
             total = taps[0] * planar[plane - RAD, :, pl.ds(lane, RUN)]
             for k in range(1, 2 * RAD + 1):
                 total = total + taps[k] * planar[plane - RAD + k, :, pl.ds(lane, RUN)]
             mid_ref[g, :, j * RUN : (j + 1) * RUN] = total.astype(mid_ref.dtype)
-        return carry
+        return jnp.maximum(have, last)
 
     def some(tile, first, count, shift):
         plane, lane = place(tile)
@@ -129,52 +154,76 @@
             total = term if total is None else total + term
         return total
 
-    def rims(g, carry):
+    def lower(g, carry):
+        for j in range(per):
+            cols = slice(j * RUN, (j + 1) * RUN)
+            at = g * per + j
+            down_ref[g, :, cols] = some(near_ref[GRP // 4 * per + at], 0, RAD, depth).astype(down_ref.dtype)
+            rim_ref[g, :, cols] = some(own_ref[at], 0, 2 * RAD, 0)
+        return carry
+
+    def upper(g, carry):
         for j in range(per):
             cols = slice(j * RUN, (j + 1) * RUN)
             at = g * per + j
             up_ref[g, :, cols] = some(near_ref[at], depth - RAD, RAD, -depth).astype(up_ref.dtype)
-            down_ref[g, :, cols] = some(near_ref[GRP // 4 * per + at], 0, RAD, depth).astype(down_ref.dtype)
-            rim_ref[g, :, cols] = some(own_ref[at], 0, 2 * RAD, 0)
             rim_ref[GRP // 4 + g, :, cols] = some(own_ref[GRP * 3 // 4 * per + at], depth - 2 * RAD, 2 * RAD, 0)
         return carry
 
-    lax.fori_loop(0, GRP // 2, middle, 0)
+    lax.fori_loop(0, 2 * RAD, more, 0)
+    lax.fori_loop(0, GRP // 4, lower, 0)
+    have = lax.fori_loop(0, GRP // 2, middle, jnp.int32(2 * RAD))
     keep = pltpu.make_async_copy(mid_ref, all_ref.at[GRP // 4 : GRP * 3 // 4], mid_sem)
     keep.start()
-    lax.fori_loop(0, GRP // 4, rims, 0)
+    lax.fori_loop(have, depth, more, 0)
+    lax.fori_loop(0, GRP // 4, upper, 0)
     keep.wait()
 
 
-def smooth(own, near, raw):
+def filter_planes(raw):
     depth, frames, extent = raw.shape
+    return pl.pallas_call(
+        planes_kernel,
+        out_shape=jax.ShapeDtypeStruct((depth, frames, extent), jnp.float32),
+        in_specs=[hbm(), hbm()],
+        out_specs=hbm(),
+        scratch_shapes=[
+            pltpu.VMEM((depth, frames, extent + 2 * LEAD), jnp.bfloat16),
+            pltpu.VMEM((PHASES, LEAD + BLOCK + LEAD, BLOCK), jnp.bfloat16),
+            pltpu.VMEM((2, depth, frames, PHASES * BLOCK), jnp.float32),
+            pltpu.SemaphoreType.DMA((extent // (PHASES * BLOCK),)),
+            pltpu.SemaphoreType.DMA,
+            pltpu.SemaphoreType.DMA((2,)),
+        ],
+        compiler_params=params(58),
+        name="planes",
+    )(jnp.asarray(plane_matrix()).astype(jnp.bfloat16), raw)
+
+
+def filter_depth(own, near, planar):
+    frames = planar.shape[1]
     per_device = own.shape[0] // GRP * RUN
-    smem = pl.BlockSpec(memory_space=pltpu.SMEM)
-    vmem = pl.BlockSpec(memory_space=pltpu.VMEM)
     quarter = (GRP // 4, frames, per_device)
     half = (GRP // 2, frames, per_device)
     return pl.pallas_call(
-        functools.partial(smooth_kernel, depth),
+        depth_kernel,
         out_shape=[
             jax.ShapeDtypeStruct((GRP, frames, per_device), jnp.bfloat16),
             jax.ShapeDtypeStruct(half, jnp.float32),
             jax.ShapeDtypeStruct(quarter, jnp.bfloat16),
             jax.ShapeDtypeStruct(quarter, jnp.bfloat16),
         ],
-        in_specs=[smem, smem, smem, pl.BlockSpec(memory_space=pltpu.HBM), pl.BlockSpec(memory_space=pltpu.HBM)],
-        out_specs=[pl.BlockSpec(memory_space=pltpu.HBM), vmem, vmem, vmem],
+        in_specs=[smem()] * 3 + [hbm()],
+        out_specs=[hbm(), *vmem(3)],
         scratch_shapes=[
-            pltpu.VMEM((depth, frames, extent + 2 * LEAD), jnp.bfloat16),
-            pltpu.VMEM((depth, frames, extent), jnp.float32),
+            pltpu.VMEM(planar.shape, jnp.float32),
             pltpu.VMEM(half, jnp.bfloat16),
-            pltpu.VMEM((PHASES, LEAD + BLOCK + LEAD, BLOCK), jnp.bfloat16),
-            pltpu.SemaphoreType.DMA((extent // (PHASES * BLOCK),)),
-            pltpu.SemaphoreType.DMA,
+            pltpu.SemaphoreType.DMA(planar.shape[:1]),
             pltpu.SemaphoreType.DMA,
         ],
-        compiler_params=pltpu.CompilerParams(vmem_limit_bytes=59 * 1024 * 1024),
-        name="smooth",
-    )(own, near, jnp.asarray(depth_table()), jnp.asarray(plane_matrix()).astype(jnp.bfloat16), raw)
+        compiler_params=params(44),
+        name="depth",
+    )(own, near, jnp.asarray(depth_table()), planar)
 
 
 NT = (((1,), (1,)), ((), ()))
@@ -204,48 +253,28 @@
     return pl.BlockSpec(memory_space=pltpu.HBM)
 
 
-PIECES = ((0, 512), (512, 1024), (1024, K))
 HALF = WIDE // 2
 
 
-def basis_copies(x, which, sub_ref, left, right, sems):
-    made = []
+def gather_parts(x, which, sub_ref, left):
     for k in range(4):
         start = pl.multiple_of(part_start((x + k) % 4 * 2 + which), 16)
-        made.append(
-            pltpu.make_async_copy(sub_ref.at[pl.ds(start, WIDE)], left.at[k * WIDE : (k + 1) * WIDE], sems.at[k])
-        )
-    for i, (lo, hi) in enumerate(PIECES):
-        rows = slice(lo, hi)
-        made.append(pltpu.make_async_copy(sub_ref.at[rows], right.at[rows], sems.at[4 + i]))
-    for copy in made:
-        copy.start()
-    return made
-
-
-def basis_other_kernel(at_ref, sub_ref, out_ref, left, right, sems):
-    made = basis_copies(at_ref[0], 1 - at_ref[1], sub_ref, left, right, sems)
-    for copy in made[:4]:
-        copy.wait()
-    for i, (lo, hi) in enumerate(PIECES):
-        made[4 + i].wait()
-        out_ref[:, lo:hi] = lax.dot_general(
-            left[...], right[lo:hi, :], NT, preferred_element_type=jnp.float32
-        ).astype(out_ref.dtype)
-
-
-def basis_own_kernel(at_ref, sub_ref, got_ref, own_ref, next_ref, far_ref, back_ref, left, right, sems):
-    made = basis_copies(at_ref[0], at_ref[1], sub_ref, left, right, sems)
-    for copy in made[:4]:
-        copy.wait()
-    for i, (lo, hi) in enumerate(PIECES):
-        made[4 + i].wait()
-        part = lax.dot_general(left[...], right[lo:hi, :], NT, preferred_element_type=jnp.float32)
-        part = (part + got_ref[:, lo:hi].astype(jnp.float32)).astype(own_ref.dtype)
-        own_ref[:, lo:hi] = part[:WIDE]
-        next_ref[:, lo:hi] = part[WIDE : 2 * WIDE]
-        far_ref[:, :, lo:hi] = part[2 * WIDE : 3 * WIDE].reshape(2, HALF, hi - lo)
-        back_ref[:, lo:hi] = part[3 * WIDE :]
+        left[k * WIDE : (k + 1) * WIDE, :] = sub_ref[pl.ds(start, WIDE), :]
+
+
+def basis_other_kernel(at_ref, sub_ref, out_ref, left):
+    gather_parts(at_ref[0], 1 - at_ref[1], sub_ref, left)
+    out_ref[...] = lax.dot_general(left[...], sub_ref[...], NT, preferred_element_type=jnp.float32).astype(out_ref.dtype)
+
+
+def basis_own_kernel(at_ref, sub_ref, got_ref, own_ref, next_ref, far_ref, back_ref, left):
+    gather_parts(at_ref[0], at_ref[1], sub_ref, left)
+    part = lax.dot_general(left[...], sub_ref[...], NT, preferred_element_type=jnp.float32)
+    part = (part + got_ref[...].astype(jnp.float32)).astype(own_ref.dtype)
+    own_ref[...] = part[:WIDE]
+    next_ref[...] = part[WIDE : 2 * WIDE]
+    far_ref[...] = part[2 * WIDE : 3 * WIDE].reshape(2, HALF, K)
+    back_ref[...] = part[3 * WIDE :]
 
 
 def basis_relay_kernel(next_ref, back_ref, low_ref, high_ref, next_out, back_out):
@@ -446,8 +475,8 @@
     steps = pl.num_programs(0)
 
     def fetch(i):
-        cols = pl.ds(pl.multiple_of(i * tile, tile), tile)
-        return pltpu.make_async_copy(base_ref.at[:, cols], held.at[i % 2], sems.at[i % 2])
+        rows = pl.ds(pl.multiple_of(i * tile, 8), tile)
+        return pltpu.make_async_copy(base_ref.at[rows], held.at[i % 2], sems.at[i % 2])
 
     @pl.when(step == 0)
     def _():
@@ -457,11 +486,14 @@
     def _():
         fetch(step + 1).start()
 
-    first = jnp.dot(turn_ref[:, :SUBJ], cen_ref[0], preferred_element_type=jnp.float32)
-    second = jnp.dot(turn_ref[:, SUBJ:], cen_ref[1], preferred_element_type=jnp.float32)
     fetch(step).wait()
-    base = held[step % 2]
-    out_ref[...] = (base + scale_ref[0:1, 0:1] * first + scale_ref[1:2, 0:1] * second).astype(out_ref.dtype)
+    slot = step % 2
+    for lo in range(0, out_ref.shape[1], 256):
+        cols = slice(lo, lo + 256)
+        first = jnp.dot(turn_ref[:, :SUBJ], cen_ref[0, :, cols], preferred_element_type=jnp.float32)
+        second = jnp.dot(turn_ref[:, SUBJ:], cen_ref[1, :, cols], preferred_element_type=jnp.float32)
+        base = held[slot, :, cols]
+        out_ref[:, cols] = (base + scale_ref[0:1, 0:1] * first + scale_ref[1:2, 0:1] * second).astype(out_ref.dtype)
 
 
 def copies(value, axis, count):
@@ -486,24 +518,22 @@
     up = [(i, i + 1) for i in range(7)]
     down = [(i + 1, i) for i in range(7)]
     packed = jnp.stack([tiles, lax.ppermute(tiles, slab, up), lax.ppermute(tiles, slab, down)])
-    every = copies(packed, "grp", GRP)
+    raw, _ = lax.optimization_barrier((jnp.transpose(raw_frames, (1, 0, 2)), packed))
+    planar = filter_planes(raw)
+    every, planar = lax.optimization_barrier((copies(packed, "grp", GRP), planar))
     own = every[:, 0].reshape(-1)
     near = jnp.concatenate([every[: GRP // 4, 2].reshape(-1), every[3 * GRP // 4 :, 1].reshape(-1)])
 
-    middles, rim, to_up, to_down = smooth(own, near, jnp.transpose(raw_frames, (1, 0, 2)))
+    middles, rim, to_up, to_down = filter_depth(own, near, planar)
     at_ss, _ = lax.optimization_barrier((at, to_down))
-    held = [
-        pltpu.VMEM((4 * WIDE, per_device), bf16),
-        pltpu.VMEM((K, per_device), bf16),
-        pltpu.SemaphoreType.DMA((4 + len(PIECES),)),
-    ]
+    held = [pltpu.VMEM((4 * WIDE, per_device), bf16)]
     other_ss = pl.pallas_call(
         basis_other_kernel,
         out_shape=like((4 * WIDE, K), bf16),
-        in_specs=[smem(), hbm()],
+        in_specs=[smem(), *vmem(1)],
         out_specs=vmem(1)[0],
         scratch_shapes=held,
-        compiler_params=params(BIG),
+        compiler_params=params(24),
         name="basis_other",
     )(at_ss, subspace)
     from_low, from_high, other_ss = lax.optimization_barrier(
@@ -525,10 +555,10 @@
     own_ss, next_ss, far_ss, back_ss = pl.pallas_call(
         basis_own_kernel,
         out_shape=[like((WIDE, K), bf16), like((WIDE, K), bf16), like((2, HALF, K), bf16), like((WIDE, K), bf16)],
-        in_specs=[smem(), hbm(), *vmem(1)],
+        in_specs=[smem(), *vmem(2)],
         out_specs=vmem(4),
         scratch_shapes=held,
-        compiler_params=params(BIG),
+        compiler_params=params(24),
         name="basis_own",
     )(at_ss, subspace, got_ss)
     ahead, behind = turns[1], turns[3]
@@ -540,7 +570,7 @@
         compiler_params=params(16),
         name="basis_relay",
     )(next_ss, back_ss, lax.ppermute(far_ss[0], "x", ahead), lax.ppermute(far_ss[1], "x", behind))
-    regrouped, next_ss, back_ss = lax.optimization_barrier((regrouped, next_ss, back_ss))
+    regrouped, _, _ = lax.optimization_barrier((regrouped, next_ss, back_ss))
     by_row = pl.pallas_call(
         basis_rows_kernel,
         out_shape=like((GRP, SHARE, RUN), bf16),
@@ -619,19 +649,19 @@
         name="assemble",
     )(at, back, rows_c, scales, share, *[lax.ppermute(share, "x", turns[k]) for k in range(1, 4)])
 
-    tile = 256
+    tile = 240
     new_subspace = pl.pallas_call(
         functools.partial(rotate_kernel, tile),
         out_shape=like((K, per_device), bf16),
-        grid=(per_device // tile,),
+        grid=(K // tile,),
         in_specs=[
             pl.BlockSpec((8, RUN), lambda i: (0, 0)),
             hbm(),
-            pl.BlockSpec((K, 2 * SUBJ), lambda i: (0, 0)),
-            pl.BlockSpec((2, SUBJ, tile), lambda i: (0, 0, i)),
+            pl.BlockSpec((tile, 2 * SUBJ), lambda i: (i, 0)),
+            pl.BlockSpec((2, SUBJ, per_device), lambda i: (0, 0, 0)),
         ],
-        out_specs=pl.BlockSpec((K, tile), lambda i: (0, i)),
-        scratch_shapes=[pltpu.VMEM((2, K, tile), f32), pltpu.SemaphoreType.DMA((2,))],
+        out_specs=pl.BlockSpec((tile, per_device), lambda i: (i, 0)),
+        scratch_shapes=[pltpu.VMEM((2, tile, per_device), f32), pltpu.SemaphoreType.DMA((2,))],
         compiler_params=params(BIG),
         name="rotate",
     )(scales, from_basis, turn, centered)

time: 188 us -> 187 us (level)
  blocking collectives: 15.6 us -> 0 us
  waiting for transfers between devices: 40 us -> 48.6 us
  starting transfers between devices: 40.1 us -> 48.3 us
  Pallas kernels: 67.6 us -> 63.3 us
  local copies, waits for them, and re-layouts: 10.9 us -> 13.5 us
    all_to_all x1 -> x0, blocking collectives: 15.6 us -> none  [copies(): lax.all_to_all(jnp.broadcast_to(value[None], (count, *value.shape)), axis...]
    all_to_all x0 -> x1, starting transfers between devices: none -> 8.16 us  [copies(): lax.all_to_all(jnp.broadcast_to(value[None], (count, *value.shape)), axis...]
    pallas_call x1, Pallas kernels: 10.6 us -> 4.95 us  [body(): pl.pallas_call(basis_own_kernel, out_shape=[like((WIDE, K), bf16), like((...]
    pallas_call x1 -> x2, Pallas kernels: 21.8 us -> 27.4 us  [the longest x1 17.9 us: filter_planes(): pl.pallas_call(planes_kernel, out_shape=jax.ShapeDtypeStruct((depth, fram...]
    ppermute x1, waiting for transfers between devices: 0.01 us -> 5.14 us  [body(): lax.ppermute(far_ss[1], 'x', behind)]
    pallas_call x1, Pallas kernels: 9.37 us -> 5.23 us  [body(): pl.pallas_call(basis_other_kernel, out_shape=like((4 * WIDE, K), bf16), i...]
    unnamed x20 -> x18, local copies, waits for them, and re-layouts: 5.13 us -> 8.72 us
    all_to_all x1, starting transfers between devices: 3.71 us -> 7.21 us  [body(): regrouped = lax.all_to_all(placed, 'grp', 0, 0, tiled=True)]
  transfers between devices with their start and end apart: 21 -> 22, of which waited for: 11 -> 12; matrix products, arithmetic and copies ran while one was open for 8% -> 7% of each run, Pallas kernels for 18% -> 22%
where the time goes in v5:
time: 187 us; the launch traced here: 186 us
  Pallas kernels  63.3 us (34%)
  waiting for transfers between devices  48.6 us (26%)
  starting transfers between devices  48.3 us (26%)
  local copies, waits for them, and re-layouts  13.5 us (7%)
  matrix products  10.7 us (6%)
    pallas_call x1, Pallas kernels, filter_planes(): pl.pallas_call(planes_kernel, out_shape=jax.ShapeDtypeStruct((depth, fram...  17.9 us
    all_to_all x1, waiting for transfers between devices, body(): summed = lax.all_to_all(sent, 'grp', 0, 0, tiled=True)  11.5 us
    ppermute x1, waiting for transfers between devices, body(): lax.ppermute(next_ss, 'x', ahead)  11 us
    dot_general x1, matrix products, body(): lax.dot_general(rotation_b[:K], subspace, contract, preferred_element_typ...  10.7 us
    pallas_call x1, Pallas kernels, body(): pl.pallas_call(functools.partial(rotate_kernel, tile), out_shape=like((K,...  10.5 us
    pallas_call x1, Pallas kernels, filter_depth(): pl.pallas_call(depth_kernel, out_shape=[jax.ShapeDtypeStruct((GRP, frames...  9.47 us
    unnamed x18, local copies, waits for them, and re-layouts  8.72 us
    all_to_all x1, waiting for transfers between devices, body(): regrouped = lax.all_to_all(placed, 'grp', 0, 0, tiled=True)  8.6 us
  transfers between devices with their start and end apart: 22, of which 12 were waited for; matrix products, arithmetic and copies ran while one was open for 7% of the time, Pallas kernels for 22%

profile of v5, /device:TPU:0, one launch (start us, length us, event | category | flops | bytes accessed | tf_op | source)
XLA Modules:
  0.0 185.5 jit_solution(14269766339510136180)
XLA Ops:
  0.6 0.8 slice_reduce_fusion
  1.5 1.3 collective-permute-start.1
  2.8 3.0 %collective-permute-start = (s32[14]{0:T(128)S(1)}, s32[14]{0:T(128)S(1)}, u32[]{:S(2)}, u32[]{:S(2)}) collective-permute-start(s32[14]{0:T(128)S(1)} %fusion.2), channel_id=1, source_target_pairs={{0,16},{16,32},{32,48},{48,64},{64,80},{80,96},{96,112},{1,17},{17... | collective-permute-start | bytes 176 | tf_op jit(solution)/shard_map/ppermute | solution.py:520
  5.8 0.8 collective-permute-done
  6.6 0.6 broadcast_in_dim.2
  7.2 8.2 %all-to-all-start = ((s32[16,3,14]{2,1,0:T(4,128)}), s32[16,3,14]{2,1,0:T(4,128)S(1)}, u32[]{:S(2)}, u32[]{:S(2)}) async-start(s32[16,3,14]{2,1,0:T(4,128)} %broadcast_in_dim.2), calls=%async_computation | async-start | bytes 65536 | tf_op jit(solution)/shard_map/all_to_all | solution.py:500
  15.4 17.9 %planes.1.made_ref = f32[12,32,10752]{2,1,0:T(8,128)} custom-call(bf16[3,1024,256]{2,1,0:T(8,128)(2,1)} %constant.42.taps_ref, bf16[12,32,10752]{2,1,0:T(8,128)(2,1)} %bitcast.27), custom_call_target="tpu_custom_call" | custom-call | tf_op jit(solution)/shard_map/planes/pallas_call | solution.py:185
  33.7 9.5 %depth.1 = (bf16[16,32,1792]{2,1,0:T(8,128)(2,1)S(1)}, f32[8,32,1792]{2,1,0:T(8,128)S(1)}, bf16[4,32,1792]{2,1,0:T(8,128)(2,1)}, bf16[4,32,1792]{2,1,0:T(8,128)(2,1)S(1)}) custom-call(s32[224]{0:T(256)S(1)} %reshape_squeeze.9.own_ref, s32[112]{0:T(128)S(1)} %pad_add_fusion.2.near_ref, f32[64]{0:T(128)S(1)} %copy-done.8, f32[12,32,10752]{2,1,0:T(8,128)} %planes.1.made_ref), custom_call_target="tpu_custom_call" | custom-call | tf_op jit(solution)/shard_map/depth/pallas_call | solution.py:208
  43.2 1.2 copy-done.3
  44.4 2.7 %collective-permute-start.2 = (bf16[4,32,1792]{2,1,0:T(8,128)(2,1)}, bf16[4,32,1792]{2,1,0:T(8,128)(2,1)S(1)}, u32[]{:S(2)}, u32[]{:S(2)}) collective-permute-start(bf16[4,32,1792]{2,1,0:T(8,128)(2,1)} %get-tuple-element.38), channel_id=1, source_target_pairs={{0,16},{16,32},{32,48},{48,64},{64,80},{80,96},{96,112},{1,17},{17... | collective-permute-start | bytes 1376264 | tf_op jit(solution)/shard_map/ppermute | solution.py:540
  47.1 1.3 collective-permute-start.3
  48.5 2.2 %copy-done = bf16[1200,1792]{1,0:T(8,128)(2,1)S(1)} copy-done((bf16[1200,1792]{1,0:T(8,128)(2,1)S(1)}, bf16[1200,1792]{1,0:T(8,128)(2,1)}, u32[]{:S(2)}) %copy-start) | copy-done | bytes 4300824
  50.7 5.2 %basis_other.1 = bf16[704,1200]{1,0:T(8,128)(2,1)} custom-call(s32[3]{0:T(128)S(1)} %pad_add_fusion.1.at_ref, bf16[1200,1792]{1,0:T(8,128)(2,1)S(1)} %copy-done), custom_call_target="tpu_custom_call" | custom-call | tf_op jit(solution)/shard_map/basis_other/pallas_call | solution.py:530
  55.9 3.5 %collective-permute-start.4 = (bf16[704,1200]{1,0:T(8,128)(2,1)}, bf16[704,1200]{1,0:T(8,128)(2,1)}, u32[]{:S(2)}, u32[]{:S(2)}) collective-permute-start(bf16[704,1200]{1,0:T(8,128)(2,1)} %basis_other.1), channel_id=1, source_target_pairs={{0,16},{16,0},{1,17},{17,1},{2,18},{18,2},{3,19},{19,3},{4,20},{20... | collective-permute-start | bytes 5068808 | tf_op jit(solution)/shard_map/ppermute | solution.py:554
  59.4 0.7 rim.1
  60.2 1.2 copy-done.2
  61.4 7.2 %all-to-all-start.1 = ((bf16[16,32,1792]{2,1,0:T(8,128)(2,1)}), bf16[16,32,1792]{2,1,0:T(8,128)(2,1)S(1)}, u32[]{:S(2)}, u32[]{:S(2)}) async-start(bf16[16,32,1792]{2,1,0:T(8,128)(2,1)} %copy-done.2), calls=%async_computation.1 | async-start | bytes 3670016 | tf_op jit(solution)/shard_map/all_to_all | solution.py:552
  68.6 2.2 %copy-done.1 = bf16[1200,1792]{1,0:T(8,128)(2,1)S(1)} copy-done((bf16[1200,1792]{1,0:T(8,128)(2,1)S(1)}, bf16[1200,1792]{1,0:T(8,128)(2,1)}, u32[]{:S(2)}) %copy-start.1) | copy-done | bytes 4300824
  70.8 5.0 %basis_own.1 = (bf16[176,1200]{1,0:T(8,128)(2,1)S(1)}, bf16[176,1200]{1,0:T(8,128)(2,1)S(1)}, bf16[2,88,1200]{2,1,0:T(8,128)(2,1)S(1)}, bf16[176,1200]{1,0:T(8,128)(2,1)S(1)}) custom-call(s32[3]{0:T(128)S(1)} %pad_add_fusion.1.at_ref, bf16[1200,1792]{1,0:T(8,128)(2,1)S(1)} %copy-done.1, bf16[704,1200]{1,0:T(8,128)(2,1)} %collective-permute-done.4.got_ref), custom_call_target="tpu_custom_call" | custom-call | tf_op jit(solution)/shard_map/basis_own/pallas_call | solution.py:555
  75.8 2.9 %collective-permute-start.6 = (bf16[88,1200]{1,0:T(8,128)(2,1)S(1)}, bf16[88,1200]{1,0:T(8,128)(2,1)S(1)}, u32[]{:S(2)}, u32[]{:S(2)}) collective-permute-start(bf16[88,1200]{1,0:T(8,128)(2,1)S(1)} %get-tuple-element.68), channel_id=1, source_target_pairs={{0,96},{32,0},{64,32},{96,64},{1,97},{33,1},{65,33},{97,65},{2,98}... | collective-permute-start | bytes 633608 | tf_op jit(solution)/shard_map/ppermute | solution.py:572
  78.8 5.1 %collective-permute-done.6.high_ref = bf16[88,1200]{1,0:T(8,128)(2,1)S(1)} collective-permute-done((bf16[88,1200]{1,0:T(8,128)(2,1)S(1)}, bf16[88,1200]{1,0:T(8,128)(2,1)S(1)}, u32[]{:S(2)}, u32[]{:S(2)}) %collective-permute-start.6) | collective-permute-done | bytes 211232 | tf_op jit(solution)/shard_map/ppermute | solution.py:572
  83.9 3.4 %collective-permute-done.5.low_ref = bf16[88,1200]{1,0:T(8,128)(2,1)S(1)} collective-permute-done((bf16[88,1200]{1,0:T(8,128)(2,1)S(1)}, bf16[88,1200]{1,0:T(8,128)(2,1)S(1)}, u32[]{:S(2)}, u32[]{:S(2)}) %collective-permute-start.5) | collective-permute-done | bytes 211232 | tf_op jit(solution)/shard_map/ppermute | solution.py:572
  87.4 8.6 %all-to-all-done.1.got_ref = bf16[16,32,1792]{2,1,0:T(8,128)(2,1)S(1)} async-done(((bf16[16,32,1792]{2,1,0:T(8,128)(2,1)}), bf16[16,32,1792]{2,1,0:T(8,128)(2,1)S(1)}, u32[]{:S(2)}, u32[]{:S(2)}) %all-to-all-start.1) | async-done | bytes 1835040 | tf_op jit(solution)/shard_map/all_to_all | solution.py:552
  96.0 6.9 %columns.1 = (bf16[2,256,1792]{2,1,0:T(8,128)(2,1)S(1)}, bf16[1712,256]{1,0:T(8,128)(2,1)S(1)}, f32[1712,256]{1,0:T(8,128)S(1)}, f32[8,128]{1,0:T(8,128)S(1)}) custom-call(s32[3]{0:T(128)S(1)} %pad_add_fusion.1.at_ref, bf16[16,32,1792]{2,1,0:T(8,128)(2,1)S(1)} %all-to-all-done.1.got_ref, bf16[1200,1792]{1,0:T(8,128)(2,1)} %basis_ref.1), custom_call_target="tpu_custom_call" | custom-call | tf_op jit(solution)/shard_map/columns/pallas_call | solution.py:584
  103.0 1.2 copy-done.5
  104.2 2.2 %collective-permute-start.8 = (bf16[176,1200]{1,0:T(8,128)(2,1)S(1)}, bf16[176,1200]{1,0:T(8,128)(2,1)S(1)}, u32[]{:S(2)}, u32[]{:S(2)}) collective-permute-start(bf16[176,1200]{1,0:T(8,128)(2,1)S(1)} %get-tuple-element.48), channel_id=1, source_target_pairs={{0,32},{32,64},{64,96},{96,0},{1,33},{33,65},{65,97},{97,1},{2,34}... | collective-permute-start | bytes 1267208 | tf_op jit(solution)/shard_map/ppermute | solution.py:582
  106.4 1.1 collective-permute-start.9
  107.6 11.0 %collective-permute-done.8.b_ref = bf16[176,1200]{1,0:T(8,128)(2,1)S(1)} collective-permute-done((bf16[176,1200]{1,0:T(8,128)(2,1)S(1)}, bf16[176,1200]{1,0:T(8,128)(2,1)S(1)}, u32[]{:S(2)}, u32[]{:S(2)}) %collective-permute-start.8) | collective-permute-done | bytes 422432 | tf_op jit(solution)/shard_map/ppermute | solution.py:582
  118.9 1.5 basis_rows.1.basis_ref
  120.4 1.9 %windows.1 = bf16[16,408,128]{2,1,0:T(8,128)(2,1)} custom-call(f32[1712,256]{1,0:T(8,128)S(1)} %get-tuple-element.51.own_ref, bf16[1712,256]{1,0:T(8,128)(2,1)S(1)} %collective-permute-done.7.got_ref, f32[8,128]{1,0:T(8,128)S(1)} %get-tuple-element.53.power_ref, bf16[16,152,128]{2,1,0:T(8,128)(2,1)S(1)} %basis_rows.1.basis_ref), custom_call_target="tpu_custom_call" | custom-call | tf_op jit(solution)/shard_map/windows/pallas_call | solution.py:598
  122.3 4.3 %all-to-all-start.2 = ((bf16[16,408,128]{2,1,0:T(8,128)(2,1)}), bf16[16,408,128]{2,1,0:T(8,128)(2,1)S(1)}, u32[]{:S(2)}, u32[]{:S(2)}) async-start(bf16[16,408,128]{2,1,0:T(8,128)(2,1)} %windows.1), calls=%async_computation.2 | async-start | bytes 3342336 | tf_op jit(solution)/shard_map/all_to_all | solution.py:607
  126.6 3.0 %slice_bitcast_fusion.turn_ref = bf16[1200,512]{1,0:T(8,128)(2,1)} fusion(bf16[1712,1200]{0,1:T(8,128)(2,1)} %param.9), kind=kLoop, calls=%fused_computation.2 | loop fusion | bytes 2457600 | tf_op jit(solution)/shard_map/transpose | solution.py:612
  129.6 10.7 %fusion.base_ref = f32[1200,1792]{1,0:T(8,128)} fusion(bf16[1200,1792]{1,0:T(8,128)(2,1)} %basis_ref.1, bf16[1712,1200]{0,1:T(8,128)(2,1)} %param.9), kind=kOutput, calls=%fused_computation | convolution fusion | flops 5160960000 | bytes 15974400 | tf_op jit(solution)/shard_map/dot_general | solution.py:611
  140.3 11.5 %all-to-all-done.2.got_ref = bf16[16,408,128]{2,1,0:T(8,128)(2,1)S(1)} async-done(((bf16[16,408,128]{2,1,0:T(8,128)(2,1)}), bf16[16,408,128]{2,1,0:T(8,128)(2,1)S(1)}, u32[]{:S(2)}, u32[]{:S(2)}) %all-to-all-start.2) | async-done | bytes 1671200 | tf_op jit(solution)/shard_map/all_to_all | solution.py:607
  152.1 2.5 %collective-permute-start.12 = (bf16[256,128]{1,0:T(8,128)(2,1)S(1)}, bf16[256,128]{1,0:T(8,128)(2,1)S(1)}, u32[]{:S(2)}, u32[]{:S(2)}) collective-permute-start(bf16[256,128]{1,0:T(8,128)(2,1)S(1)} %get-tuple-element.57.a_ref), channel_id=1, source_target_pairs={{0,96},{32,0},{64,32},{96,64},{1,97},{33,1},{65,33},{97,65},{2,98}... | collective-permute-start | bytes 196616 | tf_op jit(solution)/shard_map/ppermute | solution.py:629
  154.8 0.9 collective-permute-start.10
  155.7 0.8 collective-permute-done.12.d_ref
  156.5 4.0 %collective-permute-done.11.c_ref = bf16[256,128]{1,0:T(8,128)(2,1)S(1)} collective-permute-done((bf16[256,128]{1,0:T(8,128)(2,1)S(1)}, bf16[256,128]{1,0:T(8,128)(2,1)S(1)}, u32[]{:S(2)}, u32[]{:S(2)}) %collective-permute-start.11) | collective-permute-done | bytes 65568 | tf_op jit(solution)/shard_map/ppermute | solution.py:629
  161.1 1.3 collective-permute-done.13.got_ref
  162.4 1.7 finish.1
  164.1 0.6 copy-done.6
  164.7 3.8 %all-to-all-start.3 = ((bf16[16,128,128]{2,1,0:T(8,128)(2,1)}), bf16[16,128,128]{2,1,0:T(8,128)(2,1)S(1)}, u32[]{:S(2)}, u32[]{:S(2)}) async-start(bf16[16,128,128]{2,1,0:T(8,128)(2,1)} %get-tuple-element.58), calls=%async_computation.3 | async-start | bytes 1048576 | tf_op jit(solution)/shard_map/all_to_all | solution.py:640
  168.6 1.2 collective-permute-done.14
  169.8 0.9 collective-permute-start.17
  170.7 0.9 collective-permute-start.16
  171.6 1.3 collective-permute-start.15
  172.9 10.5 %rotate.1 = bf16[1200,1792]{1,0:T(8,128)(2,1)} custom-call(f32[8,128]{1,0:T(8,128)} %copy-done.6, f32[1200,1792]{1,0:T(8,128)} %fusion.base_ref, bf16[1200,512]{1,0:T(8,128)(2,1)} %slice_bitcast_fusion.turn_ref, bf16[2,256,1792]{2,1,0:T(8,128)(2,1)} %copy-done.5), custom_call_target="tpu_custom_call" | custom-call | tf_op jit(solution)/shard_map/rotate/pallas_call | solution.py:653
  183.4 2.1 %assemble.1 = f32[107,1712]{1,0:T(8,128)} custom-call(s32[3]{0:T(128)S(1)} %pad_add_fusion.1.at_ref, bf16[16,128,128]{2,1,0:T(8,128)(2,1)S(1)} %all-to-all-done.3.back_ref, f32[128,512]{1,0:T(8,128)S(1)} %get-tuple-element.59.rows_ref, f32[8,128]{1,0:T(8,128)S(1)} %copy-done.7, bf16[2,152,128]{2,1,0:T(8,128)(2,1)S(1)} %pad_maximum_fusion.zero_ref, ...), custom_call_target="tpu_custom_call" | custom-call | tf_op jit(solution)/shard_map/assemble/pallas_call | solution.py:642
  (44 shorter events, 2.1 us)
Async XLA Ops:
  1.5 4.4 %collective-permute-start.1 = (s32[14]{0:T(128)S(1)}, s32[14]{0:T(128)S(1)}, u32[]{:S(2)}, u32[]{:S(2)}) collective-permute-start(s32[14]{0:T(128)S(1)} %fusion.2), channel_id=1, source_target_pairs={{16,0},{32,16},{48,32},{64,48},{80,64},{96,80},{112,96},{17,1},{33... | collective-permute-start | bytes 176 | tf_op jit(solution)/shard_map/ppermute | solution.py:520
  2.8 3.8 %collective-permute-start = (s32[14]{0:T(128)S(1)}, s32[14]{0:T(128)S(1)}, u32[]{:S(2)}, u32[]{:S(2)}) collective-permute-start(s32[14]{0:T(128)S(1)} %fusion.2), channel_id=1, source_target_pairs={{0,16},{16,32},{32,48},{48,64},{64,80},{80,96},{96,112},{1,17},{17... | collective-permute-start | bytes 176 | tf_op jit(solution)/shard_map/ppermute | solution.py:520
  7.2 26.1 %all-to-all-start = ((s32[16,3,14]{2,1,0:T(4,128)}), s32[16,3,14]{2,1,0:T(4,128)S(1)}, u32[]{:S(2)}, u32[]{:S(2)}) async-start(s32[16,3,14]{2,1,0:T(4,128)} %broadcast_in_dim.2), calls=%async_computation | async-start | bytes 65536 | tf_op jit(solution)/shard_map/all_to_all | solution.py:500
  15.4 18.3 %copy-start.8 = (f32[64]{0:T(128)S(1)}, f32[64]{0:T(128)}, u32[]{:S(2)}) copy-start(f32[64]{0:T(128)} %constant.40.clone.tab_ref) | copy-start | bytes 772
  43.2 1.2 copy-start.3
  44.4 11.5 %collective-permute-start.2 = (bf16[4,32,1792]{2,1,0:T(8,128)(2,1)}, bf16[4,32,1792]{2,1,0:T(8,128)(2,1)S(1)}, u32[]{:S(2)}, u32[]{:S(2)}) collective-permute-start(bf16[4,32,1792]{2,1,0:T(8,128)(2,1)} %get-tuple-element.38), channel_id=1, source_target_pairs={{0,16},{16,32},{32,48},{48,64},{64,80},{80,96},{96,112},{1,17},{17... | collective-permute-start | bytes 1376264 | tf_op jit(solution)/shard_map/ppermute | solution.py:540
  47.1 8.8 %collective-permute-start.3 = (bf16[4,32,1792]{2,1,0:T(8,128)(2,1)S(1)}, bf16[4,32,1792]{2,1,0:T(8,128)(2,1)S(1)}, u32[]{:S(2)}, u32[]{:S(2)}) collective-permute-start(bf16[4,32,1792]{2,1,0:T(8,128)(2,1)S(1)} %get-tuple-element.39), channel_id=1, source_target_pairs={{16,0},{32,16},{48,32},{64,48},{80,64},{96,80},{112,96},{17,1},{33... | collective-permute-start | bytes 1376264 | tf_op jit(solution)/shard_map/ppermute | solution.py:540
  48.5 2.2 %copy-start = (bf16[1200,1792]{1,0:T(8,128)(2,1)S(1)}, bf16[1200,1792]{1,0:T(8,128)(2,1)}, u32[]{:S(2)}) copy-start(bf16[1200,1792]{1,0:T(8,128)(2,1)} %basis_ref.1) | copy-start | bytes 12902404
  50.7 8.7 %copy-start.4 = (f32[8,32,1792]{2,1,0:T(8,128)S(1)}, f32[8,32,1792]{2,1,0:T(8,128)}, u32[]{:S(2)}) copy-start(f32[8,32,1792]{2,1,0:T(8,128)} %copy-done.3) | copy-start | bytes 5505028
  55.9 12.7 %collective-permute-start.4 = (bf16[704,1200]{1,0:T(8,128)(2,1)}, bf16[704,1200]{1,0:T(8,128)(2,1)}, u32[]{:S(2)}, u32[]{:S(2)}) collective-permute-start(bf16[704,1200]{1,0:T(8,128)(2,1)} %basis_other.1), channel_id=1, source_target_pairs={{0,16},{16,0},{1,17},{17,1},{2,18},{18,2},{3,19},{19,3},{4,20},{20... | collective-permute-start | bytes 5068808 | tf_op jit(solution)/shard_map/ppermute | solution.py:554
  60.2 1.2 copy-start.2
  61.4 34.6 %all-to-all-start.1 = ((bf16[16,32,1792]{2,1,0:T(8,128)(2,1)}), bf16[16,32,1792]{2,1,0:T(8,128)(2,1)S(1)}, u32[]{:S(2)}, u32[]{:S(2)}) async-start(bf16[16,32,1792]{2,1,0:T(8,128)(2,1)} %copy-done.2), calls=%async_computation.1 | async-start | bytes 3670016 | tf_op jit(solution)/shard_map/all_to_all | solution.py:552
  68.6 2.2 %copy-start.1 = (bf16[1200,1792]{1,0:T(8,128)(2,1)S(1)}, bf16[1200,1792]{1,0:T(8,128)(2,1)}, u32[]{:S(2)}) copy-start(bf16[1200,1792]{1,0:T(8,128)(2,1)} %basis_ref.1) | copy-start | bytes 12902404
  75.8 8.1 %collective-permute-start.6 = (bf16[88,1200]{1,0:T(8,128)(2,1)S(1)}, bf16[88,1200]{1,0:T(8,128)(2,1)S(1)}, u32[]{:S(2)}, u32[]{:S(2)}) collective-permute-start(bf16[88,1200]{1,0:T(8,128)(2,1)S(1)} %get-tuple-element.68), channel_id=1, source_target_pairs={{0,96},{32,0},{64,32},{96,64},{1,97},{33,1},{65,33},{97,65},{2,98}... | collective-permute-start | bytes 633608 | tf_op jit(solution)/shard_map/ppermute | solution.py:572
  78.8 8.6 %collective-permute-start.5 = (bf16[88,1200]{1,0:T(8,128)(2,1)S(1)}, bf16[88,1200]{1,0:T(8,128)(2,1)S(1)}, u32[]{:S(2)}, u32[]{:S(2)}) collective-permute-start(bf16[88,1200]{1,0:T(8,128)(2,1)S(1)} %get-tuple-element.69), channel_id=1, source_target_pairs={{0,32},{32,64},{64,96},{96,0},{1,33},{33,65},{65,97},{97,1},{2,34}... | collective-permute-start | bytes 633608 | tf_op jit(solution)/shard_map/ppermute | solution.py:572
  103.0 1.2 copy-start.5
  104.2 16.2 %collective-permute-start.7 = (bf16[1712,256]{1,0:T(8,128)(2,1)S(1)}, bf16[1712,256]{1,0:T(8,128)(2,1)S(1)}, u32[]{:S(2)}, u32[]{:S(2)}) collective-permute-start(bf16[1712,256]{1,0:T(8,128)(2,1)S(1)} %get-tuple-element.52), channel_id=1, source_target_pairs={{0,16},{16,0},{1,17},{17,1},{2,18},{18,2},{3,19},{19,3},{4,20},{20... | collective-permute-start | bytes 2629640 | tf_op jit(solution)/shard_map/ppermute | solution.py:606
  104.2 14.3 %collective-permute-start.8 = (bf16[176,1200]{1,0:T(8,128)(2,1)S(1)}, bf16[176,1200]{1,0:T(8,128)(2,1)S(1)}, u32[]{:S(2)}, u32[]{:S(2)}) collective-permute-start(bf16[176,1200]{1,0:T(8,128)(2,1)S(1)} %get-tuple-element.48), channel_id=1, source_target_pairs={{0,32},{32,64},{64,96},{96,0},{1,33},{33,65},{65,97},{97,1},{2,34}... | collective-permute-start | bytes 1267208 | tf_op jit(solution)/shard_map/ppermute | solution.py:582
  106.4 12.5 %collective-permute-start.9 = (bf16[176,1200]{1,0:T(8,128)(2,1)S(1)}, bf16[176,1200]{1,0:T(8,128)(2,1)S(1)}, u32[]{:S(2)}, u32[]{:S(2)}) collective-permute-start(bf16[176,1200]{1,0:T(8,128)(2,1)S(1)} %get-tuple-element.49), channel_id=1, source_target_pairs={{0,96},{32,0},{64,32},{96,64},{1,97},{33,1},{65,33},{97,65},{2,98}... | collective-permute-start | bytes 1267208 | tf_op jit(solution)/shard_map/ppermute | solution.py:582
  122.3 29.5 %all-to-all-start.2 = ((bf16[16,408,128]{2,1,0:T(8,128)(2,1)}), bf16[16,408,128]{2,1,0:T(8,128)(2,1)S(1)}, u32[]{:S(2)}, u32[]{:S(2)}) async-start(bf16[16,408,128]{2,1,0:T(8,128)(2,1)} %windows.1), calls=%async_computation.2 | async-start | bytes 3342336 | tf_op jit(solution)/shard_map/all_to_all | solution.py:607
  152.1 4.4 %collective-permute-start.12 = (bf16[256,128]{1,0:T(8,128)(2,1)S(1)}, bf16[256,128]{1,0:T(8,128)(2,1)S(1)}, u32[]{:S(2)}, u32[]{:S(2)}) collective-permute-start(bf16[256,128]{1,0:T(8,128)(2,1)S(1)} %get-tuple-element.57.a_ref), channel_id=1, source_target_pairs={{0,96},{32,0},{64,32},{96,64},{1,97},{33,1},{65,33},{97,65},{2,98}... | collective-permute-start | bytes 196616 | tf_op jit(solution)/shard_map/ppermute | solution.py:629
  154.6 5.9 %collective-permute-start.11 = (bf16[256,128]{1,0:T(8,128)(2,1)S(1)}, bf16[256,128]{1,0:T(8,128)(2,1)S(1)}, u32[]{:S(2)}, u32[]{:S(2)}) collective-permute-start(bf16[256,128]{1,0:T(8,128)(2,1)S(1)} %get-tuple-element.57.a_ref), channel_id=1, source_target_pairs={{0,64},{32,96},{64,0},{96,32},{1,65},{33,97},{65,1},{97,33},{2,66}... | collective-permute-start | bytes 196616 | tf_op jit(solution)/shard_map/ppermute | solution.py:629
  154.8 6.2 %collective-permute-start.10 = (bf16[256,128]{1,0:T(8,128)(2,1)S(1)}, bf16[256,128]{1,0:T(8,128)(2,1)S(1)}, u32[]{:S(2)}, u32[]{:S(2)}) collective-permute-start(bf16[256,128]{1,0:T(8,128)(2,1)S(1)} %get-tuple-element.57.a_ref), channel_id=1, source_target_pairs={{0,32},{32,64},{64,96},{96,0},{1,33},{33,65},{65,97},{97,1},{2,34}... | collective-permute-start | bytes 196616 | tf_op jit(solution)/shard_map/ppermute | solution.py:629
  161.0 1.4 collective-permute-start.13
  164.1 0.6 copy-start.6
  164.7 18.6 %all-to-all-start.3 = ((bf16[16,128,128]{2,1,0:T(8,128)(2,1)}), bf16[16,128,128]{2,1,0:T(8,128)(2,1)S(1)}, u32[]{:S(2)}, u32[]{:S(2)}) async-start(bf16[16,128,128]{2,1,0:T(8,128)(2,1)} %get-tuple-element.58), calls=%async_computation.3 | async-start | bytes 1048576 | tf_op jit(solution)/shard_map/all_to_all | solution.py:640
  168.5 1.3 collective-permute-start.14
  169.8 13.5 %collective-permute-start.17 = (bf16[2,152,128]{2,1,0:T(8,128)(2,1)S(1)}, bf16[2,152,128]{2,1,0:T(8,128)(2,1)S(1)}, u32[]{:S(2)}, u32[]{:S(2)}) collective-permute-start(bf16[2,152,128]{2,1,0:T(8,128)(2,1)S(1)} %pad_maximum_fusion.zero_ref), channel_id=1, source_target_pairs={{0,96},{32,0},{64,32},{96,64},{1,97},{33,1},{65,33},{97,65},{2,98}... | collective-permute-start | bytes 233480 | tf_op jit(solution)/shard_map/ppermute | solution.py:650
  170.7 12.7 %collective-permute-start.16 = (bf16[2,152,128]{2,1,0:T(8,128)(2,1)S(1)}, bf16[2,152,128]{2,1,0:T(8,128)(2,1)S(1)}, u32[]{:S(2)}, u32[]{:S(2)}) collective-permute-start(bf16[2,152,128]{2,1,0:T(8,128)(2,1)S(1)} %pad_maximum_fusion.zero_ref), channel_id=1, source_target_pairs={{0,64},{32,96},{64,0},{96,32},{1,65},{33,97},{65,1},{97,33},{2,66}... | collective-permute-start | bytes 233480 | tf_op jit(solution)/shard_map/ppermute | solution.py:650
  171.6 11.8 %collective-permute-start.15 = (bf16[2,152,128]{2,1,0:T(8,128)(2,1)S(1)}, bf16[2,152,128]{2,1,0:T(8,128)(2,1)S(1)}, u32[]{:S(2)}, u32[]{:S(2)}) collective-permute-start(bf16[2,152,128]{2,1,0:T(8,128)(2,1)S(1)} %pad_maximum_fusion.zero_ref), channel_id=1, source_target_pairs={{0,32},{32,64},{64,96},{96,0},{1,33},{33,65},{65,97},{97,1},{2,34}... | collective-permute-start | bytes 233480 | tf_op jit(solution)/shard_map/ppermute | solution.py:650
  172.9 10.5 %copy-start.7 = (f32[8,128]{1,0:T(8,128)S(1)}, f32[8,128]{1,0:T(8,128)}, u32[]{:S(2)}) copy-start(f32[8,128]{1,0:T(8,128)} %copy-done.6) | copy-start | bytes 12292

commit v6 on v5

--- a/solution.py
+++ b/solution.py
@@ -9,6 +9,7 @@
 from jax.experimental.pallas import tpu as pltpu
 from jax.sharding import Mesh
 from jax.sharding import PartitionSpec as P
+
 
 NX = 96
 RUN = 128
@@ -22,6 +23,7 @@
 PART = 150
 WIDE = 176
 SHARE = 152
+SMOOTH_MIB = 48
 BIG = 56
 LEAD = 384
 BLOCK = 256
@@ -65,10 +67,11 @@
     return table
 
 
-def planes_kernel(taps_ref, raw_ref, planar, pad, mat_ref, made, sems, mat_sem, out_sems):
+def smooth_kernel(own_ref, near_ref, tab_ref, taps_ref, raw_ref, all_ref, rim_ref, up_ref, down_ref, pad, planar, mid_ref, mat_ref, sems, mid_sem, mat_sem):
     depth, frames, extent = raw_ref.shape
     step = PHASES * BLOCK
     steps = extent // step
+    tiles = extent // RUN
 
     def fetch(i):
         return pltpu.make_async_copy(
@@ -76,10 +79,6 @@
             pad.at[:, :, pl.ds(LEAD + i * step, step)],
             sems.at[i],
         )
-
-    def leave(i):
-        slot = i % 2
-        return pltpu.make_async_copy(made.at[slot], planar.at[:, :, pl.ds(i * step, step)], out_sems.at[slot])
 
     plan = pltpu.make_async_copy(taps_ref, mat_ref, mat_sem)
     plan.start()
@@ -96,36 +95,15 @@
         def _():
             fetch(i + 1).wait()
 
-        @pl.when(i >= 2)
-        def _():
-            leave(i - 2).wait()
-
         for phase in range(PHASES):
             start = pl.multiple_of(i * step + phase * BLOCK, BLOCK)
             cells = pad[:, :, pl.ds(start, LEAD + BLOCK + LEAD)].reshape(depth * frames, LEAD + BLOCK + LEAD)
             out = jnp.dot(cells, mat_ref[phase], preferred_element_type=jnp.float32)
-            made[i % 2, :, :, phase * BLOCK : (phase + 1) * BLOCK] = out.reshape(depth, frames, BLOCK)
-        leave(i).start()
+            planar[:, :, pl.ds(start, BLOCK)] = out.reshape(depth, frames, BLOCK)
         return carry
 
     lax.fori_loop(0, steps, block, 0)
-    leave(steps - 2).wait()
-    leave(steps - 1).wait()
-
-
-def depth_kernel(own_ref, near_ref, tab_ref, made_ref, all_ref, rim_ref, up_ref, down_ref, planar, mid_ref, sems, mid_sem):
-    depth, _, extent = planar.shape
-
-    def fetch(q):
-        return pltpu.make_async_copy(made_ref.at[q], planar.at[q], sems.at[q])
-
-    def more(q, carry):
-        fetch(q).wait()
-        return carry
-
-    for q in range(depth):
-        fetch(q).start()
-    tiles = extent // RUN
+
     taps = tap_weights()
 
     def place(tile):
@@ -134,16 +112,14 @@
 
     per = mid_ref.shape[2] // RUN
 
-    def middle(g, have):
-        last = own_ref[(g + GRP // 4) * per + per - 1] // tiles + RAD + 1
-        lax.fori_loop(have, last, more, 0)
+    def middle(g, carry):
         for j in range(per):
             plane, lane = place(own_ref[(g + GRP // 4) * per + j])
             total = taps[0] * planar[plane - RAD, :, pl.ds(lane, RUN)]
             for k in range(1, 2 * RAD + 1):
                 total = total + taps[k] * planar[plane - RAD + k, :, pl.ds(lane, RUN)]
             mid_ref[g, :, j * RUN : (j + 1) * RUN] = total.astype(mid_ref.dtype)
-        return jnp.maximum(have, last)
+        return carry
 
     def some(tile, first, count, shift):
         plane, lane = place(tile)
@@ -154,76 +130,50 @@
             total = term if total is None else total + term
         return total
 
-    def lower(g, carry):
-        for j in range(per):
-            cols = slice(j * RUN, (j + 1) * RUN)
-            at = g * per + j
-            down_ref[g, :, cols] = some(near_ref[GRP // 4 * per + at], 0, RAD, depth).astype(down_ref.dtype)
-            rim_ref[g, :, cols] = some(own_ref[at], 0, 2 * RAD, 0)
-        return carry
-
-    def upper(g, carry):
+    def rims(g, carry):
         for j in range(per):
             cols = slice(j * RUN, (j + 1) * RUN)
             at = g * per + j
             up_ref[g, :, cols] = some(near_ref[at], depth - RAD, RAD, -depth).astype(up_ref.dtype)
+            down_ref[g, :, cols] = some(near_ref[GRP // 4 * per + at], 0, RAD, depth).astype(down_ref.dtype)
+            rim_ref[g, :, cols] = some(own_ref[at], 0, 2 * RAD, 0)
             rim_ref[GRP // 4 + g, :, cols] = some(own_ref[GRP * 3 // 4 * per + at], depth - 2 * RAD, 2 * RAD, 0)
         return carry
 
-    lax.fori_loop(0, 2 * RAD, more, 0)
-    lax.fori_loop(0, GRP // 4, lower, 0)
-    have = lax.fori_loop(0, GRP // 2, middle, jnp.int32(2 * RAD))
+    lax.fori_loop(0, GRP // 2, middle, 0)
     keep = pltpu.make_async_copy(mid_ref, all_ref.at[GRP // 4 : GRP * 3 // 4], mid_sem)
     keep.start()
-    lax.fori_loop(have, depth, more, 0)
-    lax.fori_loop(0, GRP // 4, upper, 0)
+    lax.fori_loop(0, GRP // 4, rims, 0)
     keep.wait()
 
 
-def filter_planes(raw):
+def smooth(own, near, raw):
     depth, frames, extent = raw.shape
-    return pl.pallas_call(
-        planes_kernel,
-        out_shape=jax.ShapeDtypeStruct((depth, frames, extent), jnp.float32),
-        in_specs=[hbm(), hbm()],
-        out_specs=hbm(),
-        scratch_shapes=[
-            pltpu.VMEM((depth, frames, extent + 2 * LEAD), jnp.bfloat16),
-            pltpu.VMEM((PHASES, LEAD + BLOCK + LEAD, BLOCK), jnp.bfloat16),
-            pltpu.VMEM((2, depth, frames, PHASES * BLOCK), jnp.float32),
-            pltpu.SemaphoreType.DMA((extent // (PHASES * BLOCK),)),
-            pltpu.SemaphoreType.DMA,
-            pltpu.SemaphoreType.DMA((2,)),
-        ],
-        compiler_params=params(58),
-        name="planes",
-    )(jnp.asarray(plane_matrix()).astype(jnp.bfloat16), raw)
-
-
-def filter_depth(own, near, planar):
-    frames = planar.shape[1]
     per_device = own.shape[0] // GRP * RUN
     quarter = (GRP // 4, frames, per_device)
     half = (GRP // 2, frames, per_device)
     return pl.pallas_call(
-        depth_kernel,
+        smooth_kernel,
         out_shape=[
             jax.ShapeDtypeStruct((GRP, frames, per_device), jnp.bfloat16),
             jax.ShapeDtypeStruct(half, jnp.float32),
             jax.ShapeDtypeStruct(quarter, jnp.bfloat16),
             jax.ShapeDtypeStruct(quarter, jnp.bfloat16),
         ],
-        in_specs=[smem()] * 3 + [hbm()],
+        in_specs=[smem()] * 3 + [hbm(), hbm()],
         out_specs=[hbm(), *vmem(3)],
         scratch_shapes=[
-            pltpu.VMEM(planar.shape, jnp.float32),
+            pltpu.VMEM((depth, frames, extent + 2 * LEAD), jnp.bfloat16),
+            pltpu.VMEM((depth, frames, extent), jnp.float32),
             pltpu.VMEM(half, jnp.bfloat16),
-            pltpu.SemaphoreType.DMA(planar.shape[:1]),
+            pltpu.VMEM((PHASES, LEAD + BLOCK + LEAD, BLOCK), jnp.bfloat16),
+            pltpu.SemaphoreType.DMA((extent // (PHASES * BLOCK),)),
+            pltpu.SemaphoreType.DMA,
             pltpu.SemaphoreType.DMA,
         ],
-        compiler_params=params(44),
-        name="depth",
-    )(own, near, jnp.asarray(depth_table()), planar)
+        compiler_params=params(SMOOTH_MIB),
+        name="smooth",
+    )(own, near, jnp.asarray(depth_table()), jnp.asarray(plane_matrix()).astype(jnp.bfloat16), raw)
 
 
 NT = (((1,), (1,)), ((), ()))
@@ -390,12 +340,11 @@
             ].astype(out_ref.dtype)
 
 
-def total_kernel(got_ref, out_ref, share_ref):
+def total_kernel(got_ref, out_ref):
     total = got_ref[0].astype(jnp.float32)
     for g in range(1, GRP):
         total = total + got_ref[g].astype(jnp.float32)
-    out_ref[...] = total[: 2 * TALL].astype(out_ref.dtype)
-    share_ref[...] = total[2 * TALL :].astype(share_ref.dtype)
+    out_ref[...] = total.astype(out_ref.dtype)
 
     def put(rows, value):
         out_ref[rows, :] = value
@@ -403,9 +352,14 @@
     write_power(total[WIN:TALL] + total[TALL + WIN : 2 * TALL], put)
 
 
-def slab_kernel(a_ref, b_ref, c_ref, d_ref, sum_ref):
-    total = a_ref[...].astype(jnp.float32) + b_ref[...].astype(jnp.float32)
-    sum_ref[...] = total + c_ref[...].astype(jnp.float32) + d_ref[...].astype(jnp.float32)
+def slab_kernel(a_ref, b_ref, c_ref, d_ref, sum_ref, share_ref):
+    refs = (a_ref, b_ref, c_ref, d_ref)
+    total = refs[0][: 2 * TALL].astype(jnp.float32)
+    for ref in refs[1:]:
+        total = total + ref[: 2 * TALL].astype(jnp.float32)
+    sum_ref[...] = total
+    for k in range(4):
+        share_ref[k] = refs[k][2 * TALL :]
 
 
 def finish_kernel(count, at_ref, own_ref, got_ref, rows_ref, scale_ref, turned_ref):
@@ -429,22 +383,21 @@
         turned_ref[g] = lax.dot_general(pick, narrow, NT, preferred_element_type=jnp.float32).astype(turned_ref.dtype)
 
 
-def assemble_kernel(masked, at_ref, back_ref, rows_ref, scale_ref, zero_ref, one_ref, two_ref, three_ref, out_ref, basis, cross):
+def assemble_kernel(masked, at_ref, back_ref, rows_ref, scale_ref, mine_ref, other_ref, out_ref, basis, cross):
     x, core, grp = at_ref[0], at_ref[1], at_ref[2]
     first = grp * ROWS
-    shares = (zero_ref, one_ref, two_ref, three_ref)
     basis[...] = jnp.zeros_like(basis)
     cross[...] = jnp.zeros_like(cross)
     line = lax.broadcasted_iota(jnp.int32, (SHARE, 384), 0)
     lane = lax.broadcasted_iota(jnp.int32, (SHARE, 384), 1)
     for k in range(4):
-        for c, which in ((0, core), (1, 1 - core)):
+        for share, which in ((mine_ref, core), (other_ref, 1 - core)):
             part = (x - k + 4) % 4 * 2 + which
             begin = part * PART // RUN * RUN
             put = jnp.where((line + (part * PART - begin) == lane) & (line < PART), 1.0, 0.0).astype(jnp.bfloat16)
             cols = pl.ds(pl.multiple_of(begin, RUN), 384)
             basis[:, cols] += lax.dot_general(
-                shares[k][c], put, (((0,), (0,)), ((), ())), preferred_element_type=jnp.float32
+                share[k], put, (((0,), (0,)), ((), ())), preferred_element_type=jnp.float32
             )
     line = lax.broadcasted_iota(jnp.int32, (TALL, 256), 0)
     lane = lax.broadcasted_iota(jnp.int32, (TALL, 256), 1)
@@ -475,7 +428,7 @@
     steps = pl.num_programs(0)
 
     def fetch(i):
-        rows = pl.ds(pl.multiple_of(i * tile, 8), tile)
+        rows = pl.ds(pl.multiple_of(i * tile, 16), tile)
         return pltpu.make_async_copy(base_ref.at[rows], held.at[i % 2], sems.at[i % 2])
 
     @pl.when(step == 0)
@@ -492,7 +445,7 @@
         cols = slice(lo, lo + 256)
         first = jnp.dot(turn_ref[:, :SUBJ], cen_ref[0, :, cols], preferred_element_type=jnp.float32)
         second = jnp.dot(turn_ref[:, SUBJ:], cen_ref[1, :, cols], preferred_element_type=jnp.float32)
-        base = held[slot, :, cols]
+        base = held[slot, :, cols].astype(jnp.float32)
         out_ref[:, cols] = (base + scale_ref[0:1, 0:1] * first + scale_ref[1:2, 0:1] * second).astype(out_ref.dtype)
 
 
@@ -518,14 +471,7 @@
     up = [(i, i + 1) for i in range(7)]
     down = [(i + 1, i) for i in range(7)]
     packed = jnp.stack([tiles, lax.ppermute(tiles, slab, up), lax.ppermute(tiles, slab, down)])
-    raw, _ = lax.optimization_barrier((jnp.transpose(raw_frames, (1, 0, 2)), packed))
-    planar = filter_planes(raw)
-    every, planar = lax.optimization_barrier((copies(packed, "grp", GRP), planar))
-    own = every[:, 0].reshape(-1)
-    near = jnp.concatenate([every[: GRP // 4, 2].reshape(-1), every[3 * GRP // 4 :, 1].reshape(-1)])
-
-    middles, rim, to_up, to_down = filter_depth(own, near, planar)
-    at_ss, _ = lax.optimization_barrier((at, to_down))
+    at_ss, _ = lax.optimization_barrier((at, packed))
     held = [pltpu.VMEM((4 * WIDE, per_device), bf16)]
     other_ss = pl.pallas_call(
         basis_other_kernel,
@@ -536,9 +482,12 @@
         compiler_params=params(24),
         name="basis_other",
     )(at_ss, subspace)
-    from_low, from_high, other_ss = lax.optimization_barrier(
-        (lax.ppermute(to_up, slab, up), lax.ppermute(to_down, slab, down), other_ss)
-    )
+    every, other_ss = lax.optimization_barrier((copies(packed, "grp", GRP), other_ss))
+    own = every[:, 0].reshape(-1)
+    near = jnp.concatenate([every[: GRP // 4, 2].reshape(-1), every[3 * GRP // 4 :, 1].reshape(-1)])
+
+    middles, rim, to_up, to_down = smooth(own, near, jnp.transpose(raw_frames, (1, 0, 2)))
+    from_low, from_high = lax.ppermute(to_up, slab, up), lax.ppermute(to_down, slab, down)
     placed = pl.pallas_call(
         rim_kernel,
         out_shape=like(middles.shape, bf16),
@@ -552,6 +501,7 @@
     regrouped = lax.all_to_all(placed, "grp", 0, 0, tiled=True)
 
     got_ss = lax.ppermute(other_ss, "core", swap)
+    at_own, _ = lax.optimization_barrier((at, placed))
     own_ss, next_ss, far_ss, back_ss = pl.pallas_call(
         basis_own_kernel,
         out_shape=[like((WIDE, K), bf16), like((WIDE, K), bf16), like((2, HALF, K), bf16), like((WIDE, K), bf16)],
@@ -560,7 +510,7 @@
         scratch_shapes=held,
         compiler_params=params(24),
         name="basis_own",
-    )(at_ss, subspace, got_ss)
+    )(at_own, subspace, got_ss)
     ahead, behind = turns[1], turns[3]
     next_ss, back_ss = pl.pallas_call(
         basis_relay_kernel,
@@ -571,6 +521,8 @@
         name="basis_relay",
     )(next_ss, back_ss, lax.ppermute(far_ss[0], "x", ahead), lax.ppermute(far_ss[1], "x", behind))
     regrouped, _, _ = lax.optimization_barrier((regrouped, next_ss, back_ss))
+    went_on = lax.ppermute(next_ss, "x", ahead)
+    went_back = lax.ppermute(back_ss, "x", behind)
     by_row = pl.pallas_call(
         basis_rows_kernel,
         out_shape=like((GRP, SHARE, RUN), bf16),
@@ -579,7 +531,7 @@
         scratch_shapes=[pltpu.VMEM((WIDE, 1408), f32)],
         compiler_params=params(16),
         name="basis_rows",
-    )(at, own_ss, lax.ppermute(next_ss, "x", ahead), lax.ppermute(back_ss, "x", behind))
+    )(at, own_ss, went_on, went_back)
 
     centered, other_c, own_c, power = pl.pallas_call(
         columns_kernel,
@@ -608,26 +560,25 @@
 
     rotation_b, _ = lax.optimization_barrier((rotation, sent))
     contract = (((0,), (0,)), ((), ()))
-    from_basis = lax.dot_general(rotation_b[:K], subspace, contract, preferred_element_type=f32)
+    from_basis = lax.dot_general(rotation_b[:K], subspace, contract, preferred_element_type=f32).astype(bf16)
     summed, from_basis, turn = lax.optimization_barrier((summed, from_basis, rotation_b[K:].T))
 
-    total, share = pl.pallas_call(
+    total = pl.pallas_call(
         total_kernel,
-        out_shape=[like((2 * TALL, RUN), bf16), like((SHARE, RUN), bf16)],
+        out_shape=like((2 * TALL + SHARE, RUN), bf16),
         in_specs=vmem(1),
-        out_specs=vmem(2),
+        out_specs=vmem(1)[0],
         compiler_params=params(16),
         name="total",
     )(summed)
-    sum_c = pl.pallas_call(
+    sum_c, share = pl.pallas_call(
         slab_kernel,
-        out_shape=like((2 * TALL, RUN), f32),
+        out_shape=[like((2 * TALL, RUN), f32), like((4, SHARE, RUN), bf16)],
         in_specs=vmem(4),
-        out_specs=vmem(1)[0],
+        out_specs=vmem(2),
         compiler_params=params(16),
         name="slab",
     )(total, *[lax.ppermute(total, "x", turns[k]) for k in range(1, 4)])
-    share = jnp.stack([share, lax.ppermute(share, "core", swap)])
     rows_c, scales, turned = pl.pallas_call(
         functools.partial(finish_kernel, float(masked * SUBJ)),
         out_shape=[like((TALL, 2 * SUBJ), f32), like((8, RUN), f32), like((GRP, TALL, TALL), bf16)],
@@ -638,16 +589,15 @@
     )(at, sum_c, lax.ppermute(sum_c, "core", swap))
 
     back = lax.all_to_all(turned, "grp", 0, 0, tiled=True)
-    share, _ = lax.optimization_barrier((share, turned))
     gram_rows = pl.pallas_call(
         functools.partial(assemble_kernel, float(masked)),
         out_shape=like((ROWS, KX), f32),
-        in_specs=[smem(), *vmem(7)],
+        in_specs=[smem(), *vmem(5)],
         out_specs=vmem(1)[0],
         scratch_shapes=[pltpu.VMEM((TALL, 1408), f32), pltpu.VMEM((TALL, 1408), f32)],
         compiler_params=params(16),
         name="assemble",
-    )(at, back, rows_c, scales, share, *[lax.ppermute(share, "x", turns[k]) for k in range(1, 4)])
+    )(at, back, rows_c, scales, share, lax.ppermute(share, "core", swap))
 
     tile = 240
     new_subspace = pl.pallas_call(
@@ -661,7 +611,7 @@
             pl.BlockSpec((2, SUBJ, per_device), lambda i: (0, 0, 0)),
         ],
         out_specs=pl.BlockSpec((tile, per_device), lambda i: (i, 0)),
-        scratch_shapes=[pltpu.VMEM((2, tile, per_device), f32), pltpu.SemaphoreType.DMA((2,))],
+        scratch_shapes=[pltpu.VMEM((2, tile, per_device), bf16), pltpu.SemaphoreType.DMA((2,))],
         compiler_params=params(BIG),
         name="rotate",
     )(scales, from_basis, turn, centered)

time: 187 us -> 177 us (0.947)
  Pallas kernels: 63.3 us -> 52.2 us
  starting transfers between devices: 48.3 us -> 57.1 us
  waiting for transfers between devices: 48.6 us -> 42 us
    pallas_call x4 -> x3, Pallas kernels: 27.6 us -> 18 us  [the longest x1 17.8 us: smooth(): pl.pallas_call(smooth_kernel, out_shape=[jax.ShapeDtypeStruct((GRP, frame...]
    all_to_all x1, waiting for transfers between devices: 8.6 us -> 0.01 us  [body(): regrouped = lax.all_to_all(placed, 'grp', 0, 0, tiled=True)]
    ppermute x1, starting transfers between devices: 0.01 us -> 6.37 us  [body(): lax.ppermute(far_ss[0], 'x', ahead)]
    ppermute x1, waiting for transfers between devices: 0.01 us -> 4.43 us  [body(): lax.ppermute(to_down, slab, down)]
    ppermute x1, starting transfers between devices: 0.01 us -> 4.42 us  [body(): lax.ppermute(other_c, 'core', swap)]
    ppermute x1, waiting for transfers between devices: 5.14 us -> 0.97 us  [body(): lax.ppermute(far_ss[1], 'x', behind)]
    all_to_all x1, waiting for transfers between devices: 0.01 us -> 2.84 us  [body(): back = lax.all_to_all(turned, 'grp', 0, 0, tiled=True)]
    ppermute x1, starting transfers between devices: 3.49 us -> 0.73 us  [body(): got_ss = lax.ppermute(other_ss, 'core', swap)]
  transfers between devices with their start and end apart: 22 -> 19, of which waited for: 12 -> 14; matrix products, arithmetic and copies ran while one was open for 7% -> 8% of each run, Pallas kernels for 22% -> 22%
where the time goes in v6:
time: 177 us; the launch traced here: 176 us
  starting transfers between devices  57.1 us (32%)
  Pallas kernels  52.2 us (29%)
  waiting for transfers between devices  42 us (24%)
  local copies, waits for them, and re-layouts  13.8 us (8%)
  matrix products  9.96 us (6%)
    pallas_call x1, Pallas kernels, smooth(): pl.pallas_call(smooth_kernel, out_shape=[jax.ShapeDtypeStruct((GRP, frame...  17.8 us
    all_to_all x1, waiting for transfers between devices, body(): summed = lax.all_to_all(sent, 'grp', 0, 0, tiled=True)  11.1 us
    dot_general x1, matrix products, body(): lax.dot_general(rotation_b[:K], subspace, contract, preferred_element_typ...  9.96 us
    ppermute x1, waiting for transfers between devices, body(): went_on = lax.ppermute(next_ss, 'x', ahead)  9.76 us
    unnamed x24, local copies, waits for them, and re-layouts  9.05 us
    pallas_call x1, Pallas kernels, body(): pl.pallas_call(functools.partial(rotate_kernel, tile), out_shape=like((K,...  8.95 us
    all_to_all x1, starting transfers between devices, copies(): lax.all_to_all(jnp.broadcast_to(value[None], (count, *value.shape)), axis...  8.16 us
    all_to_all x1, starting transfers between devices, body(): regrouped = lax.all_to_all(placed, 'grp', 0, 0, tiled=True)  7.13 us
  transfers between devices with their start and end apart: 19, of which 14 were waited for; matrix products, arithmetic and copies ran while one was open for 8% of the time, Pallas kernels for 22%

profile of v6, /device:TPU:0, one launch (start us, length us, event | category | flops | bytes accessed | tf_op | source)
XLA Modules:
  0.0 176.1 jit_solution(16618581398857348446)
XLA Ops:
  0.6 0.8 slice_reduce_fusion
  1.5 1.3 collective-permute-start.1
  2.8 3.0 %collective-permute-start = (s32[14]{0:T(128)S(1)}, s32[14]{0:T(128)S(1)}, u32[]{:S(2)}, u32[]{:S(2)}) collective-permute-start(s32[14]{0:T(128)S(1)} %fusion.1), channel_id=1, source_target_pairs={{0,16},{16,32},{32,48},{48,64},{64,80},{80,96},{96,112},{1,17},{17... | collective-permute-start | bytes 176 | tf_op jit(solution)/shard_map/ppermute | solution.py:473
  5.8 0.8 collective-permute-done
  6.6 0.6 broadcast_in_dim.2
  7.2 8.2 %all-to-all-start = ((s32[16,3,14]{2,1,0:T(4,128)}), s32[16,3,14]{2,1,0:T(4,128)S(1)}, u32[]{:S(2)}, u32[]{:S(2)}) async-start(s32[16,3,14]{2,1,0:T(4,128)} %broadcast_in_dim.2), calls=%async_computation | async-start | bytes 65536 | tf_op jit(solution)/shard_map/all_to_all | solution.py:453
  15.5 2.2 %copy-done = bf16[1200,1792]{1,0:T(8,128)(2,1)S(1)} copy-done((bf16[1200,1792]{1,0:T(8,128)(2,1)S(1)}, bf16[1200,1792]{1,0:T(8,128)(2,1)}, u32[]{:S(2)}) %copy-start) | copy-done | bytes 4300824
  17.7 5.2 %basis_other.1 = bf16[704,1200]{1,0:T(8,128)(2,1)} custom-call(s32[3]{0:T(128)S(1)} %pad_add_fusion.1.at_ref, bf16[1200,1792]{1,0:T(8,128)(2,1)S(1)} %copy-done), custom_call_target="tpu_custom_call" | custom-call | tf_op jit(solution)/shard_map/basis_other/pallas_call | solution.py:476
  23.1 0.7 collective-permute-start.4
  24.1 17.8 %smooth.1 = (bf16[16,32,1792]{2,1,0:T(8,128)(2,1)S(1)}, f32[8,32,1792]{2,1,0:T(8,128)S(1)}, bf16[4,32,1792]{2,1,0:T(8,128)(2,1)S(1)}, bf16[4,32,1792]{2,1,0:T(8,128)(2,1)S(1)}) custom-call(s32[224]{0:T(256)S(1)} %reshape_squeeze.9.own_ref, s32[112]{0:T(128)S(1)} %pad_add_fusion.2.near_ref, f32[64]{0:T(128)S(1)} %copy-done.7, ...), custom_call_target="tpu_custom_call" | custom-call | tf_op jit(solution)/shard_map/smooth/pallas_call | solution.py:155
  41.9 1.9 %collective-permute-start.2 = (bf16[4,32,1792]{2,1,0:T(8,128)(2,1)S(1)}, bf16[4,32,1792]{2,1,0:T(8,128)(2,1)S(1)}, u32[]{:S(2)}, u32[]{:S(2)}) collective-permute-start(bf16[4,32,1792]{2,1,0:T(8,128)(2,1)S(1)} %get-tuple-element.33), channel_id=1, source_target_pairs={{0,16},{16,32},{32,48},{48,64},{64,80},{80,96},{96,112},{1,17},{17... | collective-permute-start | bytes 1376264 | tf_op jit(solution)/shard_map/ppermute | solution.py:490
  43.9 1.3 collective-permute-start.3
  45.3 4.4 %collective-permute-done.3.high_ref = bf16[4,32,1792]{2,1,0:T(8,128)(2,1)S(1)} collective-permute-done((bf16[4,32,1792]{2,1,0:T(8,128)(2,1)S(1)}, bf16[4,32,1792]{2,1,0:T(8,128)(2,1)S(1)}, u32[]{:S(2)}, u32[]{:S(2)}) %collective-permute-start.3) | collective-permute-done | bytes 458784 | tf_op jit(solution)/shard_map/ppermute | solution.py:490
  49.7 0.7 rim.1
  50.5 1.2 copy-done.2
  51.7 7.1 %all-to-all-start.1 = ((bf16[16,32,1792]{2,1,0:T(8,128)(2,1)}), bf16[16,32,1792]{2,1,0:T(8,128)(2,1)S(1)}, u32[]{:S(2)}, u32[]{:S(2)}) async-start(bf16[16,32,1792]{2,1,0:T(8,128)(2,1)} %copy-done.2), calls=%async_computation.1 | async-start | bytes 3670016 | tf_op jit(solution)/shard_map/all_to_all | solution.py:501
  58.8 2.2 %copy-done.1 = bf16[1200,1792]{1,0:T(8,128)(2,1)S(1)} copy-done((bf16[1200,1792]{1,0:T(8,128)(2,1)S(1)}, bf16[1200,1792]{1,0:T(8,128)(2,1)}, u32[]{:S(2)}) %copy-start.1) | copy-done | bytes 4300824
  61.0 5.0 %basis_own.1 = (bf16[176,1200]{1,0:T(8,128)(2,1)S(1)}, bf16[176,1200]{1,0:T(8,128)(2,1)S(1)}, bf16[2,88,1200]{2,1,0:T(8,128)(2,1)S(1)}, bf16[176,1200]{1,0:T(8,128)(2,1)S(1)}) custom-call(s32[3]{0:T(128)S(1)} %pad_add_fusion.1.at_ref, bf16[1200,1792]{1,0:T(8,128)(2,1)S(1)} %copy-done.1, bf16[704,1200]{1,0:T(8,128)(2,1)} %collective-permute-done.4.got_ref), custom_call_target="tpu_custom_call" | custom-call | tf_op jit(solution)/shard_map/basis_own/pallas_call | solution.py:505
  66.0 6.4 %collective-permute-start.5 = (bf16[88,1200]{1,0:T(8,128)(2,1)S(1)}, bf16[88,1200]{1,0:T(8,128)(2,1)S(1)}, u32[]{:S(2)}, u32[]{:S(2)}) collective-permute-start(bf16[88,1200]{1,0:T(8,128)(2,1)S(1)} %get-tuple-element.61), channel_id=1, source_target_pairs={{0,32},{32,64},{64,96},{96,0},{1,33},{33,65},{65,97},{97,1},{2,34}... | collective-permute-start | bytes 633608 | tf_op jit(solution)/shard_map/ppermute | solution.py:522
  72.4 1.6 collective-permute-start.6
  74.0 5.6 %collective-permute-done.5.low_ref = bf16[88,1200]{1,0:T(8,128)(2,1)S(1)} collective-permute-done((bf16[88,1200]{1,0:T(8,128)(2,1)S(1)}, bf16[88,1200]{1,0:T(8,128)(2,1)S(1)}, u32[]{:S(2)}, u32[]{:S(2)}) %collective-permute-start.5) | collective-permute-done | bytes 211232 | tf_op jit(solution)/shard_map/ppermute | solution.py:522
  79.6 1.0 collective-permute-done.6.high_ref
  80.7 0.8 copy-done.8
  81.5 0.8 copy-done.10
  82.2 7.0 %columns.1 = (bf16[2,256,1792]{2,1,0:T(8,128)(2,1)S(1)}, bf16[1712,256]{1,0:T(8,128)(2,1)S(1)}, f32[1712,256]{1,0:T(8,128)S(1)}, f32[8,128]{1,0:T(8,128)S(1)}) custom-call(s32[3]{0:T(128)S(1)} %pad_add_fusion.1.at_ref, bf16[16,32,1792]{2,1,0:T(8,128)(2,1)S(1)} %all-to-all-done.1.got_ref, bf16[1200,1792]{1,0:T(8,128)(2,1)} %basis_ref.1), custom_call_target="tpu_custom_call" | custom-call | tf_op jit(solution)/shard_map/columns/pallas_call | solution.py:536
  89.2 1.3 copy-done.3
  90.5 4.4 %collective-permute-start.7 = (bf16[1712,256]{1,0:T(8,128)(2,1)S(1)}, bf16[1712,256]{1,0:T(8,128)(2,1)S(1)}, u32[]{:S(2)}, u32[]{:S(2)}) collective-permute-start(bf16[1712,256]{1,0:T(8,128)(2,1)S(1)} %get-tuple-element.45), channel_id=1, source_target_pairs={{0,16},{16,0},{1,17},{17,1},{2,18},{18,2},{3,19},{19,3},{4,20},{20... | collective-permute-start | bytes 2629640 | tf_op jit(solution)/shard_map/ppermute | solution.py:558
  94.9 6.6 %collective-permute-start.8 = (bf16[176,1200]{1,0:T(8,128)(2,1)S(1)}, bf16[176,1200]{1,0:T(8,128)(2,1)S(1)}, u32[]{:S(2)}, u32[]{:S(2)}) collective-permute-start(bf16[176,1200]{1,0:T(8,128)(2,1)S(1)} %copy-done.11), channel_id=1, source_target_pairs={{0,32},{32,64},{64,96},{96,0},{1,33},{33,65},{65,97},{97,1},{2,34}... | collective-permute-start | bytes 1267208 | tf_op jit(solution)/shard_map/ppermute | solution.py:524
  101.5 9.8 %collective-permute-done.8.b_ref = bf16[176,1200]{1,0:T(8,128)(2,1)S(1)} collective-permute-done((bf16[176,1200]{1,0:T(8,128)(2,1)S(1)}, bf16[176,1200]{1,0:T(8,128)(2,1)S(1)}, u32[]{:S(2)}, u32[]{:S(2)}) %collective-permute-start.8) | collective-permute-done | bytes 422432 | tf_op jit(solution)/shard_map/ppermute | solution.py:524
  111.3 2.2 %collective-permute-done.9.c_ref = bf16[176,1200]{1,0:T(8,128)(2,1)S(1)} collective-permute-done((bf16[176,1200]{1,0:T(8,128)(2,1)S(1)}, bf16[176,1200]{1,0:T(8,128)(2,1)S(1)}, u32[]{:S(2)}, u32[]{:S(2)}) %collective-permute-start.9) | collective-permute-done | bytes 422432 | tf_op jit(solution)/shard_map/ppermute | solution.py:525
  113.5 1.5 basis_rows.1.basis_ref
  115.0 1.9 %windows.1 = bf16[16,408,128]{2,1,0:T(8,128)(2,1)} custom-call(f32[1712,256]{1,0:T(8,128)S(1)} %get-tuple-element.44.own_ref, bf16[1712,256]{1,0:T(8,128)(2,1)S(1)} %collective-permute-done.7.got_ref, f32[8,128]{1,0:T(8,128)S(1)} %get-tuple-element.46.power_ref, bf16[16,152,128]{2,1,0:T(8,128)(2,1)S(1)} %basis_rows.1.basis_ref), custom_call_target="tpu_custom_call" | custom-call | tf_op jit(solution)/shard_map/windows/pallas_call | solution.py:550
  116.9 5.4 %all-to-all-start.2 = ((bf16[16,408,128]{2,1,0:T(8,128)(2,1)}), bf16[16,408,128]{2,1,0:T(8,128)(2,1)S(1)}, u32[]{:S(2)}, u32[]{:S(2)}) async-start(bf16[16,408,128]{2,1,0:T(8,128)(2,1)} %windows.1), calls=%async_computation.2 | async-start | bytes 3342336 | tf_op jit(solution)/shard_map/all_to_all | solution.py:559
  122.3 3.0 %slice_bitcast_fusion.turn_ref = bf16[1200,512]{1,0:T(8,128)(2,1)} fusion(bf16[1712,1200]{0,1:T(8,128)(2,1)} %param.9), kind=kLoop, calls=%fused_computation.2 | loop fusion | bytes 2457600 | tf_op jit(solution)/shard_map/transpose | solution.py:564
  125.3 10.0 %convolution_convert_fusion.base_ref = bf16[1200,1792]{1,0:T(8,128)(2,1)} fusion(bf16[1200,1792]{1,0:T(8,128)(2,1)} %basis_ref.1, bf16[1712,1200]{0,1:T(8,128)(2,1)} %param.9), kind=kOutput, calls=%fused_computation | convolution fusion | flops 5163110400 | bytes 11673600 | tf_op jit(solution)/shard_map/dot_general | solution.py:563
  135.2 11.1 %all-to-all-done.2.got_ref = bf16[16,408,128]{2,1,0:T(8,128)(2,1)S(1)} async-done(((bf16[16,408,128]{2,1,0:T(8,128)(2,1)}), bf16[16,408,128]{2,1,0:T(8,128)(2,1)S(1)}, u32[]{:S(2)}, u32[]{:S(2)}) %all-to-all-start.2) | async-done | bytes 1671200 | tf_op jit(solution)/shard_map/all_to_all | solution.py:559
  146.6 1.7 collective-permute-start.10
  148.3 1.6 collective-permute-start.11
  149.9 1.9 %collective-permute-start.12 = (bf16[408,128]{1,0:T(8,128)(2,1)S(1)}, bf16[408,128]{1,0:T(8,128)(2,1)S(1)}, u32[]{:S(2)}, u32[]{:S(2)}) collective-permute-start(bf16[408,128]{1,0:T(8,128)(2,1)S(1)} %total.1.a_ref), channel_id=1, source_target_pairs={{0,96},{32,0},{64,32},{96,64},{1,97},{33,1},{65,33},{97,65},{2,98}... | collective-permute-start | bytes 313352 | tf_op jit(solution)/shard_map/ppermute | solution.py:581
  151.8 0.8 collective-permute-done.10.b_ref
  152.6 1.9 %collective-permute-done.11.c_ref = bf16[408,128]{1,0:T(8,128)(2,1)S(1)} collective-permute-done((bf16[408,128]{1,0:T(8,128)(2,1)S(1)}, bf16[408,128]{1,0:T(8,128)(2,1)S(1)}, u32[]{:S(2)}, u32[]{:S(2)}) %collective-permute-start.11) | collective-permute-done | bytes 104480 | tf_op jit(solution)/shard_map/ppermute | solution.py:581
  154.7 1.3 collective-permute-done.13.got_ref
  156.1 1.7 finish.1
  157.8 0.6 copy-done.5
  158.4 3.6 %all-to-all-start.3 = ((bf16[16,128,128]{2,1,0:T(8,128)(2,1)}), bf16[16,128,128]{2,1,0:T(8,128)(2,1)S(1)}, u32[]{:S(2)}, u32[]{:S(2)}) async-start(bf16[16,128,128]{2,1,0:T(8,128)(2,1)} %get-tuple-element.51), calls=%async_computation.3 | async-start | bytes 1048576 | tf_op jit(solution)/shard_map/all_to_all | solution.py:591
  162.2 9.0 %rotate.1 = bf16[1200,1792]{1,0:T(8,128)(2,1)} custom-call(f32[8,128]{1,0:T(8,128)} %copy-done.5, bf16[1200,1792]{1,0:T(8,128)(2,1)} %convolution_convert_fusion.base_ref, bf16[1200,512]{1,0:T(8,128)(2,1)} %slice_bitcast_fusion.turn_ref, bf16[2,256,1792]{2,1,0:T(8,128)(2,1)} %copy-done.3), custom_call_target="tpu_custom_call" | custom-call | tf_op jit(solution)/shard_map/rotate/pallas_call | solution.py:603
  171.2 2.8 %all-to-all-done.3.back_ref = bf16[16,128,128]{2,1,0:T(8,128)(2,1)S(1)} async-done(((bf16[16,128,128]{2,1,0:T(8,128)(2,1)}), bf16[16,128,128]{2,1,0:T(8,128)(2,1)S(1)}, u32[]{:S(2)}, u32[]{:S(2)}) %all-to-all-start.3) | async-done | bytes 524320 | tf_op jit(solution)/shard_map/all_to_all | solution.py:591
  174.0 2.1 %assemble.1 = f32[107,1712]{1,0:T(8,128)} custom-call(s32[3]{0:T(128)S(1)} %pad_add_fusion.1.at_ref, bf16[16,128,128]{2,1,0:T(8,128)(2,1)S(1)} %all-to-all-done.3.back_ref, f32[128,512]{1,0:T(8,128)S(1)} %get-tuple-element.52.rows_ref, f32[8,128]{1,0:T(8,128)S(1)} %copy-done.6, bf16[4,152,128]{2,1,0:T(8,128)(2,1)S(1)} %get-tuple-element.54.mine_ref, ...), custom_call_target="tpu_custom_call" | custom-call | tf_op jit(solution)/shard_map/assemble/pallas_call | solution.py:592
  (42 shorter events, 1.6 us)
Async XLA Ops:
  1.5 4.4 %collective-permute-start.1 = (s32[14]{0:T(128)S(1)}, s32[14]{0:T(128)S(1)}, u32[]{:S(2)}, u32[]{:S(2)}) collective-permute-start(s32[14]{0:T(128)S(1)} %fusion.1), channel_id=1, source_target_pairs={{16,0},{32,16},{48,32},{64,48},{80,64},{96,80},{112,96},{17,1},{33... | collective-permute-start | bytes 176 | tf_op jit(solution)/shard_map/ppermute | solution.py:473
  2.8 3.8 %collective-permute-start = (s32[14]{0:T(128)S(1)}, s32[14]{0:T(128)S(1)}, u32[]{:S(2)}, u32[]{:S(2)}) collective-permute-start(s32[14]{0:T(128)S(1)} %fusion.1), channel_id=1, source_target_pairs={{0,16},{16,32},{32,48},{48,64},{64,80},{80,96},{96,112},{1,17},{17... | collective-permute-start | bytes 176 | tf_op jit(solution)/shard_map/ppermute | solution.py:473
  7.2 15.8 %all-to-all-start = ((s32[16,3,14]{2,1,0:T(4,128)}), s32[16,3,14]{2,1,0:T(4,128)S(1)}, u32[]{:S(2)}, u32[]{:S(2)}) async-start(s32[16,3,14]{2,1,0:T(4,128)} %broadcast_in_dim.2), calls=%async_computation | async-start | bytes 65536 | tf_op jit(solution)/shard_map/all_to_all | solution.py:453
  15.5 2.2 %copy-start = (bf16[1200,1792]{1,0:T(8,128)(2,1)S(1)}, bf16[1200,1792]{1,0:T(8,128)(2,1)}, u32[]{:S(2)}) copy-start(bf16[1200,1792]{1,0:T(8,128)(2,1)} %basis_ref.1) | copy-start | bytes 12902404
  17.7 6.4 %copy-start.4 = (bf16[3,1024,256]{2,1,0:T(8,128)(2,1)S(1)}, bf16[3,1024,256]{2,1,0:T(8,128)(2,1)}, u32[]{:S(2)}) copy-start(bf16[3,1024,256]{2,1,0:T(8,128)(2,1)} %constant.42.taps_ref) | copy-start | bytes 4718596
  17.7 6.4 %copy-start.7 = (f32[64]{0:T(128)S(1)}, f32[64]{0:T(128)}, u32[]{:S(2)}) copy-start(f32[64]{0:T(128)} %constant.39.clone.tab_ref) | copy-start | bytes 772
  23.1 35.7 %collective-permute-start.4 = (bf16[704,1200]{1,0:T(8,128)(2,1)}, bf16[704,1200]{1,0:T(8,128)(2,1)}, u32[]{:S(2)}, u32[]{:S(2)}) collective-permute-start(bf16[704,1200]{1,0:T(8,128)(2,1)} %basis_other.1), channel_id=1, source_target_pairs={{0,16},{16,0},{1,17},{17,1},{2,18},{18,2},{3,19},{19,3},{4,20},{20... | collective-permute-start | bytes 5068808 | tf_op jit(solution)/shard_map/ppermute | solution.py:503
  41.9 3.4 %collective-permute-start.2 = (bf16[4,32,1792]{2,1,0:T(8,128)(2,1)S(1)}, bf16[4,32,1792]{2,1,0:T(8,128)(2,1)S(1)}, u32[]{:S(2)}, u32[]{:S(2)}) collective-permute-start(bf16[4,32,1792]{2,1,0:T(8,128)(2,1)S(1)} %get-tuple-element.33), channel_id=1, source_target_pairs={{0,16},{16,32},{32,48},{48,64},{64,80},{80,96},{96,112},{1,17},{17... | collective-permute-start | bytes 1376264 | tf_op jit(solution)/shard_map/ppermute | solution.py:490
  43.9 5.8 %collective-permute-start.3 = (bf16[4,32,1792]{2,1,0:T(8,128)(2,1)S(1)}, bf16[4,32,1792]{2,1,0:T(8,128)(2,1)S(1)}, u32[]{:S(2)}, u32[]{:S(2)}) collective-permute-start(bf16[4,32,1792]{2,1,0:T(8,128)(2,1)S(1)} %get-tuple-element.34), channel_id=1, source_target_pairs={{16,0},{32,16},{48,32},{64,48},{80,64},{96,80},{112,96},{17,1},{33... | collective-permute-start | bytes 1376264 | tf_op jit(solution)/shard_map/ppermute | solution.py:490
  50.4 1.2 copy-start.2
  51.7 30.6 %all-to-all-start.1 = ((bf16[16,32,1792]{2,1,0:T(8,128)(2,1)}), bf16[16,32,1792]{2,1,0:T(8,128)(2,1)S(1)}, u32[]{:S(2)}, u32[]{:S(2)}) async-start(bf16[16,32,1792]{2,1,0:T(8,128)(2,1)} %copy-done.2), calls=%async_computation.1 | async-start | bytes 3670016 | tf_op jit(solution)/shard_map/all_to_all | solution.py:501
  58.8 2.2 %copy-start.1 = (bf16[1200,1792]{1,0:T(8,128)(2,1)S(1)}, bf16[1200,1792]{1,0:T(8,128)(2,1)}, u32[]{:S(2)}) copy-start(bf16[1200,1792]{1,0:T(8,128)(2,1)} %basis_ref.1) | copy-start | bytes 12902404
  66.0 13.5 %collective-permute-start.5 = (bf16[88,1200]{1,0:T(8,128)(2,1)S(1)}, bf16[88,1200]{1,0:T(8,128)(2,1)S(1)}, u32[]{:S(2)}, u32[]{:S(2)}) collective-permute-start(bf16[88,1200]{1,0:T(8,128)(2,1)S(1)} %get-tuple-element.61), channel_id=1, source_target_pairs={{0,32},{32,64},{64,96},{96,0},{1,33},{33,65},{65,97},{97,1},{2,34}... | collective-permute-start | bytes 633608 | tf_op jit(solution)/shard_map/ppermute | solution.py:522
  72.4 8.1 %collective-permute-start.6 = (bf16[88,1200]{1,0:T(8,128)(2,1)S(1)}, bf16[88,1200]{1,0:T(8,128)(2,1)S(1)}, u32[]{:S(2)}, u32[]{:S(2)}) collective-permute-start(bf16[88,1200]{1,0:T(8,128)(2,1)S(1)} %get-tuple-element.60), channel_id=1, source_target_pairs={{0,96},{32,0},{64,32},{96,64},{1,97},{33,1},{65,33},{97,65},{2,98}... | collective-permute-start | bytes 633608 | tf_op jit(solution)/shard_map/ppermute | solution.py:522
  80.7 0.8 copy-start.8
  81.5 0.8 copy-start.10
  82.2 12.7 %copy-start.11 = (bf16[176,1200]{1,0:T(8,128)(2,1)S(1)}, bf16[176,1200]{1,0:T(8,128)(2,1)}, u32[]{:S(2)}) copy-start(bf16[176,1200]{1,0:T(8,128)(2,1)} %copy-done.10) | copy-start | bytes 1267204
  82.2 19.3 %copy-start.9 = (bf16[176,1200]{1,0:T(8,128)(2,1)S(1)}, bf16[176,1200]{1,0:T(8,128)(2,1)}, u32[]{:S(2)}) copy-start(bf16[176,1200]{1,0:T(8,128)(2,1)} %copy-done.8) | copy-start | bytes 1267204
  89.2 1.3 copy-start.3
  90.5 24.5 %collective-permute-start.7 = (bf16[1712,256]{1,0:T(8,128)(2,1)S(1)}, bf16[1712,256]{1,0:T(8,128)(2,1)S(1)}, u32[]{:S(2)}, u32[]{:S(2)}) collective-permute-start(bf16[1712,256]{1,0:T(8,128)(2,1)S(1)} %get-tuple-element.45), channel_id=1, source_target_pairs={{0,16},{16,0},{1,17},{17,1},{2,18},{18,2},{3,19},{19,3},{4,20},{20... | collective-permute-start | bytes 2629640 | tf_op jit(solution)/shard_map/ppermute | solution.py:558
  94.9 16.4 %collective-permute-start.8 = (bf16[176,1200]{1,0:T(8,128)(2,1)S(1)}, bf16[176,1200]{1,0:T(8,128)(2,1)S(1)}, u32[]{:S(2)}, u32[]{:S(2)}) collective-permute-start(bf16[176,1200]{1,0:T(8,128)(2,1)S(1)} %copy-done.11), channel_id=1, source_target_pairs={{0,32},{32,64},{64,96},{96,0},{1,33},{33,65},{65,97},{97,1},{2,34}... | collective-permute-start | bytes 1267208 | tf_op jit(solution)/shard_map/ppermute | solution.py:524
  101.5 12.0 %collective-permute-start.9 = (bf16[176,1200]{1,0:T(8,128)(2,1)S(1)}, bf16[176,1200]{1,0:T(8,128)(2,1)S(1)}, u32[]{:S(2)}, u32[]{:S(2)}) collective-permute-start(bf16[176,1200]{1,0:T(8,128)(2,1)S(1)} %copy-done.9), channel_id=1, source_target_pairs={{0,96},{32,0},{64,32},{96,64},{1,97},{33,1},{65,33},{97,65},{2,98}... | collective-permute-start | bytes 1267208 | tf_op jit(solution)/shard_map/ppermute | solution.py:525
  116.9 29.5 %all-to-all-start.2 = ((bf16[16,408,128]{2,1,0:T(8,128)(2,1)}), bf16[16,408,128]{2,1,0:T(8,128)(2,1)S(1)}, u32[]{:S(2)}, u32[]{:S(2)}) async-start(bf16[16,408,128]{2,1,0:T(8,128)(2,1)} %windows.1), calls=%async_computation.2 | async-start | bytes 3342336 | tf_op jit(solution)/shard_map/all_to_all | solution.py:559
  146.6 6.0 %collective-permute-start.10 = (bf16[408,128]{1,0:T(8,128)(2,1)S(1)}, bf16[408,128]{1,0:T(8,128)(2,1)S(1)}, u32[]{:S(2)}, u32[]{:S(2)}) collective-permute-start(bf16[408,128]{1,0:T(8,128)(2,1)S(1)} %total.1.a_ref), channel_id=1, source_target_pairs={{0,32},{32,64},{64,96},{96,0},{1,33},{33,65},{65,97},{97,1},{2,34}... | collective-permute-start | bytes 313352 | tf_op jit(solution)/shard_map/ppermute | solution.py:581
  148.3 6.2 %collective-permute-start.11 = (bf16[408,128]{1,0:T(8,128)(2,1)S(1)}, bf16[408,128]{1,0:T(8,128)(2,1)S(1)}, u32[]{:S(2)}, u32[]{:S(2)}) collective-permute-start(bf16[408,128]{1,0:T(8,128)(2,1)S(1)} %total.1.a_ref), channel_id=1, source_target_pairs={{0,64},{32,96},{64,0},{96,32},{1,65},{33,97},{65,1},{97,33},{2,66}... | collective-permute-start | bytes 313352 | tf_op jit(solution)/shard_map/ppermute | solution.py:581
  149.9 4.7 %collective-permute-start.12 = (bf16[408,128]{1,0:T(8,128)(2,1)S(1)}, bf16[408,128]{1,0:T(8,128)(2,1)S(1)}, u32[]{:S(2)}, u32[]{:S(2)}) collective-permute-start(bf16[408,128]{1,0:T(8,128)(2,1)S(1)} %total.1.a_ref), channel_id=1, source_target_pairs={{0,96},{32,0},{64,32},{96,64},{1,97},{33,1},{65,33},{97,65},{2,98}... | collective-permute-start | bytes 313352 | tf_op jit(solution)/shard_map/ppermute | solution.py:581
  154.6 1.4 collective-permute-start.13
  157.8 0.6 copy-start.5
  158.4 15.6 %all-to-all-start.3 = ((bf16[16,128,128]{2,1,0:T(8,128)(2,1)}), bf16[16,128,128]{2,1,0:T(8,128)(2,1)S(1)}, u32[]{:S(2)}, u32[]{:S(2)}) async-start(bf16[16,128,128]{2,1,0:T(8,128)(2,1)} %get-tuple-element.51), calls=%async_computation.3 | async-start | bytes 1048576 | tf_op jit(solution)/shard_map/all_to_all | solution.py:591
  162.0 9.2 %collective-permute-start.14 = (bf16[4,152,128]{2,1,0:T(8,128)(2,1)S(1)}, bf16[4,152,128]{2,1,0:T(8,128)(2,1)S(1)}, u32[]{:S(2)}, u32[]{:S(2)}) collective-permute-start(bf16[4,152,128]{2,1,0:T(8,128)(2,1)S(1)} %get-tuple-element.54.mine_ref), channel_id=1, source_target_pairs={{0,16},{16,0},{1,17},{17,1},{2,18},{18,2},{3,19},{19,3},{4,20},{20... | collective-permute-start | bytes 466952 | tf_op jit(solution)/shard_map/ppermute | solution.py:600
  162.2 11.8 %copy-start.6 = (f32[8,128]{1,0:T(8,128)S(1)}, f32[8,128]{1,0:T(8,128)}, u32[]{:S(2)}) copy-start(f32[8,128]{1,0:T(8,128)} %copy-done.5) | copy-start | bytes 12292
